TPU v7x, 32 devices: a whole 2x2x4 slice. The times are simulated.
32 devices in a mesh: loop: 8 (over z, y), row: 4 (over x, core).
Axes of the slice: x: 2, y: 2, z: 4, core: 2. Of those that a mesh axis runs over, the one named last changes fastest.
Arguments:
- slab: float32 [2048, 16384], P('row', 'loop'), may hold values from -6 to 6
- rotations: float32 [32, 512, 512], P('loop', 'row')
- slab_pair: int32 [4], replicated, may hold values from 0 to 31, as said below
Outputs:
- moved: float32 [2048, 16384], P('row', 'loop')
Inputs may be any that keep to these rules, and one draw needn't show every extreme that they name: `slab_pair`: distinct pair numbers.
All inputs are finite; a program needn't handle non-finite values.
Results may differ from a plain program's by a relative error of at most 0.00009.
Values sent between devices are 32-bit elements; how exact they have to be, the bound alone decides.
No kernel may reach another device: no remote copies, remote signals or barrier semaphores. Data moves between devices by JAX's collectives and lax.ppermute only.
A program may use at most 64 MiB of HBM per device.

v0:
```python
import jax
import jax.numpy as jnp
from jax import lax
from jax.sharding import PartitionSpec as P


def from_behind(shard, axis, by):
    length = lax.axis_size(axis)
    pairs = [(i, i + by) for i in range(length) if 0 <= i + by < length]
    return lax.ppermute(shard, axis, pairs)


def from_root(shard, axis, root):
    mine = lax.axis_index(axis) == root
    return lax.psum(jnp.where(mine, shard, jnp.zeros_like(shard)), axis)


def left_apply(rotation, columns):
    return jnp.einsum("ij,in->jn", rotation, columns, precision=lax.Precision.HIGHEST)


def move_blocks(last_top, first_bottom):
    incoming_top = from_behind(last_top, "loop", 1)
    incoming_bottom = from_behind(first_bottom, "loop", -1)
    return (incoming_top, incoming_bottom)


def arrange(updated, incoming_top, incoming_bottom, pair_dev, half):
    rows = updated.shape[0]
    blocks = updated.reshape(rows, pair_dev, 2, half)
    tops = blocks[:, :, 0]
    bottoms = blocks[:, :, 1]
    new_tops = jnp.concatenate([incoming_top[:, None], tops[:, : pair_dev - 1]], axis=1)
    new_bottoms = jnp.concatenate([bottoms[:, 1:], incoming_bottom[:, None]], axis=1)
    place = lax.axis_index("loop") * pair_dev + jnp.arange(pair_dev, dtype=jnp.int32)
    total_pairs = pair_dev * lax.axis_size("loop")
    new_tops = jnp.where((place == 0)[None, :, None], tops, new_tops)
    new_tops = jnp.where((place == 1)[None, :, None], bottoms[:, :1], new_tops)
    new_bottoms = jnp.where(
        (place == total_pairs - 1)[None, :, None], tops[:, pair_dev - 1 :], new_bottoms
    )
    return jnp.stack([new_tops, new_bottoms], axis=2).reshape(rows, pair_dev * 2 * half)


def per_device(slab, rotations, slab_pair):
    pair_dev = rotations.shape[0]
    width = rotations.shape[2]
    half = width // 2
    rows = slab.shape[0]
    panels = slab.reshape(rows, pair_dev, width)
    wanted = slab_pair[lax.axis_index("row")]
    local_slot = wanted % pair_dev
    owner = wanted // pair_dev
    gathered = lax.all_gather(rotations, "row", axis=1, tiled=True)
    turned = jnp.einsum("rpi,pij->rpj", panels, gathered, precision=lax.Precision.HIGHEST)
    picked = lax.dynamic_index_in_dim(gathered, local_slot, 0, keepdims=False)
    rotation = from_root(picked, "loop", owner)
    flat = turned.reshape(rows, pair_dev * width)
    updated = left_apply(rotation, flat)
    last_top = updated[:, (pair_dev - 1) * width : (pair_dev - 1) * width + half]
    first_bottom = updated[:, half:width]
    incoming_top, incoming_bottom = move_blocks(last_top, first_bottom)
    return arrange(updated, incoming_top, incoming_bottom, pair_dev, half)


def solution(mesh):
    return jax.shard_map(
        per_device,
        mesh=mesh,
        in_specs=(P("row", "loop"), P("loop", "row", None), P()),
        out_specs=P("row", "loop"),
        check_vma=False,
    )
```

profile of v0, /device:TPU:0, one launch (start us, length us, event | category | flops | bytes accessed | tf_op | source)
XLA Modules:
  0.0 199.6 jit_solution(9748989037205450885)
XLA Ops:
  6.5 0.0 copy-start.1
  6.5 0.0 all-gather.2.cloned.1.call-start
  6.5 2.5 %copy.13 = f32[4,128,512]{1,2,0:T(8,128)} copy(f32[4,128,512]{2,1,0:T(8,128)} %param.4) | data formatting | bytes 2097152 | tf_op args[1]
  9.1 0.0 all-gather.2.cloned.1.call-update
  9.1 0.0 all-reduce.2.cloned.1.call-start
  9.2 0.0 copy-done.1
  9.2 0.7 dynamic_slice.7
  12.6 34.4 %all-gather.2.cloned.1.call-done = f32[4,512,512]{1,2,0:T(8,128)} async-done(((f32[4,128,512]{1,2,0:T(8,128)}), f32[4,512,512]{1,2,0:T(8,128)}) %all-gather.2.cloned.1.call-update) | async-done | bytes 4194320 | tf_op jit(solution)/shard_map/all_gather | solution.py:54
  47.0 2.3 %select_bitcast_fusion = f32[512,512]{0,1:T(8,128)} fusion(f32[4,512,512]{1,2,0:T(8,128)} %all-gather.2.cloned.1.call-done, s32[]{:T(128)S(6)} %select_n.53, pred[]{:T(512)S(6)} %eq.27), kind=kLoop, calls=%fused_computation.11 | loop fusion | flops 262144 | bytes 2097157 | tf_op jit(solution)/shard_map/jit(_where)/select_n | solution.py:15
  49.3 0.0 all-reduce.2.cloned.1.call-update
  49.4 12.0 %fusion = f32[4,512,512]{2,1,0:T(8,128)} fusion(f32[4,512,512]{1,2,0:T(8,128)} %all-gather.2.cloned.1.call-done, f32[64,4,8,512]{3,2,1,0:T(8,128)} %bitcast.36), kind=kOutput, calls=%fused_computation | convolution fusion | flops 6442450944 | bytes 12582912 | tf_op jit(solution)/shard_map/rpi,pij->rpj/dot_general | solution.py:55
  61.4 67.1 %all-reduce.2.cloned.1.call-done = f32[512,512]{0,1:T(8,128)} async-done(((f32[512,512]{0,1:T(8,128)}), f32[512,512]{0,1:T(8,128)}) %all-reduce.2.cloned.1.call-update) | async-done | bytes 1048592 | tf_op jit(solution)/shard_map/psum | solution.py:15
  128.5 9.0 %fusion.9 = f32[512,2048]{1,0:T(8,128)S(1)} fusion(f32[512,512]{0,1:T(8,128)} %all-reduce.2.cloned.1.call-done, f32[512,2048]{0,1:T(8,128)} %bitcast.30), kind=kOutput, calls=%fused_computation.20 | convolution fusion | flops 6442450944 | bytes 9437184 | tf_op jit(solution)/shard_map/ij,in->jn/dot_general | solution.py:19
  137.6 0.0 copy-start
  137.6 2.0 %copy-done = f32[512,2048]{1,0:T(8,128)} copy-done((f32[512,2048]{1,0:T(8,128)}, f32[512,2048]{1,0:T(8,128)S(1)}, u32[]{:S(2)}) %copy-start) | copy-done | bytes 4194328
  139.6 0.1 fusion.7
  139.7 6.6 %reshape.61 = f32[512,4,2,256]{3,2,1,0:T(2,128)} reshape(f32[512,2048]{1,0:T(8,128)} %copy-done) | data formatting | bytes 8388608 | tf_op jit(solution)/shard_map/reshape | solution.py:30
  146.3 7.1 %fusion.8 = (f32[512,4,1,256]{3,2,1,0:T(1,128)S(1)}, f32[512,4,1,256]{3,2,1,0:T(1,128)S(1)}) fusion(f32[512,4,2,256]{3,2,1,0:T(2,128)} %reshape.61), kind=kLoop, calls=%fused_computation.19 | loop fusion | bytes 8388608 | tf_op jit(solution)/shard_map/slice | solution.py:31
  153.3 0.4 copy.29
  153.8 0.1 slice_bitcast_fusion
  153.9 3.2 %collective-permute-start = (f32[512,256]{1,0:T(8,128)S(1)}, f32[512,256]{1,0:T(8,128)S(1)}, u32[]{:S(2)}, u32[]{:S(2)}) collective-permute-start(f32[512,256]{1,0:T(8,128)S(1)} %get-tuple-element.5), channel_id=1, source_target_pairs={{0,4},{4,8},{8,12},{12,16},{16,20},{20,24},{24,28},{1,5},{5,9},{9,... | collective-permute-start | bytes 1572872 | tf_op jit(solution)/shard_map/ppermute | solution.py:10
  157.1 1.3 collective-permute-start.1
  158.4 0.4 copy.30
  158.8 0.1 slice_bitcast_fusion.1
  159.0 13.0 %collective-permute-done.1 = f32[512,256]{1,0:T(8,128)S(1)} collective-permute-done((f32[512,256]{1,0:T(8,128)S(1)}, f32[512,256]{1,0:T(8,128)S(1)}, u32[]{:S(2)}, u32[]{:S(2)}) %collective-permute-start.1) | collective-permute-done | bytes 524320 | tf_op jit(solution)/shard_map/ppermute | solution.py:10
  172.0 0.2 maximum_select_fusion.1
  172.3 6.8 %collective-permute-done = f32[512,256]{1,0:T(8,128)S(1)} collective-permute-done((f32[512,256]{1,0:T(8,128)S(1)}, f32[512,256]{1,0:T(8,128)S(1)}, u32[]{:S(2)}, u32[]{:S(2)}) %collective-permute-start) | collective-permute-done | bytes 524320 | tf_op jit(solution)/shard_map/ppermute | solution.py:10
  179.1 0.6 fusion.3
  179.7 2.5 %pad_maximum_fusion = f32[512,4,2,256]{3,0,2,1:T(8,128)} fusion(f32[512,4,1,256]{3,0,2,1:T(8,128)S(1)} %maximum_select_fusion.1, f32[512,4,1,256]{3,0,2,1:T(8,128)S(1)} %fusion.3), kind=kLoop, calls=%fused_computation.3 | loop fusion | flops 1048576 | bytes 8388608 | tf_op jit(solution)/shard_map/stack | solution.py:42
  182.2 5.2 %copy.17 = f32[512,4,2,256]{0,3,2,1:T(8,128)} copy(f32[512,4,2,256]{3,0,2,1:T(8,128)} %pad_maximum_fusion) | data formatting | bytes 8388608 | tf_op jit(solution)/shard_map/stack | solution.py:42
  187.4 5.3 %copy.18 = f32[512,2048]{1,0:T(8,128)} copy(f32[512,2048]{0,1:T(8,128)} %bitcast.31) | data formatting | bytes 8388608 | tf_op jit(solution)/shard_map/reshape | solution.py:42
  (4 shorter events, 0.1 us)
Async XLA Ops:
  6.5 2.6 %copy-start.1 = (s32[4]{0:T(128)S(1)}, s32[4]{0:T(128)}, u32[]{:S(2)}) copy-start(s32[4]{0:T(128)} %param.5) | copy-start | bytes 52
  6.5 40.4 %all-gather.2.cloned.1.call-start = ((), (), s32[]{:S(2)}) async-start(), calls=%async_computation | async-start | bytes 5242880 | tf_op jit(solution)/shard_map/all_gather | solution.py:54
  9.1 119.4 %all-reduce.2.cloned.1.call-start = ((), (), s32[]{:S(2)}) async-start(), calls=%async_computation.1 | async-start | bytes 2097152 | tf_op jit(solution)/shard_map/psum | solution.py:15
  137.6 2.0 %copy-start = (f32[512,2048]{1,0:T(8,128)}, f32[512,2048]{1,0:T(8,128)S(1)}, u32[]{:S(2)}) copy-start(f32[512,2048]{1,0:T(8,128)S(1)} %fusion.9) | copy-start | bytes 12582916
  153.9 25.2 %collective-permute-start = (f32[512,256]{1,0:T(8,128)S(1)}, f32[512,256]{1,0:T(8,128)S(1)}, u32[]{:S(2)}, u32[]{:S(2)}) collective-permute-start(f32[512,256]{1,0:T(8,128)S(1)} %get-tuple-element.5), channel_id=1, source_target_pairs={{0,4},{4,8},{8,12},{12,16},{16,20},{20,24},{24,28},{1,5},{5,9},{9,... | collective-permute-start | bytes 1572872 | tf_op jit(solution)/shard_map/ppermute | solution.py:10
  157.1 14.9 %collective-permute-start.1 = (f32[512,256]{1,0:T(8,128)S(1)}, f32[512,256]{1,0:T(8,128)S(1)}, u32[]{:S(2)}, u32[]{:S(2)}) collective-permute-start(f32[512,256]{1,0:T(8,128)S(1)} %get-tuple-element.6), channel_id=1, source_target_pairs={{4,0},{8,4},{12,8},{16,12},{20,16},{24,20},{28,24},{5,1},{9,5},{13... | collective-permute-start | bytes 1572872 | tf_op jit(solution)/shard_map/ppermute | solution.py:10
Sparse Core Ops, SparseCore 0:
  9.2 37.7 all-gather.1
  50.5 77.9 all-reduce.1
where the time goes:
time: 200 us
  waiting for transfers between devices  121 us (60%)
  local copies, waits for them, and re-layouts  30.6 us (15%)
  matrix products  21.1 us (11%)
  between operations  16.3 us (8%)
  other arithmetic  5.63 us (3%)
  starting transfers between devices  4.53 us (2%)
    psum x1, waiting for transfers between devices, from_root(): return lax.psum(jnp.where(mine, shard, jnp.zeros_like(shard)), axis)  67.1 us
    all_gather x1, waiting for transfers between devices, per_device(): gathered = lax.all_gather(rotations, 'row', axis=1, tiled=True)  34.4 us
    ppermute x2, waiting for transfers between devices, from_behind(): return lax.ppermute(shard, axis, pairs)  19.9 us
    dot_general x1, matrix products, per_device(): jnp.einsum('rpi,pij->rpj', panels, gathered, precision=lax.Precision.HIGH...  12 us
    dot_general x1, matrix products, left_apply(): jnp.einsum('ij,in->jn', rotation, columns, precision=lax.Precision.HIGHEST)  9.04 us
    slice x1, local copies, waits for them, and re-layouts, arrange(): tops = blocks[:, :, 0]  7.06 us
    reshape x1, local copies, waits for them, and re-layouts, arrange(): blocks = updated.reshape(rows, pair_dev, 2, half)  6.59 us
    unnamed x7, local copies, waits for them, and re-layouts  5.36 us
  transfers between devices with their start and end apart: 4, of which 4 were waited for; matrix products, arithmetic and copies ran while one was open for 7% of the time, Pallas kernels for 0%

commit v1 on v0

v1 whole, which is shorter than its diff:
```python
from functools import partial

import jax
import jax.numpy as jnp
from jax import lax
from jax.experimental import pallas as pl
from jax.experimental.pallas import tpu as pltpu
from jax.sharding import PartitionSpec as P

VMEM = pl.BlockSpec(memory_space=pltpu.VMEM)
SMEM = pl.BlockSpec(memory_space=pltpu.SMEM)
HBM = pl.BlockSpec(memory_space=pltpu.HBM)
F32, BF16 = jnp.float32, jnp.bfloat16
SPREAD = (0, 2, 1, 3)


def flip(x, axis, bit):
    n = lax.axis_size(axis)
    return lax.ppermute(x, axis, [(i, i ^ bit) for i in range(n)])


def trade(x, first):
    n = lax.axis_size("loop")
    pairs = []
    for i in range(first, n - 1, 2):
        pairs += [(i, i + 1), (i + 1, i)]
    return lax.ppermute(x, "loop", pairs)


def after(x, *others):
    return lax.optimization_barrier((x,) + others)[0]


def params(mib):
    return pltpu.CompilerParams(vmem_limit_bytes=mib << 20)


def cost(flops, bytes_accessed):
    return pl.CostEstimate(flops=flops, bytes_accessed=bytes_accessed, transcendentals=0)


def split(x):
    hi = x.astype(BF16)
    lo = (x - hi.astype(F32)).astype(BF16)
    return hi, lo


def dot3(a_hi, a_lo, b_hi, b_lo):
    def dot(a, b):
        return jnp.dot(a, b, preferred_element_type=F32)

    return dot(a_hi, b_hi) + (dot(a_hi, b_lo) + dot(a_lo, b_hi))


def prepare_kernel(pair_ref, rot_ref, give_ref, keep_ref, edge_ref, rest_ref, sem):
    pairs, piece, width = rot_ref.shape
    half = width // 2
    last = pairs - 1
    side = lax.axis_index("loop") % 2
    away = pl.multiple_of((1 - side) * half, half)
    home = pl.multiple_of(side * half, half)
    copies = []
    for t in range(give_ref.shape[0]):
        copies.append((rot_ref.at[pair_ref[t] % pairs, :, pl.ds(away, half)], give_ref.at[t]))
    copies.append((rot_ref.at[0, :, half:], edge_ref.at[0]))
    copies.append((rot_ref.at[last, :, :half], edge_ref.at[1]))
    for t in range(give_ref.shape[0]):
        copies.append((rot_ref.at[pair_ref[t] % pairs, :, pl.ds(home, half)], keep_ref.at[t]))
    copies.append((rot_ref.at[0, :, :half], rest_ref.at[:, :half]))
    for p in range(1, last):
        copies.append((rot_ref.at[p], rest_ref.at[:, half + (p - 1) * width : half + p * width]))
    copies.append((rot_ref.at[last, :, half:], rest_ref.at[:, half + (last - 1) * width :]))
    copies = [pltpu.make_async_copy(src, dst, sem.at[n]) for n, (src, dst) in enumerate(copies)]
    for copy in copies:
        copy.start()
    for copy in copies:
        copy.wait()


def take(pair_ref, pairs, bit, t, kept, got):
    l = lax.axis_index("loop")
    return jnp.where(((pair_ref[t] // pairs) & bit) == (l & bit), kept, got)


def halve_kernel(pairs, bit, pair_ref, kept_ref, got_ref, give_ref, keep_ref):
    half = give_ref.shape[-1]
    up = (lax.axis_index("loop") // (2 * bit)) % 2
    away = pl.ds(pl.multiple_of((1 - up) * half, half), half)
    home = pl.ds(pl.multiple_of(up * half, half), half)
    for t in range(give_ref.shape[0]):
        give_ref[t] = take(pair_ref, pairs, bit, t, kept_ref[t, :, away], got_ref[t, :, away])
        keep_ref[t] = take(pair_ref, pairs, bit, t, kept_ref[t, :, home], got_ref[t, :, home])


def pick_kernel(pairs, bit, pair_ref, kept_ref, got_ref, out_ref):
    for t in range(out_ref.shape[0]):
        out_ref[t] = take(pair_ref, pairs, bit, t, kept_ref[t], got_ref[t])


def last_pick_kernel(pairs, bit, pair_ref, kept_ref, got_ref, give_ref, keep_ref):
    high = lax.axis_index("row") // 2
    for n in range(2):
        for ref, t in ((give_ref, 2 * (1 - high) + n), (keep_ref, 2 * high + n)):
            ref[n] = take(pair_ref, pairs, bit, t, kept_ref[t], got_ref[t])


def cross_kernel(kept_ref, got_ref, give_ref, keep_ref):
    odd = lax.axis_index("row") % 2
    for n, ref in enumerate((kept_ref, got_ref)):
        give_ref[n] = ref[1 - odd]
        keep_ref[n] = ref[odd]


def join_kernel(a_ref, b_ref, out_ref):
    out_ref[:2] = a_ref[...]
    out_ref[2:] = b_ref[...]


def split_kernel(slab_ref, hi_ref, lo_ref):
    hi_ref[...], lo_ref[...] = split(slab_ref[...])


def stack_parts(hi_ref, lo_ref, n, parts):
    piece, wide = parts[0].shape
    r = lax.axis_index("row")
    for k, part in enumerate(parts):
        rows = pl.ds(pl.multiple_of((r ^ k) * piece, piece), piece)
        hi, lo = split(part)
        hi_ref[n, rows, :wide] = hi
        lo_ref[n, rows, :wide] = lo


def edge_kernel(shi0, slo0, shi1, slo1, own_ref, core0, core1, far_ref, far_core_ref, even_ref, odd_ref, hi_ref, lo_ref):
    side = lax.axis_index("loop") % 2
    for n, core in enumerate((core0, core1)):
        stack_parts(hi_ref, lo_ref, n, (own_ref[n], core[0], far_ref[n], far_core_ref[n]))
    bottom = dot3(shi0[...], slo0[...], hi_ref[0], lo_ref[0])
    top = dot3(shi1[...], slo1[...], hi_ref[1], lo_ref[1])

    @pl.when(side == 0)
    def _():
        even_ref[...] = top
        odd_ref[...] = bottom

    @pl.when(side == 1)
    def _():
        even_ref[...] = bottom
        odd_ref[...] = top


def turn_kernel(
    shi_ref, slo_ref, own_ref, core_ref, far_ref, far_core_ref, even_ref, odd_ref, thi_ref, tlo_ref, hi_ref, lo_ref
):
    pairs, piece, width = core_ref.shape
    half, last = width // 2, pairs - 1
    side = lax.axis_index("loop") % 2
    for p in range(pairs):
        cols = slice(0, half) if p == 0 else slice(half, width) if p == last else slice(0, width)
        at = 0 if p == 0 else half + (p - 1) * width
        here = slice(at, at + cols.stop - cols.start)
        stack_parts(hi_ref, lo_ref, p, (own_ref[:, here], core_ref[p, :, cols], far_ref[:, here], far_core_ref[:, here]))

    def put(block, n):
        hi, lo = split(block)
        thi_ref[n] = hi
        tlo_ref[n] = lo

    for p in range(pairs):
        a_hi, a_lo = (ref[:, p * width : (p + 1) * width] for ref in (shi_ref, slo_ref))
        if p == 0:
            put(dot3(a_hi, a_lo, hi_ref[p, :, :half], lo_ref[p, :, :half]), 0)
        elif p == last:
            put(dot3(a_hi, a_lo, hi_ref[p, :, :half], lo_ref[p, :, :half]), 2 * p + 1)
        else:
            made = dot3(a_hi, a_lo, hi_ref[p], lo_ref[p])
            put(made[:, :half], 2 * p)
            put(made[:, half:], 2 * p + 1)

    @pl.when(side == 0)
    def _():
        put(odd_ref[...], 1)
        put(even_ref[...], 2 * last)

    @pl.when(side == 1)
    def _():
        put(even_ref[...], 1)
        put(odd_ref[...], 2 * last)


def left_kernel(*refs):
    pieces, (thi_ref, tlo_ref, even_ref, odd_ref, out_ref, rot_ref, hi_ref, lo_ref) = refs[:4], refs[4:]
    k = pl.program_id(0)
    blocks = thi_ref.shape[0]
    teams, piece, quarter = pieces[0].shape
    l, loops = lax.axis_index("loop"), lax.axis_size("loop")
    r = lax.axis_index("row")

    @pl.when(k == 0)
    def _():
        mine = 2 * (l % 2) + (l // 2) % 2
        for which, block in enumerate(pieces):
            cols = pl.ds(pl.multiple_of((mine ^ which) * quarter, quarter), quarter)
            for n, there in enumerate(SPREAD):
                rows = pl.ds(pl.multiple_of((r ^ there) * piece, piece), piece)
                rot_ref[rows, cols] = block[n]
        hi_ref[...], lo_ref[...] = split(rot_ref[...].T)

    from_left = (k == 0) & (l > 0)
    from_right = (k == blocks - 1) & (l < loops - 1)
    src = jnp.where(k % 2 == 0, k - 2, k + 2)
    src = jnp.where(l == 0, jnp.where(k == 0, 0, jnp.where(k == 2, 1, src)), src)
    src = jnp.where((l == loops - 1) & (k == blocks - 1), blocks - 2, src)

    @pl.when(jnp.logical_not(from_left | from_right))
    def _():
        out_ref[...] = dot3(hi_ref[...], lo_ref[...], thi_ref[src], tlo_ref[src])

    by_even = (from_left & (l % 2 == 1)) | (from_right & (l % 2 == 0))
    by_odd = (from_left & (l % 2 == 0)) | (from_right & (l % 2 == 1))

    @pl.when(by_even)
    def _():
        out_ref[...] = dot3(hi_ref[...], lo_ref[...], *split(even_ref[...]))

    @pl.when(by_odd)
    def _():
        out_ref[...] = dot3(hi_ref[...], lo_ref[...], *split(odd_ref[...]))


def per_device(slab, rotations, slab_pair):
    pairs, piece, width = rotations.shape
    half, quarter = width // 2, width // 4
    rows, columns = slab.shape
    loops, teams = lax.axis_size("loop"), lax.axis_size("row")
    last = pairs - 1
    array = jax.ShapeDtypeStruct

    def glue(kernel, shapes, *operands, pair=False):
        return pl.pallas_call(
            kernel,
            out_shape=tuple(array(shape, F32) for shape in shapes),
            in_specs=[SMEM] * pair + [VMEM] * len(operands),
            out_specs=(VMEM,) * len(shapes),
            compiler_params=params(4),
            cost_estimate=cost(0, 0),
        )(*([slab_pair] * pair), *operands)

    give, keep, edge, rest = pl.pallas_call(
        prepare_kernel,
        out_shape=(
            array((teams, piece, half), F32),
            array((teams, piece, half), F32),
            array((2, piece, half), F32),
            array((piece, last * width), F32),
        ),
        in_specs=[SMEM, HBM],
        out_specs=(VMEM,) * 4,
        scratch_shapes=[pltpu.SemaphoreType.DMA((2 * teams + 2 + pairs,))],
        compiler_params=params(8),
        cost_estimate=cost(0, 0),
    )(slab_pair, pltpu.with_memory_space_constraint(rotations, pltpu.HBM))

    got = flip(give, "loop", 1)
    far_edge = flip(edge, "row", 2)
    core = flip(rotations, "row", 1)

    slab_hi, slab_lo = pl.pallas_call(
        split_kernel,
        grid=(4,),
        out_shape=(array((rows, columns), BF16),) * 2,
        in_specs=[pl.BlockSpec((rows // 4, columns), lambda i: (i, 0))],
        out_specs=(pl.BlockSpec((rows // 4, columns), lambda i: (i, 0)),) * 2,
        compiler_params=params(8),
        cost_estimate=cost(0, 0),
    )(pltpu.with_memory_space_constraint(after(slab, give), pltpu.HBM))

    far_edge = after(far_edge, slab_hi)
    far_core_edge = flip(far_edge, "row", 1)
    far = flip(after(rest, far_edge), "row", 2)

    even, odd = pl.pallas_call(
        edge_kernel,
        grid=(1,),
        out_shape=(array((rows, half), F32),) * 2,
        in_specs=[
            pl.BlockSpec((rows, width), lambda i: (0, 0)),
            pl.BlockSpec((rows, width), lambda i: (0, 0)),
            pl.BlockSpec((rows, width), lambda i: (0, last)),
            pl.BlockSpec((rows, width), lambda i: (0, last)),
            pl.BlockSpec((2, piece, half), lambda i: (0, 0, 0)),
            pl.BlockSpec((1, piece, half), lambda i: (0, 0, 1)),
            pl.BlockSpec((1, piece, half), lambda i: (last, 0, 0)),
            pl.BlockSpec((2, piece, half), lambda i: (0, 0, 0)),
            pl.BlockSpec((2, piece, half), lambda i: (0, 0, 0)),
        ],
        out_specs=(pl.BlockSpec((rows, half), lambda i: (0, 0)),) * 2,
        scratch_shapes=[pltpu.VMEM((2, width, half), BF16)] * 2,
        compiler_params=params(20),
        cost_estimate=cost(0, 0),
    )(slab_hi, slab_lo, slab_hi, slab_lo, edge, core, core, far_edge, far_core_edge)
    even_in = trade(even, 0)
    odd_in = trade(odd, 1)

    quarters = (teams, piece, quarter)
    give, held = glue(partial(halve_kernel, pairs, 1), (quarters, quarters), keep, after(got, even), pair=True)
    got = flip(give, "loop", 2)
    far = after(far, got)
    far_core = flip(far, "row", 1)
    blocks = array((2 * pairs, rows, half), BF16)
    turned_hi, turned_lo = pl.pallas_call(
        turn_kernel,
        out_shape=(blocks, blocks),
        in_specs=[VMEM] * 8,
        out_specs=(VMEM, VMEM),
        scratch_shapes=[pltpu.VMEM((pairs, width, width), BF16)] * 2,
        compiler_params=params(28),
        cost_estimate=cost(0, 0),
    )(slab_hi, slab_lo, rest, core, far, far_core, even, odd)

    bits = [1 << b for b in range(1, (loops - 1).bit_length())]
    for bit in bits[:-1]:
        (held,) = glue(partial(pick_kernel, pairs, bit), (quarters,), held, got, pair=True)
        got = flip(held, "loop", 2 * bit)
    got = after(got, turned_hi, even_in, odd_in)
    pieces = (2, piece, quarter)
    give, held = glue(partial(last_pick_kernel, pairs, bits[-1]), (pieces, pieces), held, got, pair=True)
    give, held = glue(cross_kernel, (pieces, pieces), held, flip(give, "row", 2))
    (held,) = glue(join_kernel, (quarters,), held, flip(give, "row", 1))

    near = flip(held, "loop", 2)
    side = flip(held, "loop", 1)
    across = flip(side, "loop", 2)

    return pl.pallas_call(
        left_kernel,
        grid=(2 * pairs,),
        out_shape=array((rows, columns), F32),
        in_specs=[VMEM] * 8,
        out_specs=pl.BlockSpec((rows, half), lambda k: (0, k)),
        scratch_shapes=[pltpu.VMEM((width, width), F32)] + [pltpu.VMEM((width, width), BF16)] * 2,
        compiler_params=params(28),
        cost_estimate=cost(0, 0),
    )(held, near, side, across, turned_hi, turned_lo, even_in, odd_in)


def solution(mesh):
    return jax.shard_map(
        per_device,
        mesh=mesh,
        in_specs=(P("row", "loop"), P("loop", "row", None), P()),
        out_specs=P("row", "loop"),
        check_vma=False,
    )
```

time: 200 us -> 92 us (0.46)
  waiting for transfers between devices: 121 us -> 55.1 us
  local copies, waits for them, and re-layouts: 30.6 us -> 0.66 us
  matrix products: 21.1 us -> 0 us
  Pallas kernels: 0 us -> 18.6 us
  between operations: 16.3 us -> 0.1 us
  starting transfers between devices: 4.53 us -> 17.3 us
  other arithmetic: 5.63 us -> 0 us
    psum x1 -> x0, waiting for transfers between devices: 67.1 us -> none  [from_root(): return lax.psum(jnp.where(mine, shard, jnp.zeros_like(shard)), axis)]
    ppermute x2 -> x15, waiting for transfers between devices: 19.9 us -> 55.1 us  [the longest x13 41 us: flip(): return lax.ppermute(x, axis, [(i, i ^ bit) for i in range(n)])]
    all_gather x1 -> x0, waiting for transfers between devices: 34.4 us -> none  [per_device(): gathered = lax.all_gather(rotations, 'row', axis=1, tiled=True)]
    dot_general x2 -> x0, matrix products: 21.1 us -> none  [the longest x1 12 us: per_device(): jnp.einsum('rpi,pij->rpj', panels, gathered, precision=lax.Precision.HIGH...]
    pallas_call x0 -> x10, Pallas kernels: none -> 18.6 us  [the longest x1 6.66 us: per_device(): pl.pallas_call(left_kernel, grid=(2 * pairs,), out_shape=array((rows, col...]
    ppermute x2 -> x15, starting transfers between devices: 4.49 us -> 17.3 us  [the longest x13 15.1 us: flip(): return lax.ppermute(x, axis, [(i, i ^ bit) for i in range(n)])]
    reshape x2 -> x0, local copies, waits for them, and re-layouts: 11.9 us -> none  [the longest x1 6.59 us: arrange(): blocks = updated.reshape(rows, pair_dev, 2, half)]
    slice x2 -> x0, local copies, waits for them, and re-layouts: 7.15 us -> none  [the longest x1 7.06 us: arrange(): tops = blocks[:, :, 0]]
  transfers between devices with their start and end apart: 4 -> 15, of which waited for: 4 -> 11; matrix products, arithmetic and copies ran while one was open for 7% -> 0% of each run, Pallas kernels for 0% -> 12%
where the time goes in v1:
time: 92 us; the launch traced here: 91.8 us
  waiting for transfers between devices  55.1 us (60%)
  Pallas kernels  18.6 us (20%)
  starting transfers between devices  17.3 us (19%)
    ppermute x13, waiting for transfers between devices, flip(): return lax.ppermute(x, axis, [(i, i ^ bit) for i in range(n)])  41 us
    ppermute x13, starting transfers between devices, flip(): return lax.ppermute(x, axis, [(i, i ^ bit) for i in range(n)])  15.1 us
    ppermute x2, waiting for transfers between devices, trade(): return lax.ppermute(x, 'loop', pairs)  14.2 us
    pallas_call x1, Pallas kernels, per_device(): pl.pallas_call(left_kernel, grid=(2 * pairs,), out_shape=array((rows, col...  6.66 us
    pallas_call x1, Pallas kernels, per_device(): pl.pallas_call(turn_kernel, out_shape=(blocks, blocks), in_specs=[VMEM] *...  3.4 us
    pallas_call x1, Pallas kernels, per_device(): pl.pallas_call(split_kernel, grid=(4,), out_shape=(array((rows, columns),...  3.14 us
    pallas_call x1, Pallas kernels, per_device(): pl.pallas_call(prepare_kernel, out_shape=(array((teams, piece, half), F32...  2.35 us
    ppermute x2, starting transfers between devices, trade(): return lax.ppermute(x, 'loop', pairs)  2.27 us
  transfers between devices with their start and end apart: 15, of which 11 were waited for; matrix products, arithmetic and copies ran while one was open for 0% of the time, Pallas kernels for 12%

profile of v1, /device:TPU:0, one launch (start us, length us, event | category | flops | bytes accessed | tf_op | source)
XLA Modules:
  0.0 91.8 jit_solution(3551100552285696229)
XLA Ops:
  0.0 0.5 collective-permute-start.1
  0.5 0.0 copy-start
  0.5 0.7 copy-done
  1.1 2.4 %shard_map.37 = (f32[4,128,256]{2,1,0:T(8,128)S(1)}, f32[4,128,256]{2,1,0:T(8,128)S(1)}, f32[2,128,256]{2,1,0:T(8,128)S(1)}, f32[128,1536]{1,0:T(8,128)S(1)}) custom-call(s32[4]{0:T(128)S(1)} %copy-done, f32[4,128,512]{2,1,0:T(8,128)} %rot_ref.1), custom_call_target="tpu_custom_call" | custom-call | tf_op jit(solution)/shard_map/pallas_call | solution.py:248
  3.5 2.6 %collective-permute-start.2 = (f32[2,128,256]{2,1,0:T(8,128)S(1)}, f32[2,128,256]{2,1,0:T(8,128)S(1)}, u32[]{:S(2)}, u32[]{:S(2)}) collective-permute-start(f32[2,128,256]{2,1,0:T(8,128)S(1)} %get-tuple-element.32.own_ref), channel_id=1, source_target_pairs={{0,2},{1,3},{2,0},{3,1},{4,6},{5,7},{6,4},{7,5},{8,10},{9,11},{10,... | collective-permute-start | bytes 786440 | tf_op jit(solution)/shard_map/ppermute | solution.py:19
  6.0 1.5 %collective-permute-start = (f32[4,128,256]{2,1,0:T(8,128)S(1)}, f32[4,128,256]{2,1,0:T(8,128)S(1)}, u32[]{:S(2)}, u32[]{:S(2)}) collective-permute-start(f32[4,128,256]{2,1,0:T(8,128)S(1)} %get-tuple-element.28), channel_id=1, source_target_pairs={{0,4},{4,0},{8,12},{12,8},{16,20},{20,16},{24,28},{28,24},{1,5},{5... | collective-permute-start | bytes 1572872 | tf_op jit(solution)/shard_map/ppermute | solution.py:19
  7.6 3.1 %shard_map.38 = (bf16[512,2048]{1,0:T(8,128)(2,1)S(1)}, bf16[512,2048]{1,0:T(8,128)(2,1)S(1)}) custom-call(f32[512,2048]{1,0:T(8,128)} %slab_ref), custom_call_target="tpu_custom_call" | custom-call | tf_op jit(solution)/shard_map/pallas_call | solution.py:267
  10.7 2.3 %collective-permute-done.2.far_ref = f32[2,128,256]{2,1,0:T(8,128)S(1)} collective-permute-done((f32[2,128,256]{2,1,0:T(8,128)S(1)}, f32[2,128,256]{2,1,0:T(8,128)S(1)}, u32[]{:S(2)}, u32[]{:S(2)}) %collective-permute-start.2) | collective-permute-done | bytes 262176 | tf_op jit(solution)/shard_map/ppermute | solution.py:19
  13.0 1.7 %collective-permute-start.6 = (f32[128,1536]{1,0:T(8,128)S(1)}, f32[128,1536]{1,0:T(8,128)S(1)}, u32[]{:S(2)}, u32[]{:S(2)}) collective-permute-start(f32[128,1536]{1,0:T(8,128)S(1)} %get-tuple-element.39.own_ref), channel_id=1, source_target_pairs={{0,2},{1,3},{2,0},{3,1},{4,6},{5,7},{6,4},{7,5},{8,10},{9,11},{10,... | collective-permute-start | bytes 2359304 | tf_op jit(solution)/shard_map/ppermute | solution.py:19
  14.7 0.0 collective-permute-start.3
  14.7 1.5 %collective-permute-done.3.far_core_ref = f32[2,128,256]{2,1,0:T(8,128)S(1)} collective-permute-done((f32[2,128,256]{2,1,0:T(8,128)S(1)}, f32[2,128,256]{2,1,0:T(8,128)S(1)}, u32[]{:S(2)}, u32[]{:S(2)}) %collective-permute-start.3) | collective-permute-done | bytes 262176 | tf_op jit(solution)/shard_map/ppermute | solution.py:19
  16.3 0.0 collective-permute-done.1.core0.core1.core_ref
  16.3 0.0 copy-start.1
  16.3 1.2 %shard_map.39 = (f32[512,256]{1,0:T(8,128)S(1)}, f32[512,256]{1,0:T(8,128)S(1)}) custom-call(bf16[512,2048]{1,0:T(8,128)(2,1)S(1)} %get-tuple-element.30.shi0.shi1.shi_ref, bf16[512,2048]{1,0:T(8,128)(2,1)S(1)} %get-tuple-element.31.slo0.slo1.slo_ref, bf16[512,2048]{1,0:T(8,128)(2,1)S(1)} %get-tuple-element.30.shi0.shi1.shi_ref, ...), custom_call_target="tpu_custom_call" | custom-call | tf_op jit(solution)/shard_map/pallas_call | solution.py:281
  17.5 2.6 %collective-permute-done.got_ref = f32[4,128,256]{2,1,0:T(8,128)S(1)} collective-permute-done((f32[4,128,256]{2,1,0:T(8,128)S(1)}, f32[4,128,256]{2,1,0:T(8,128)S(1)}, u32[]{:S(2)}, u32[]{:S(2)}) %collective-permute-start) | collective-permute-done | bytes 524320 | tf_op jit(solution)/shard_map/ppermute | solution.py:19
  20.1 0.0 copy-done.1
  20.1 0.6 shard_map.40
  20.7 1.6 %collective-permute-start.4 = (f32[4,128,128]{2,1,0:T(8,128)S(1)}, f32[4,128,128]{2,1,0:T(8,128)S(1)}, u32[]{:S(2)}, u32[]{:S(2)}) collective-permute-start(f32[4,128,128]{2,1,0:T(8,128)S(1)} %get-tuple-element.37), channel_id=1, source_target_pairs={{0,8},{4,12},{8,0},{12,4},{16,24},{20,28},{24,16},{28,20},{1,9},{5... | collective-permute-start | bytes 786440 | tf_op jit(solution)/shard_map/ppermute | solution.py:19
  22.4 10.0 %collective-permute-done.6.far_ref = f32[128,1536]{1,0:T(8,128)S(1)} collective-permute-done((f32[128,1536]{1,0:T(8,128)S(1)}, f32[128,1536]{1,0:T(8,128)S(1)}, u32[]{:S(2)}, u32[]{:S(2)}) %collective-permute-start.6) | collective-permute-done | bytes 786464 | tf_op jit(solution)/shard_map/ppermute | solution.py:19
  32.4 0.0 collective-permute-done.4.got_ref
  32.4 0.0 collective-permute-start.7
  32.4 1.6 %collective-permute-start.8 = (f32[512,256]{1,0:T(8,128)S(1)}, f32[512,256]{1,0:T(8,128)S(1)}, u32[]{:S(2)}, u32[]{:S(2)}) collective-permute-start(f32[512,256]{1,0:T(8,128)S(1)} %get-tuple-element.34.even_ref), channel_id=1, source_target_pairs={{0,4},{4,0},{8,12},{12,8},{16,20},{20,16},{24,28},{28,24},{1,5},{5... | collective-permute-start | bytes 1572872 | tf_op jit(solution)/shard_map/ppermute | solution.py:27
  34.0 0.7 collective-permute-start.9
  34.7 0.6 shard_map.41.kept_ref
  35.3 4.2 %collective-permute-start.5 = (f32[4,128,128]{2,1,0:T(8,128)S(1)}, f32[4,128,128]{2,1,0:T(8,128)S(1)}, u32[]{:S(2)}, u32[]{:S(2)}) collective-permute-start(f32[4,128,128]{2,1,0:T(8,128)S(1)} %shard_map.41.kept_ref), channel_id=1, source_target_pairs={{0,16},{4,20},{8,24},{12,28},{16,0},{20,4},{24,8},{28,12},{1,17},{... | collective-permute-start | bytes 786440 | tf_op jit(solution)/shard_map/ppermute | solution.py:19
  39.5 0.0 collective-permute-done.7.far_core_ref
  39.5 3.4 %shard_map.42 = (bf16[8,512,256]{2,1,0:T(8,128)(2,1)S(1)}, bf16[8,512,256]{2,1,0:T(8,128)(2,1)S(1)}) custom-call(bf16[512,2048]{1,0:T(8,128)(2,1)S(1)} %get-tuple-element.30.shi0.shi1.shi_ref, bf16[512,2048]{1,0:T(8,128)(2,1)S(1)} %get-tuple-element.31.slo0.slo1.slo_ref, f32[128,1536]{1,0:T(8,128)S(1)} %get-tuple-element.39.own_ref, ...), custom_call_target="tpu_custom_call" | custom-call | tf_op jit(solution)/shard_map/pallas_call | solution.py:310
  42.9 14.2 %collective-permute-done.8.refs_6_ = f32[512,256]{1,0:T(8,128)S(1)} collective-permute-done((f32[512,256]{1,0:T(8,128)S(1)}, f32[512,256]{1,0:T(8,128)S(1)}, u32[]{:S(2)}, u32[]{:S(2)}) %collective-permute-start.8) | collective-permute-done | bytes 524320 | tf_op jit(solution)/shard_map/ppermute | solution.py:27
  57.1 0.0 collective-permute-done.9.refs_7_
  57.1 5.1 %collective-permute-done.5.got_ref = f32[4,128,128]{2,1,0:T(8,128)S(1)} collective-permute-done((f32[4,128,128]{2,1,0:T(8,128)S(1)}, f32[4,128,128]{2,1,0:T(8,128)S(1)}, u32[]{:S(2)}, u32[]{:S(2)}) %collective-permute-start.5) | collective-permute-done | bytes 262176 | tf_op jit(solution)/shard_map/ppermute | solution.py:19
  62.1 0.6 shard_map.43
  62.7 1.6 %collective-permute-start.10 = (f32[2,128,128]{2,1,0:T(8,128)S(1)}, f32[2,128,128]{2,1,0:T(8,128)S(1)}, u32[]{:S(2)}, u32[]{:S(2)}) collective-permute-start(f32[2,128,128]{2,1,0:T(8,128)S(1)} %get-tuple-element.45), channel_id=1, source_target_pairs={{0,2},{1,3},{2,0},{3,1},{4,6},{5,7},{6,4},{7,5},{8,10},{9,11},{10,... | collective-permute-start | bytes 393224 | tf_op jit(solution)/shard_map/ppermute | solution.py:19
  64.3 3.5 %collective-permute-done.10.got_ref = f32[2,128,128]{2,1,0:T(8,128)S(1)} collective-permute-done((f32[2,128,128]{2,1,0:T(8,128)S(1)}, f32[2,128,128]{2,1,0:T(8,128)S(1)}, u32[]{:S(2)}, u32[]{:S(2)}) %collective-permute-start.10) | collective-permute-done | bytes 131104 | tf_op jit(solution)/shard_map/ppermute | solution.py:19
  67.8 0.1 collective-permute-start.11
  67.9 1.3 %collective-permute-done.11.b_ref = f32[2,128,128]{2,1,0:T(8,128)S(1)} collective-permute-done((f32[2,128,128]{2,1,0:T(8,128)S(1)}, f32[2,128,128]{2,1,0:T(8,128)S(1)}, u32[]{:S(2)}, u32[]{:S(2)}) %collective-permute-start.11) | collective-permute-done | bytes 131104 | tf_op jit(solution)/shard_map/ppermute | solution.py:19
  69.2 0.1 collective-permute-start.13
  69.3 1.2 %collective-permute-start.12 = (f32[4,128,128]{2,1,0:T(8,128)S(1)}, f32[4,128,128]{2,1,0:T(8,128)S(1)}, u32[]{:S(2)}, u32[]{:S(2)}) collective-permute-start(f32[4,128,128]{2,1,0:T(8,128)S(1)} %shard_map.45.refs_0_), channel_id=1, source_target_pairs={{0,8},{4,12},{8,0},{12,4},{16,24},{20,28},{24,16},{28,20},{1,9},{5... | collective-permute-start | bytes 786440 | tf_op jit(solution)/shard_map/ppermute | solution.py:19
  70.5 7.2 %collective-permute-done.13.refs_2_ = f32[4,128,128]{2,1,0:T(8,128)S(1)} collective-permute-done((f32[4,128,128]{2,1,0:T(8,128)S(1)}, f32[4,128,128]{2,1,0:T(8,128)S(1)}, u32[]{:S(2)}, u32[]{:S(2)}) %collective-permute-start.13) | collective-permute-done | bytes 262176 | tf_op jit(solution)/shard_map/ppermute | solution.py:19
  77.6 0.0 collective-permute-start.14
  77.6 0.1 collective-permute-done.12.refs_1_
  77.7 7.5 %collective-permute-done.14.refs_3_ = f32[4,128,128]{2,1,0:T(8,128)S(1)} collective-permute-done((f32[4,128,128]{2,1,0:T(8,128)S(1)}, f32[4,128,128]{2,1,0:T(8,128)S(1)}, u32[]{:S(2)}, u32[]{:S(2)}) %collective-permute-start.14) | collective-permute-done | bytes 262176 | tf_op jit(solution)/shard_map/ppermute | solution.py:19
  85.2 6.7 %shard_map.46 = f32[512,2048]{1,0:T(8,128)} custom-call(f32[4,128,128]{2,1,0:T(8,128)S(1)} %shard_map.45.refs_0_, f32[4,128,128]{2,1,0:T(8,128)S(1)} %collective-permute-done.12.refs_1_, f32[4,128,128]{2,1,0:T(8,128)S(1)} %collective-permute-done.13.refs_2_, f32[4,128,128]{2,1,0:T(8,128)S(1)} %collective-permute-done.14.refs_3_, ...), custom_call_target="tpu_custom_call" | custom-call | tf_op jit(solution)/shard_map/pallas_call | solution.py:334
  (2 shorter events, 0.0 us)
Async XLA Ops:
  0.0 16.3 %collective-permute-start.1 = (f32[4,128,512]{2,1,0:T(8,128)}, f32[4,128,512]{2,1,0:T(8,128)S(1)}, u32[]{:S(2)}, u32[]{:S(2)}) collective-permute-start(f32[4,128,512]{2,1,0:T(8,128)} %rot_ref.1), channel_id=1, source_target_pairs={{0,1},{1,0},{2,3},{3,2},{4,5},{5,4},{6,7},{7,6},{8,9},{9,8},{10,11... | collective-permute-start | bytes 3145736 | tf_op jit(solution)/shard_map/ppermute | solution.py:19
  0.5 0.7 copy-start
  3.5 9.5 %collective-permute-start.2 = (f32[2,128,256]{2,1,0:T(8,128)S(1)}, f32[2,128,256]{2,1,0:T(8,128)S(1)}, u32[]{:S(2)}, u32[]{:S(2)}) collective-permute-start(f32[2,128,256]{2,1,0:T(8,128)S(1)} %get-tuple-element.32.own_ref), channel_id=1, source_target_pairs={{0,2},{1,3},{2,0},{3,1},{4,6},{5,7},{6,4},{7,5},{8,10},{9,11},{10,... | collective-permute-start | bytes 786440 | tf_op jit(solution)/shard_map/ppermute | solution.py:19
  6.0 14.1 %collective-permute-start = (f32[4,128,256]{2,1,0:T(8,128)S(1)}, f32[4,128,256]{2,1,0:T(8,128)S(1)}, u32[]{:S(2)}, u32[]{:S(2)}) collective-permute-start(f32[4,128,256]{2,1,0:T(8,128)S(1)} %get-tuple-element.28), channel_id=1, source_target_pairs={{0,4},{4,0},{8,12},{12,8},{16,20},{20,16},{24,28},{28,24},{1,5},{5... | collective-permute-start | bytes 1572872 | tf_op jit(solution)/shard_map/ppermute | solution.py:19
  13.0 19.4 %collective-permute-start.6 = (f32[128,1536]{1,0:T(8,128)S(1)}, f32[128,1536]{1,0:T(8,128)S(1)}, u32[]{:S(2)}, u32[]{:S(2)}) collective-permute-start(f32[128,1536]{1,0:T(8,128)S(1)} %get-tuple-element.39.own_ref), channel_id=1, source_target_pairs={{0,2},{1,3},{2,0},{3,1},{4,6},{5,7},{6,4},{7,5},{8,10},{9,11},{10,... | collective-permute-start | bytes 2359304 | tf_op jit(solution)/shard_map/ppermute | solution.py:19
  14.7 1.5 %collective-permute-start.3 = (f32[2,128,256]{2,1,0:T(8,128)S(1)}, f32[2,128,256]{2,1,0:T(8,128)S(1)}, u32[]{:S(2)}, u32[]{:S(2)}) collective-permute-start(f32[2,128,256]{2,1,0:T(8,128)S(1)} %collective-permute-done.2.far_ref), channel_id=1, source_target_pairs={{0,1},{1,0},{2,3},{3,2},{4,5},{5,4},{6,7},{7,6},{8,9},{9,8},{10,11... | collective-permute-start | bytes 786440 | tf_op jit(solution)/shard_map/ppermute | solution.py:19
  16.3 3.8 %copy-start.1 = (s32[4]{0:T(128)S(1)}, s32[4]{0:T(128)}, u32[]{:S(2)}) copy-start(s32[4]{0:T(128)} %pair_ref.7) | copy-start | bytes 52
  20.7 11.7 %collective-permute-start.4 = (f32[4,128,128]{2,1,0:T(8,128)S(1)}, f32[4,128,128]{2,1,0:T(8,128)S(1)}, u32[]{:S(2)}, u32[]{:S(2)}) collective-permute-start(f32[4,128,128]{2,1,0:T(8,128)S(1)} %get-tuple-element.37), channel_id=1, source_target_pairs={{0,8},{4,12},{8,0},{12,4},{16,24},{20,28},{24,16},{28,20},{1,9},{5... | collective-permute-start | bytes 786440 | tf_op jit(solution)/shard_map/ppermute | solution.py:19
  32.4 7.1 %collective-permute-start.7 = (f32[128,1536]{1,0:T(8,128)S(1)}, f32[128,1536]{1,0:T(8,128)S(1)}, u32[]{:S(2)}, u32[]{:S(2)}) collective-permute-start(f32[128,1536]{1,0:T(8,128)S(1)} %collective-permute-done.6.far_ref), channel_id=1, source_target_pairs={{0,1},{1,0},{2,3},{3,2},{4,5},{5,4},{6,7},{7,6},{8,9},{9,8},{10,11... | collective-permute-start | bytes 2359304 | tf_op jit(solution)/shard_map/ppermute | solution.py:19
  32.4 24.7 %collective-permute-start.8 = (f32[512,256]{1,0:T(8,128)S(1)}, f32[512,256]{1,0:T(8,128)S(1)}, u32[]{:S(2)}, u32[]{:S(2)}) collective-permute-start(f32[512,256]{1,0:T(8,128)S(1)} %get-tuple-element.34.even_ref), channel_id=1, source_target_pairs={{0,4},{4,0},{8,12},{12,8},{16,20},{20,16},{24,28},{28,24},{1,5},{5... | collective-permute-start | bytes 1572872 | tf_op jit(solution)/shard_map/ppermute | solution.py:27
  34.0 23.1 %collective-permute-start.9 = (f32[512,256]{1,0:T(8,128)S(1)}, f32[512,256]{1,0:T(8,128)S(1)}, u32[]{:S(2)}, u32[]{:S(2)}) collective-permute-start(f32[512,256]{1,0:T(8,128)S(1)} %get-tuple-element.41.odd_ref), channel_id=1, source_target_pairs={{4,8},{8,4},{12,16},{16,12},{20,24},{24,20},{5,9},{9,5},{13,17},{1... | collective-permute-start | bytes 1572872 | tf_op jit(solution)/shard_map/ppermute | solution.py:27
  35.3 26.9 %collective-permute-start.5 = (f32[4,128,128]{2,1,0:T(8,128)S(1)}, f32[4,128,128]{2,1,0:T(8,128)S(1)}, u32[]{:S(2)}, u32[]{:S(2)}) collective-permute-start(f32[4,128,128]{2,1,0:T(8,128)S(1)} %shard_map.41.kept_ref), channel_id=1, source_target_pairs={{0,16},{4,20},{8,24},{12,28},{16,0},{20,4},{24,8},{28,12},{1,17},{... | collective-permute-start | bytes 786440 | tf_op jit(solution)/shard_map/ppermute | solution.py:19
  62.7 5.0 %collective-permute-start.10 = (f32[2,128,128]{2,1,0:T(8,128)S(1)}, f32[2,128,128]{2,1,0:T(8,128)S(1)}, u32[]{:S(2)}, u32[]{:S(2)}) collective-permute-start(f32[2,128,128]{2,1,0:T(8,128)S(1)} %get-tuple-element.45), channel_id=1, source_target_pairs={{0,2},{1,3},{2,0},{3,1},{4,6},{5,7},{6,4},{7,5},{8,10},{9,11},{10,... | collective-permute-start | bytes 393224 | tf_op jit(solution)/shard_map/ppermute | solution.py:19
  67.8 1.4 %collective-permute-start.11 = (f32[2,128,128]{2,1,0:T(8,128)S(1)}, f32[2,128,128]{2,1,0:T(8,128)S(1)}, u32[]{:S(2)}, u32[]{:S(2)}) collective-permute-start(f32[2,128,128]{2,1,0:T(8,128)S(1)} %get-tuple-element.47), channel_id=1, source_target_pairs={{0,1},{1,0},{2,3},{3,2},{4,5},{5,4},{6,7},{7,6},{8,9},{9,8},{10,11... | collective-permute-start | bytes 393224 | tf_op jit(solution)/shard_map/ppermute | solution.py:19
  69.2 8.4 %collective-permute-start.13 = (f32[4,128,128]{2,1,0:T(8,128)S(1)}, f32[4,128,128]{2,1,0:T(8,128)S(1)}, u32[]{:S(2)}, u32[]{:S(2)}) collective-permute-start(f32[4,128,128]{2,1,0:T(8,128)S(1)} %shard_map.45.refs_0_), channel_id=1, source_target_pairs={{0,4},{4,0},{8,12},{12,8},{16,20},{20,16},{24,28},{28,24},{1,5},{5... | collective-permute-start | bytes 786440 | tf_op jit(solution)/shard_map/ppermute | solution.py:19
  69.3 8.4 %collective-permute-start.12 = (f32[4,128,128]{2,1,0:T(8,128)S(1)}, f32[4,128,128]{2,1,0:T(8,128)S(1)}, u32[]{:S(2)}, u32[]{:S(2)}) collective-permute-start(f32[4,128,128]{2,1,0:T(8,128)S(1)} %shard_map.45.refs_0_), channel_id=1, source_target_pairs={{0,8},{4,12},{8,0},{12,4},{16,24},{20,28},{24,16},{28,20},{1,9},{5... | collective-permute-start | bytes 786440 | tf_op jit(solution)/shard_map/ppermute | solution.py:19
  77.6 7.5 %collective-permute-start.14 = (f32[4,128,128]{2,1,0:T(8,128)S(1)}, f32[4,128,128]{2,1,0:T(8,128)S(1)}, u32[]{:S(2)}, u32[]{:S(2)}) collective-permute-start(f32[4,128,128]{2,1,0:T(8,128)S(1)} %collective-permute-done.13.refs_2_), channel_id=1, source_target_pairs={{0,8},{4,12},{8,0},{12,4},{16,24},{20,28},{24,16},{28,20},{1,9},{5... | collective-permute-start | bytes 786440 | tf_op jit(solution)/shard_map/ppermute | solution.py:19

commit v2 on v1

--- a/solution.py
+++ b/solution.py
@@ -11,7 +11,6 @@
 SMEM = pl.BlockSpec(memory_space=pltpu.SMEM)
 HBM = pl.BlockSpec(memory_space=pltpu.HBM)
 F32, BF16 = jnp.float32, jnp.bfloat16
-SPREAD = (0, 2, 1, 3)
 
 
 def flip(x, axis, bit):
@@ -52,24 +51,7 @@
     return dot(a_hi, b_hi) + (dot(a_hi, b_lo) + dot(a_lo, b_hi))
 
 
-def prepare_kernel(pair_ref, rot_ref, give_ref, keep_ref, edge_ref, rest_ref, sem):
-    pairs, piece, width = rot_ref.shape
-    half = width // 2
-    last = pairs - 1
-    side = lax.axis_index("loop") % 2
-    away = pl.multiple_of((1 - side) * half, half)
-    home = pl.multiple_of(side * half, half)
-    copies = []
-    for t in range(give_ref.shape[0]):
-        copies.append((rot_ref.at[pair_ref[t] % pairs, :, pl.ds(away, half)], give_ref.at[t]))
-    copies.append((rot_ref.at[0, :, half:], edge_ref.at[0]))
-    copies.append((rot_ref.at[last, :, :half], edge_ref.at[1]))
-    for t in range(give_ref.shape[0]):
-        copies.append((rot_ref.at[pair_ref[t] % pairs, :, pl.ds(home, half)], keep_ref.at[t]))
-    copies.append((rot_ref.at[0, :, :half], rest_ref.at[:, :half]))
-    for p in range(1, last):
-        copies.append((rot_ref.at[p], rest_ref.at[:, half + (p - 1) * width : half + p * width]))
-    copies.append((rot_ref.at[last, :, half:], rest_ref.at[:, half + (last - 1) * width :]))
+def copy_all(copies, sem):
     copies = [pltpu.make_async_copy(src, dst, sem.at[n]) for n, (src, dst) in enumerate(copies)]
     for copy in copies:
         copy.start()
@@ -77,19 +59,62 @@
         copy.wait()
 
 
+def candidate_kernel(home, pair_ref, rot_ref, a_ref, b_ref, sem):
+    pairs, piece, width = rot_ref.shape
+    chunk, half, quarter = piece // 2, width // 2, width // 4
+    l = lax.axis_index("loop")
+    side, up = l % 2, (l // 2) % 2
+    if not home:
+        side, up = 1 - side, 1 - up
+    copies = []
+    for t in range(a_ref.shape[0]):
+        slot = pair_ref[t] % pairs
+        copies.append((rot_ref.at[slot, :chunk, pl.ds(pl.multiple_of(side * half, half), half)], a_ref.at[t]))
+        for s in range(2):
+            cols = pl.ds(pl.multiple_of(s * half + up * quarter, quarter), quarter)
+            copies.append((rot_ref.at[slot, chunk:, cols], b_ref.at[t, :, s * quarter : (s + 1) * quarter]))
+    copy_all(copies, sem)
+
+
+def cut_kernel(rot_ref, edge_ref, rest_ref, sem):
+    pairs, _, width = rot_ref.shape
+    half, last = width // 2, pairs - 1
+    copies = [
+        (rot_ref.at[0, :, half:], edge_ref.at[0]),
+        (rot_ref.at[last, :, :half], edge_ref.at[1]),
+        (rot_ref.at[0, :, :half], rest_ref.at[:, :half]),
+        (rot_ref.at[last, :, half:], rest_ref.at[:, half + (last - 1) * width :]),
+    ]
+    for p in range(1, last):
+        copies.append((rot_ref.at[p], rest_ref.at[:, half + (p - 1) * width : half + p * width]))
+    copy_all(copies, sem)
+
+
 def take(pair_ref, pairs, bit, t, kept, got):
     l = lax.axis_index("loop")
     return jnp.where(((pair_ref[t] // pairs) & bit) == (l & bit), kept, got)
 
 
-def halve_kernel(pairs, bit, pair_ref, kept_ref, got_ref, give_ref, keep_ref):
-    half = give_ref.shape[-1]
-    up = (lax.axis_index("loop") // (2 * bit)) % 2
-    away = pl.ds(pl.multiple_of((1 - up) * half, half), half)
-    home = pl.ds(pl.multiple_of(up * half, half), half)
-    for t in range(give_ref.shape[0]):
-        give_ref[t] = take(pair_ref, pairs, bit, t, kept_ref[t, :, away], got_ref[t, :, away])
-        keep_ref[t] = take(pair_ref, pairs, bit, t, kept_ref[t, :, home], got_ref[t, :, home])
+def halve_kernel(pairs, pair_ref, a_kept, b_kept, a_got, b_got, a_give, b_give, a_keep, b_keep):
+    l = lax.axis_index("loop")
+    quarter = a_give.shape[-1]
+    side, up = l % 2, (l // 2) % 2
+    for bit, cut, kept, got, give, keep in (
+        (1, up, a_kept, a_got, a_give, a_keep),
+        (2, side, b_kept, b_got, b_give, b_keep),
+    ):
+        away = pl.ds(pl.multiple_of((1 - cut) * quarter, quarter), quarter)
+        home = pl.ds(pl.multiple_of(cut * quarter, quarter), quarter)
+        for t in range(give.shape[0]):
+            give[t] = take(pair_ref, pairs, bit, t, kept[t, :, away], got[t, :, away])
+            keep[t] = take(pair_ref, pairs, bit, t, kept[t, :, home], got[t, :, home])
+
+
+def meet_kernel(pairs, pair_ref, a_kept, b_kept, a_got, b_got, out_ref):
+    chunk = a_kept.shape[1]
+    for t in range(out_ref.shape[0]):
+        out_ref[t, :chunk] = take(pair_ref, pairs, 2, t, a_kept[t], a_got[t])
+        out_ref[t, chunk:] = take(pair_ref, pairs, 1, t, b_kept[t], b_got[t])
 
 
 def pick_kernel(pairs, bit, pair_ref, kept_ref, got_ref, out_ref):
@@ -109,11 +134,6 @@
     for n, ref in enumerate((kept_ref, got_ref)):
         give_ref[n] = ref[1 - odd]
         keep_ref[n] = ref[odd]
-
-
-def join_kernel(a_ref, b_ref, out_ref):
-    out_ref[:2] = a_ref[...]
-    out_ref[2:] = b_ref[...]
 
 
 def split_kernel(slab_ref, hi_ref, lo_ref):
@@ -188,20 +208,21 @@
 
 
 def left_kernel(*refs):
-    pieces, (thi_ref, tlo_ref, even_ref, odd_ref, out_ref, rot_ref, hi_ref, lo_ref) = refs[:4], refs[4:]
+    pieces, (thi_ref, tlo_ref, even_ref, odd_ref, out_ref, rot_ref, hi_ref, lo_ref) = refs[:8], refs[8:]
     k = pl.program_id(0)
     blocks = thi_ref.shape[0]
-    teams, piece, quarter = pieces[0].shape
+    _, piece, quarter = pieces[0].shape
     l, loops = lax.axis_index("loop"), lax.axis_size("loop")
     r = lax.axis_index("row")
 
     @pl.when(k == 0)
     def _():
         mine = 2 * (l % 2) + (l // 2) % 2
-        for which, block in enumerate(pieces):
+        for place, block in enumerate(pieces):
+            which, core = divmod(place, 2)
             cols = pl.ds(pl.multiple_of((mine ^ which) * quarter, quarter), quarter)
-            for n, there in enumerate(SPREAD):
-                rows = pl.ds(pl.multiple_of((r ^ there) * piece, piece), piece)
+            for n in range(2):
+                rows = pl.ds(pl.multiple_of((r ^ (2 * n + core)) * piece, piece), piece)
                 rot_ref[rows, cols] = block[n]
         hi_ref[...], lo_ref[...] = split(rot_ref[...].T)
 
@@ -245,22 +266,31 @@
             cost_estimate=cost(0, 0),
         )(*([slab_pair] * pair), *operands)
 
-    give, keep, edge, rest = pl.pallas_call(
-        prepare_kernel,
-        out_shape=(
-            array((teams, piece, half), F32),
-            array((teams, piece, half), F32),
-            array((2, piece, half), F32),
-            array((piece, last * width), F32),
-        ),
-        in_specs=[SMEM, HBM],
-        out_specs=(VMEM,) * 4,
-        scratch_shapes=[pltpu.SemaphoreType.DMA((2 * teams + 2 + pairs,))],
-        compiler_params=params(8),
-        cost_estimate=cost(0, 0),
-    )(slab_pair, pltpu.with_memory_space_constraint(rotations, pltpu.HBM))
-
-    got = flip(give, "loop", 1)
+    def copied(kernel, shapes, count, pair=False):
+        return pl.pallas_call(
+            kernel,
+            out_shape=tuple(array(shape, F32) for shape in shapes),
+            in_specs=[SMEM] * pair + [HBM],
+            out_specs=(VMEM,) * len(shapes),
+            scratch_shapes=[pltpu.SemaphoreType.DMA((count,))],
+            compiler_params=params(4),
+            cost_estimate=cost(0, 0),
+        )
+
+    transforms = pltpu.with_memory_space_constraint(rotations, pltpu.HBM)
+    chunks = (teams, piece // 2, half)
+    a_give, b_give = copied(partial(candidate_kernel, False), (chunks, chunks), 3 * teams, pair=True)(
+        slab_pair, transforms
+    )
+    edge, rest = copied(cut_kernel, ((2, piece, half), (piece, last * width)), pairs + 2)(
+        after(transforms, a_give)
+    )
+    a_keep, b_keep = copied(partial(candidate_kernel, True), (chunks, chunks), 3 * teams, pair=True)(
+        slab_pair, after(transforms, edge)
+    )
+
+    a_got = flip(a_give, "loop", 1)
+    b_got = flip(b_give, "loop", 2)
     far_edge = flip(edge, "row", 2)
     core = flip(rotations, "row", 1)
 
@@ -272,10 +302,18 @@
         out_specs=(pl.BlockSpec((rows // 4, columns), lambda i: (i, 0)),) * 2,
         compiler_params=params(8),
         cost_estimate=cost(0, 0),
-    )(pltpu.with_memory_space_constraint(after(slab, give), pltpu.HBM))
-
-    far_edge = after(far_edge, slab_hi)
-    far_core_edge = flip(far_edge, "row", 1)
+    )(pltpu.with_memory_space_constraint(after(slab, a_keep), pltpu.HBM))
+
+    fine = (teams, piece // 2, quarter)
+    a_give, b_give, a_keep, b_keep = glue(
+        partial(halve_kernel, pairs), (fine,) * 4, a_keep, b_keep, a_got, b_got, pair=True
+    )
+    a_got = flip(a_give, "loop", 2)
+    b_got = flip(b_give, "loop", 1)
+    far_edge = after(far_edge, slab_hi, a_got, b_got)
+    quarters = (teams, piece, quarter)
+    (held,) = glue(partial(meet_kernel, pairs), (quarters,), a_keep, b_keep, a_got, b_got, pair=True)
+    far_core_edge = after(flip(far_edge, "row", 1), held)
     far = flip(after(rest, far_edge), "row", 2)
 
     even, odd = pl.pallas_call(
@@ -299,13 +337,14 @@
         cost_estimate=cost(0, 0),
     )(slab_hi, slab_lo, slab_hi, slab_lo, edge, core, core, far_edge, far_core_edge)
     even_in = trade(even, 0)
-    odd_in = trade(odd, 1)
-
-    quarters = (teams, piece, quarter)
-    give, held = glue(partial(halve_kernel, pairs, 1), (quarters, quarters), keep, after(got, even), pair=True)
-    got = flip(give, "loop", 2)
-    far = after(far, got)
-    far_core = flip(far, "row", 1)
+    odd_in = trade(after(odd, even_in), 1)
+
+    bits = [1 << b for b in range(2, (loops - 1).bit_length())]
+    got = flip(held, "loop", bits[0])
+    for bit in bits[:-1]:
+        (held,) = glue(partial(pick_kernel, pairs, bit), (quarters,), held, got, pair=True)
+        got = flip(held, "loop", 2 * bit)
+    far_core = flip(after(far, even_in, got), "row", 1)
     blocks = array((2 * pairs, rows, half), BF16)
     turned_hi, turned_lo = pl.pallas_call(
         turn_kernel,
@@ -317,30 +356,25 @@
         cost_estimate=cost(0, 0),
     )(slab_hi, slab_lo, rest, core, far, far_core, even, odd)
 
-    bits = [1 << b for b in range(1, (loops - 1).bit_length())]
-    for bit in bits[:-1]:
-        (held,) = glue(partial(pick_kernel, pairs, bit), (quarters,), held, got, pair=True)
-        got = flip(held, "loop", 2 * bit)
-    got = after(got, turned_hi, even_in, odd_in)
     pieces = (2, piece, quarter)
     give, held = glue(partial(last_pick_kernel, pairs, bits[-1]), (pieces, pieces), held, got, pair=True)
-    give, held = glue(cross_kernel, (pieces, pieces), held, flip(give, "row", 2))
-    (held,) = glue(join_kernel, (quarters,), held, flip(give, "row", 1))
-
-    near = flip(held, "loop", 2)
-    side = flip(held, "loop", 1)
-    across = flip(side, "loop", 2)
+    give, held = glue(cross_kernel, (pieces, pieces), held, after(flip(give, "row", 2), odd_in))
+    more = flip(give, "row", 1)
+
+    near = flip(held, "loop", 2), flip(more, "loop", 2)
+    side = flip(held, "loop", 1), flip(more, "loop", 1)
+    across = flip(near[0], "loop", 1), flip(side[1], "loop", 2)
 
     return pl.pallas_call(
         left_kernel,
         grid=(2 * pairs,),
         out_shape=array((rows, columns), F32),
-        in_specs=[VMEM] * 8,
+        in_specs=[VMEM] * 12,
         out_specs=pl.BlockSpec((rows, half), lambda k: (0, k)),
         scratch_shapes=[pltpu.VMEM((width, width), F32)] + [pltpu.VMEM((width, width), BF16)] * 2,
         compiler_params=params(28),
         cost_estimate=cost(0, 0),
-    )(held, near, side, across, turned_hi, turned_lo, even_in, odd_in)
+    )(held, more, *near, *side, *across, turned_hi, turned_lo, even_in, odd_in)
 
 
 def solution(mesh):

time: 92 us -> 73.5 us (0.80)
  waiting for transfers between devices: 55.1 us -> 22.1 us
  starting transfers between devices: 17.3 us -> 29.2 us
  Pallas kernels: 18.6 us -> 21 us
    ppermute x13 -> x18, waiting for transfers between devices: 41 us -> 11.1 us  [flip(): return lax.ppermute(x, axis, [(i, i ^ bit) for i in range(n)])]
    ppermute x13 -> x18, starting transfers between devices: 15.1 us -> 28 us  [flip(): return lax.ppermute(x, axis, [(i, i ^ bit) for i in range(n)])]
    ppermute x2, waiting for transfers between devices: 14.2 us -> 11 us  [trade(): return lax.ppermute(x, 'loop', pairs)]
    pallas_call x1 -> x3, Pallas kernels: 2.35 us -> 4.76 us  [the longest x1 1.71 us: per_device(): copied(partial(candidate_kernel, True), (chunks, chunks), 3 * teams, pair...]
    ppermute x2, starting transfers between devices: 2.27 us -> 1.26 us  [trade(): return lax.ppermute(x, 'loop', pairs)]
  transfers between devices with their start and end apart: 15 -> 20, of which waited for: 11 -> 11; matrix products, arithmetic and copies ran while one was open for 0% -> 0% of each run, Pallas kernels for 12% -> 20%
where the time goes in v2:
time: 73.5 us; the launch traced here: 73.1 us
  starting transfers between devices  29.2 us (40%)
  waiting for transfers between devices  22.1 us (30%)
  Pallas kernels  21 us (29%)
    ppermute x18, starting transfers between devices, flip(): return lax.ppermute(x, axis, [(i, i ^ bit) for i in range(n)])  28 us
    ppermute x18, waiting for transfers between devices, flip(): return lax.ppermute(x, axis, [(i, i ^ bit) for i in range(n)])  11.1 us
    ppermute x2, waiting for transfers between devices, trade(): return lax.ppermute(x, 'loop', pairs)  11 us
    pallas_call x1, Pallas kernels, per_device(): pl.pallas_call(left_kernel, grid=(2 * pairs,), out_shape=array((rows, col...  6.67 us
    pallas_call x1, Pallas kernels, per_device(): pl.pallas_call(turn_kernel, out_shape=(blocks, blocks), in_specs=[VMEM] *...  3.41 us
    pallas_call x1, Pallas kernels, per_device(): pl.pallas_call(split_kernel, grid=(4,), out_shape=(array((rows, columns),...  3.14 us
    pallas_call x4, Pallas kernels, glue(): pl.pallas_call(kernel, out_shape=tuple((array(shape, F32) for shape in sh...  1.83 us
    pallas_call x1, Pallas kernels, per_device(): copied(partial(candidate_kernel, True), (chunks, chunks), 3 * teams, pair...  1.71 us
  transfers between devices with their start and end apart: 20, of which 11 were waited for; matrix products, arithmetic and copies ran while one was open for 0% of the time, Pallas kernels for 20%

profile of v2, /device:TPU:0, one launch (start us, length us, event | category | flops | bytes accessed | tf_op | source)
XLA Modules:
  0.0 73.1 jit_solution(2519500079266419336)
XLA Ops:
  0.0 0.5 collective-permute-start.6
  0.5 0.0 copy-start
  0.5 0.7 copy-done
  1.1 1.7 %shard_map.37 = (f32[4,64,256]{2,1,0:T(8,128)S(1)}, f32[4,64,256]{2,1,0:T(8,128)S(1)}) custom-call(s32[4]{0:T(128)S(1)} %copy-done, f32[4,128,512]{2,1,0:T(8,128)} %rot_ref.3), custom_call_target="tpu_custom_call" | custom-call | tf_op jit(solution)/shard_map/pallas_call | solution.py:282
  2.8 2.6 %collective-permute-start = (f32[4,64,256]{2,1,0:T(8,128)S(1)}, f32[4,64,256]{2,1,0:T(8,128)S(1)}, u32[]{:S(2)}, u32[]{:S(2)}) collective-permute-start(f32[4,64,256]{2,1,0:T(8,128)S(1)} %get-tuple-element.34), channel_id=1, source_target_pairs={{0,4},{4,0},{8,12},{12,8},{16,20},{20,16},{24,28},{28,24},{1,5},{5... | collective-permute-start | bytes 786440 | tf_op jit(solution)/shard_map/ppermute | solution.py:18
  5.4 1.6 %collective-permute-start.1 = (f32[4,64,256]{2,1,0:T(8,128)S(1)}, f32[4,64,256]{2,1,0:T(8,128)S(1)}, u32[]{:S(2)}, u32[]{:S(2)}) collective-permute-start(f32[4,64,256]{2,1,0:T(8,128)S(1)} %get-tuple-element.40), channel_id=1, source_target_pairs={{0,8},{4,12},{8,0},{12,4},{16,24},{20,28},{24,16},{28,20},{1,9},{5... | collective-permute-start | bytes 786440 | tf_op jit(solution)/shard_map/ppermute | solution.py:18
  7.0 1.3 %shard_map.38 = (f32[2,128,256]{2,1,0:T(8,128)S(1)}, f32[128,1536]{1,0:T(8,128)S(1)}) custom-call(f32[4,128,512]{2,1,0:T(8,128)} %rot_ref.3), custom_call_target="tpu_custom_call" | custom-call | tf_op jit(solution)/shard_map/pallas_call | solution.py:285
  8.3 1.6 %collective-permute-start.7 = (f32[2,128,256]{2,1,0:T(8,128)S(1)}, f32[2,128,256]{2,1,0:T(8,128)S(1)}, u32[]{:S(2)}, u32[]{:S(2)}) collective-permute-start(f32[2,128,256]{2,1,0:T(8,128)S(1)} %get-tuple-element.36.own_ref), channel_id=1, source_target_pairs={{0,2},{1,3},{2,0},{3,1},{4,6},{5,7},{6,4},{7,5},{8,10},{9,11},{10,... | collective-permute-start | bytes 786440 | tf_op jit(solution)/shard_map/ppermute | solution.py:18
  9.9 1.7 %shard_map.39 = (f32[4,64,256]{2,1,0:T(8,128)S(1)}, f32[4,64,256]{2,1,0:T(8,128)S(1)}) custom-call(s32[4]{0:T(128)S(1)} %copy-done, f32[4,128,512]{2,1,0:T(8,128)} %rot_ref.3), custom_call_target="tpu_custom_call" | custom-call | tf_op jit(solution)/shard_map/pallas_call | solution.py:288
  11.6 0.8 %collective-permute-done.a_got = f32[4,64,256]{2,1,0:T(8,128)S(1)} collective-permute-done((f32[4,64,256]{2,1,0:T(8,128)S(1)}, f32[4,64,256]{2,1,0:T(8,128)S(1)}, u32[]{:S(2)}, u32[]{:S(2)}) %collective-permute-start) | collective-permute-done | bytes 262176 | tf_op jit(solution)/shard_map/ppermute | solution.py:18
  12.4 1.5 %collective-permute-done.1.b_got = f32[4,64,256]{2,1,0:T(8,128)S(1)} collective-permute-done((f32[4,64,256]{2,1,0:T(8,128)S(1)}, f32[4,64,256]{2,1,0:T(8,128)S(1)}, u32[]{:S(2)}, u32[]{:S(2)}) %collective-permute-start.1) | collective-permute-done | bytes 262176 | tf_op jit(solution)/shard_map/ppermute | solution.py:18
  13.8 0.6 shard_map.40
  14.5 1.6 %collective-permute-start.2 = (f32[4,64,128]{2,1,0:T(8,128)S(1)}, f32[4,64,128]{2,1,0:T(8,128)S(1)}, u32[]{:S(2)}, u32[]{:S(2)}) collective-permute-start(f32[4,64,128]{2,1,0:T(8,128)S(1)} %get-tuple-element.43), channel_id=1, source_target_pairs={{0,8},{4,12},{8,0},{12,4},{16,24},{20,28},{24,16},{28,20},{1,9},{5... | collective-permute-start | bytes 393224 | tf_op jit(solution)/shard_map/ppermute | solution.py:18
  16.1 0.0 copy-start.1
  16.1 0.5 collective-permute-start.3
  16.6 3.1 %shard_map.43 = (bf16[512,2048]{1,0:T(8,128)(2,1)S(1)}, bf16[512,2048]{1,0:T(8,128)(2,1)S(1)}) custom-call(f32[512,2048]{1,0:T(8,128)} %slab_ref), custom_call_target="tpu_custom_call" | custom-call | tf_op jit(solution)/shard_map/pallas_call | solution.py:297
  19.8 0.0 collective-permute-done.7.far_ref
  19.8 0.0 collective-permute-done.2.a_got
  19.8 1.3 %collective-permute-done.3.b_got = f32[4,64,128]{2,1,0:T(8,128)S(1)} collective-permute-done((f32[4,64,128]{2,1,0:T(8,128)S(1)}, f32[4,64,128]{2,1,0:T(8,128)S(1)}, u32[]{:S(2)}, u32[]{:S(2)}) %collective-permute-start.3) | collective-permute-done | bytes 131104 | tf_op jit(solution)/shard_map/ppermute | solution.py:18
  21.1 0.0 collective-permute-start.8
  21.1 1.5 %collective-permute-start.18 = (f32[128,1536]{1,0:T(8,128)S(1)}, f32[128,1536]{1,0:T(8,128)S(1)}, u32[]{:S(2)}, u32[]{:S(2)}) collective-permute-start(f32[128,1536]{1,0:T(8,128)S(1)} %get-tuple-element.59.own_ref), channel_id=1, source_target_pairs={{0,2},{1,3},{2,0},{3,1},{4,6},{5,7},{6,4},{7,5},{8,10},{9,11},{10,... | collective-permute-start | bytes 2359304 | tf_op jit(solution)/shard_map/ppermute | solution.py:18
  22.6 0.0 copy-done.1
  22.6 0.6 shard_map.41.kept_ref
  23.2 0.0 collective-permute-done.8.far_core_ref
  23.2 0.0 collective-permute-done.6.core0.core1.core_ref
  23.2 1.2 %shard_map.44 = (f32[512,256]{1,0:T(8,128)S(1)}, f32[512,256]{1,0:T(8,128)S(1)}) custom-call(bf16[512,2048]{1,0:T(8,128)(2,1)S(1)} %get-tuple-element.48.shi0.shi1.shi_ref, bf16[512,2048]{1,0:T(8,128)(2,1)S(1)} %get-tuple-element.49.slo0.slo1.slo_ref, bf16[512,2048]{1,0:T(8,128)(2,1)S(1)} %get-tuple-element.48.shi0.shi1.shi_ref, ...), custom_call_target="tpu_custom_call" | custom-call | tf_op jit(solution)/shard_map/pallas_call | solution.py:319
  24.4 0.6 collective-permute-start.9
  25.0 2.6 %collective-permute-start.4 = (f32[4,128,128]{2,1,0:T(8,128)S(1)}, f32[4,128,128]{2,1,0:T(8,128)S(1)}, u32[]{:S(2)}, u32[]{:S(2)}) collective-permute-start(f32[4,128,128]{2,1,0:T(8,128)S(1)} %shard_map.41.kept_ref), channel_id=1, source_target_pairs={{0,16},{4,20},{8,24},{12,28},{16,0},{20,4},{24,8},{28,12},{1,17},{... | collective-permute-start | bytes 786440 | tf_op jit(solution)/shard_map/ppermute | solution.py:18
  27.6 11.0 %collective-permute-done.9.refs_10_ = f32[512,256]{1,0:T(8,128)S(1)} collective-permute-done((f32[512,256]{1,0:T(8,128)S(1)}, f32[512,256]{1,0:T(8,128)S(1)}, u32[]{:S(2)}, u32[]{:S(2)}) %collective-permute-start.9) | collective-permute-done | bytes 524320 | tf_op jit(solution)/shard_map/ppermute | solution.py:26
  38.5 0.7 collective-permute-start.10
  39.2 0.3 collective-permute-done.4.got_ref
  39.5 1.5 %collective-permute-done.18.far_ref = f32[128,1536]{1,0:T(8,128)S(1)} collective-permute-done((f32[128,1536]{1,0:T(8,128)S(1)}, f32[128,1536]{1,0:T(8,128)S(1)}, u32[]{:S(2)}, u32[]{:S(2)}) %collective-permute-start.18) | collective-permute-done | bytes 786464 | tf_op jit(solution)/shard_map/ppermute | solution.py:18
  41.1 0.0 collective-permute-start.19
  41.1 0.6 shard_map.42
  41.7 1.6 %collective-permute-start.5 = (f32[2,128,128]{2,1,0:T(8,128)S(1)}, f32[2,128,128]{2,1,0:T(8,128)S(1)}, u32[]{:S(2)}, u32[]{:S(2)}) collective-permute-start(f32[2,128,128]{2,1,0:T(8,128)S(1)} %get-tuple-element.46), channel_id=1, source_target_pairs={{0,2},{1,3},{2,0},{3,1},{4,6},{5,7},{6,4},{7,5},{8,10},{9,11},{10,... | collective-permute-start | bytes 393224 | tf_op jit(solution)/shard_map/ppermute | solution.py:18
  43.2 4.4 %collective-permute-done.5.got_ref = f32[2,128,128]{2,1,0:T(8,128)S(1)} collective-permute-done((f32[2,128,128]{2,1,0:T(8,128)S(1)}, f32[2,128,128]{2,1,0:T(8,128)S(1)}, u32[]{:S(2)}, u32[]{:S(2)}) %collective-permute-start.5) | collective-permute-done | bytes 131104 | tf_op jit(solution)/shard_map/ppermute | solution.py:18
  47.6 0.0 collective-permute-done.10.refs_11_
  47.7 0.1 collective-permute-start.11
  47.7 7.4 %collective-permute-start.12 = (f32[2,128,128]{2,1,0:T(8,128)S(1)}, f32[2,128,128]{2,1,0:T(8,128)S(1)}, u32[]{:S(2)}, u32[]{:S(2)}) collective-permute-start(f32[2,128,128]{2,1,0:T(8,128)S(1)} %get-tuple-element.56.refs_0_), channel_id=1, source_target_pairs={{0,8},{4,12},{8,0},{12,4},{16,24},{20,28},{24,16},{28,20},{1,9},{5... | collective-permute-start | bytes 393224 | tf_op jit(solution)/shard_map/ppermute | solution.py:18
  55.2 0.0 collective-permute-done.11.refs_1_
  55.2 1.6 %collective-permute-start.15 = (f32[2,128,128]{2,1,0:T(8,128)S(1)}, f32[2,128,128]{2,1,0:T(8,128)S(1)}, u32[]{:S(2)}, u32[]{:S(2)}) collective-permute-start(f32[2,128,128]{2,1,0:T(8,128)S(1)} %collective-permute-done.11.refs_1_), channel_id=1, source_target_pairs={{0,4},{4,0},{8,12},{12,8},{16,20},{20,16},{24,28},{28,24},{1,5},{5... | collective-permute-start | bytes 393224 | tf_op jit(solution)/shard_map/ppermute | solution.py:18
  56.7 0.5 collective-permute-start.14
  57.2 1.3 %collective-permute-start.13 = (f32[2,128,128]{2,1,0:T(8,128)S(1)}, f32[2,128,128]{2,1,0:T(8,128)S(1)}, u32[]{:S(2)}, u32[]{:S(2)}) collective-permute-start(f32[2,128,128]{2,1,0:T(8,128)S(1)} %collective-permute-done.11.refs_1_), channel_id=1, source_target_pairs={{0,8},{4,12},{8,0},{12,4},{16,24},{20,28},{24,16},{28,20},{1,9},{5... | collective-permute-start | bytes 393224 | tf_op jit(solution)/shard_map/ppermute | solution.py:18
  58.5 0.8 %collective-permute-done.12.refs_2_ = f32[2,128,128]{2,1,0:T(8,128)S(1)} collective-permute-done((f32[2,128,128]{2,1,0:T(8,128)S(1)}, f32[2,128,128]{2,1,0:T(8,128)S(1)}, u32[]{:S(2)}, u32[]{:S(2)}) %collective-permute-start.12) | collective-permute-done | bytes 131104 | tf_op jit(solution)/shard_map/ppermute | solution.py:18
  59.3 1.9 %collective-permute-start.16 = (f32[2,128,128]{2,1,0:T(8,128)S(1)}, f32[2,128,128]{2,1,0:T(8,128)S(1)}, u32[]{:S(2)}, u32[]{:S(2)}) collective-permute-start(f32[2,128,128]{2,1,0:T(8,128)S(1)} %collective-permute-done.12.refs_2_), channel_id=1, source_target_pairs={{0,4},{4,0},{8,12},{12,8},{16,20},{20,16},{24,28},{28,24},{1,5},{5... | collective-permute-start | bytes 393224 | tf_op jit(solution)/shard_map/ppermute | solution.py:18
  61.1 0.4 collective-permute-done.15.refs_5_
  61.5 1.4 %collective-permute-start.17 = (f32[2,128,128]{2,1,0:T(8,128)S(1)}, f32[2,128,128]{2,1,0:T(8,128)S(1)}, u32[]{:S(2)}, u32[]{:S(2)}) collective-permute-start(f32[2,128,128]{2,1,0:T(8,128)S(1)} %collective-permute-done.15.refs_5_), channel_id=1, source_target_pairs={{0,8},{4,12},{8,0},{12,4},{16,24},{20,28},{24,16},{28,20},{1,9},{5... | collective-permute-start | bytes 393224 | tf_op jit(solution)/shard_map/ppermute | solution.py:18
  62.9 0.0 collective-permute-done.19.far_core_ref
  62.9 3.4 %shard_map.46 = (bf16[8,512,256]{2,1,0:T(8,128)(2,1)S(1)}, bf16[8,512,256]{2,1,0:T(8,128)(2,1)S(1)}) custom-call(bf16[512,2048]{1,0:T(8,128)(2,1)S(1)} %get-tuple-element.48.shi0.shi1.shi_ref, bf16[512,2048]{1,0:T(8,128)(2,1)S(1)} %get-tuple-element.49.slo0.slo1.slo_ref, f32[128,1536]{1,0:T(8,128)S(1)} %get-tuple-element.59.own_ref, ...), custom_call_target="tpu_custom_call" | custom-call | tf_op jit(solution)/shard_map/pallas_call | solution.py:349
  66.3 0.0 collective-permute-done.14.refs_4_
  66.3 0.0 collective-permute-done.13.refs_3_
  66.3 0.1 collective-permute-done.16.refs_6_
  66.3 0.1 collective-permute-done.17.refs_7_
  66.5 6.7 %shard_map.47 = f32[512,2048]{1,0:T(8,128)} custom-call(f32[2,128,128]{2,1,0:T(8,128)S(1)} %get-tuple-element.56.refs_0_, f32[2,128,128]{2,1,0:T(8,128)S(1)} %collective-permute-done.11.refs_1_, f32[2,128,128]{2,1,0:T(8,128)S(1)} %collective-permute-done.12.refs_2_, f32[2,128,128]{2,1,0:T(8,128)S(1)} %collective-permute-done.13.refs_3_, ...), custom_call_target="tpu_custom_call" | custom-call | tf_op jit(solution)/shard_map/pallas_call | solution.py:368
  (1 shorter events, 0.0 us)
Async XLA Ops:
  0.0 23.2 %collective-permute-start.6 = (f32[4,128,512]{2,1,0:T(8,128)}, f32[4,128,512]{2,1,0:T(8,128)S(1)}, u32[]{:S(2)}, u32[]{:S(2)}) collective-permute-start(f32[4,128,512]{2,1,0:T(8,128)} %rot_ref.3), channel_id=1, source_target_pairs={{0,1},{1,0},{2,3},{3,2},{4,5},{5,4},{6,7},{7,6},{8,9},{9,8},{10,11... | collective-permute-start | bytes 3145736 | tf_op jit(solution)/shard_map/ppermute | solution.py:18
  0.5 0.7 copy-start
  2.8 9.6 %collective-permute-start = (f32[4,64,256]{2,1,0:T(8,128)S(1)}, f32[4,64,256]{2,1,0:T(8,128)S(1)}, u32[]{:S(2)}, u32[]{:S(2)}) collective-permute-start(f32[4,64,256]{2,1,0:T(8,128)S(1)} %get-tuple-element.34), channel_id=1, source_target_pairs={{0,4},{4,0},{8,12},{12,8},{16,20},{20,16},{24,28},{28,24},{1,5},{5... | collective-permute-start | bytes 786440 | tf_op jit(solution)/shard_map/ppermute | solution.py:18
  5.4 8.4 %collective-permute-start.1 = (f32[4,64,256]{2,1,0:T(8,128)S(1)}, f32[4,64,256]{2,1,0:T(8,128)S(1)}, u32[]{:S(2)}, u32[]{:S(2)}) collective-permute-start(f32[4,64,256]{2,1,0:T(8,128)S(1)} %get-tuple-element.40), channel_id=1, source_target_pairs={{0,8},{4,12},{8,0},{12,4},{16,24},{20,28},{24,16},{28,20},{1,9},{5... | collective-permute-start | bytes 786440 | tf_op jit(solution)/shard_map/ppermute | solution.py:18
  8.3 11.5 %collective-permute-start.7 = (f32[2,128,256]{2,1,0:T(8,128)S(1)}, f32[2,128,256]{2,1,0:T(8,128)S(1)}, u32[]{:S(2)}, u32[]{:S(2)}) collective-permute-start(f32[2,128,256]{2,1,0:T(8,128)S(1)} %get-tuple-element.36.own_ref), channel_id=1, source_target_pairs={{0,2},{1,3},{2,0},{3,1},{4,6},{5,7},{6,4},{7,5},{8,10},{9,11},{10,... | collective-permute-start | bytes 786440 | tf_op jit(solution)/shard_map/ppermute | solution.py:18
  14.5 5.3 %collective-permute-start.2 = (f32[4,64,128]{2,1,0:T(8,128)S(1)}, f32[4,64,128]{2,1,0:T(8,128)S(1)}, u32[]{:S(2)}, u32[]{:S(2)}) collective-permute-start(f32[4,64,128]{2,1,0:T(8,128)S(1)} %get-tuple-element.43), channel_id=1, source_target_pairs={{0,8},{4,12},{8,0},{12,4},{16,24},{20,28},{24,16},{28,20},{1,9},{5... | collective-permute-start | bytes 393224 | tf_op jit(solution)/shard_map/ppermute | solution.py:18
  16.1 6.5 %copy-start.1 = (s32[4]{0:T(128)S(1)}, s32[4]{0:T(128)}, u32[]{:S(2)}) copy-start(s32[4]{0:T(128)} %pair_ref.9) | copy-start | bytes 52
  16.1 5.0 %collective-permute-start.3 = (f32[4,64,128]{2,1,0:T(8,128)S(1)}, f32[4,64,128]{2,1,0:T(8,128)S(1)}, u32[]{:S(2)}, u32[]{:S(2)}) collective-permute-start(f32[4,64,128]{2,1,0:T(8,128)S(1)} %get-tuple-element.44), channel_id=1, source_target_pairs={{0,4},{4,0},{8,12},{12,8},{16,20},{20,16},{24,28},{28,24},{1,5},{5... | collective-permute-start | bytes 393224 | tf_op jit(solution)/shard_map/ppermute | solution.py:18
  21.1 2.1 %collective-permute-start.8 = (f32[2,128,256]{2,1,0:T(8,128)S(1)}, f32[2,128,256]{2,1,0:T(8,128)S(1)}, u32[]{:S(2)}, u32[]{:S(2)}) collective-permute-start(f32[2,128,256]{2,1,0:T(8,128)S(1)} %collective-permute-done.7.far_ref), channel_id=1, source_target_pairs={{0,1},{1,0},{2,3},{3,2},{4,5},{5,4},{6,7},{7,6},{8,9},{9,8},{10,11... | collective-permute-start | bytes 786440 | tf_op jit(solution)/shard_map/ppermute | solution.py:18
  21.1 20.0 %collective-permute-start.18 = (f32[128,1536]{1,0:T(8,128)S(1)}, f32[128,1536]{1,0:T(8,128)S(1)}, u32[]{:S(2)}, u32[]{:S(2)}) collective-permute-start(f32[128,1536]{1,0:T(8,128)S(1)} %get-tuple-element.59.own_ref), channel_id=1, source_target_pairs={{0,2},{1,3},{2,0},{3,1},{4,6},{5,7},{6,4},{7,5},{8,10},{9,11},{10,... | collective-permute-start | bytes 2359304 | tf_op jit(solution)/shard_map/ppermute | solution.py:18
  24.4 14.1 %collective-permute-start.9 = (f32[512,256]{1,0:T(8,128)S(1)}, f32[512,256]{1,0:T(8,128)S(1)}, u32[]{:S(2)}, u32[]{:S(2)}) collective-permute-start(f32[512,256]{1,0:T(8,128)S(1)} %get-tuple-element.53.even_ref), channel_id=1, source_target_pairs={{0,4},{4,0},{8,12},{12,8},{16,20},{20,16},{24,28},{28,24},{1,5},{5... | collective-permute-start | bytes 1572872 | tf_op jit(solution)/shard_map/ppermute | solution.py:26
  25.0 14.6 %collective-permute-start.4 = (f32[4,128,128]{2,1,0:T(8,128)S(1)}, f32[4,128,128]{2,1,0:T(8,128)S(1)}, u32[]{:S(2)}, u32[]{:S(2)}) collective-permute-start(f32[4,128,128]{2,1,0:T(8,128)S(1)} %shard_map.41.kept_ref), channel_id=1, source_target_pairs={{0,16},{4,20},{8,24},{12,28},{16,0},{20,4},{24,8},{28,12},{1,17},{... | collective-permute-start | bytes 786440 | tf_op jit(solution)/shard_map/ppermute | solution.py:18
  38.5 9.1 %collective-permute-start.10 = (f32[512,256]{1,0:T(8,128)S(1)}, f32[512,256]{1,0:T(8,128)S(1)}, u32[]{:S(2)}, u32[]{:S(2)}) collective-permute-start(f32[512,256]{1,0:T(8,128)S(1)} %get-tuple-element.54.odd_ref), channel_id=1, source_target_pairs={{4,8},{8,4},{12,16},{16,12},{20,24},{24,20},{5,9},{9,5},{13,17},{1... | collective-permute-start | bytes 1572872 | tf_op jit(solution)/shard_map/ppermute | solution.py:26
  41.1 21.8 %collective-permute-start.19 = (f32[128,1536]{1,0:T(8,128)S(1)}, f32[128,1536]{1,0:T(8,128)S(1)}, u32[]{:S(2)}, u32[]{:S(2)}) collective-permute-start(f32[128,1536]{1,0:T(8,128)S(1)} %collective-permute-done.18.far_ref), channel_id=1, source_target_pairs={{0,1},{1,0},{2,3},{3,2},{4,5},{5,4},{6,7},{7,6},{8,9},{9,8},{10,11... | collective-permute-start | bytes 2359304 | tf_op jit(solution)/shard_map/ppermute | solution.py:18
  41.7 6.0 %collective-permute-start.5 = (f32[2,128,128]{2,1,0:T(8,128)S(1)}, f32[2,128,128]{2,1,0:T(8,128)S(1)}, u32[]{:S(2)}, u32[]{:S(2)}) collective-permute-start(f32[2,128,128]{2,1,0:T(8,128)S(1)} %get-tuple-element.46), channel_id=1, source_target_pairs={{0,2},{1,3},{2,0},{3,1},{4,6},{5,7},{6,4},{7,5},{8,10},{9,11},{10,... | collective-permute-start | bytes 393224 | tf_op jit(solution)/shard_map/ppermute | solution.py:18
  47.7 7.5 %collective-permute-start.11 = (f32[2,128,128]{2,1,0:T(8,128)S(1)}, f32[2,128,128]{2,1,0:T(8,128)S(1)}, u32[]{:S(2)}, u32[]{:S(2)}) collective-permute-start(f32[2,128,128]{2,1,0:T(8,128)S(1)} %get-tuple-element.57), channel_id=1, source_target_pairs={{0,1},{1,0},{2,3},{3,2},{4,5},{5,4},{6,7},{7,6},{8,9},{9,8},{10,11... | collective-permute-start | bytes 393224 | tf_op jit(solution)/shard_map/ppermute | solution.py:18
  47.7 11.5 %collective-permute-start.12 = (f32[2,128,128]{2,1,0:T(8,128)S(1)}, f32[2,128,128]{2,1,0:T(8,128)S(1)}, u32[]{:S(2)}, u32[]{:S(2)}) collective-permute-start(f32[2,128,128]{2,1,0:T(8,128)S(1)} %get-tuple-element.56.refs_0_), channel_id=1, source_target_pairs={{0,8},{4,12},{8,0},{12,4},{16,24},{20,28},{24,16},{28,20},{1,9},{5... | collective-permute-start | bytes 393224 | tf_op jit(solution)/shard_map/ppermute | solution.py:18
  55.2 6.3 %collective-permute-start.15 = (f32[2,128,128]{2,1,0:T(8,128)S(1)}, f32[2,128,128]{2,1,0:T(8,128)S(1)}, u32[]{:S(2)}, u32[]{:S(2)}) collective-permute-start(f32[2,128,128]{2,1,0:T(8,128)S(1)} %collective-permute-done.11.refs_1_), channel_id=1, source_target_pairs={{0,4},{4,0},{8,12},{12,8},{16,20},{20,16},{24,28},{28,24},{1,5},{5... | collective-permute-start | bytes 393224 | tf_op jit(solution)/shard_map/ppermute | solution.py:18
  56.7 9.6 %collective-permute-start.14 = (f32[2,128,128]{2,1,0:T(8,128)S(1)}, f32[2,128,128]{2,1,0:T(8,128)S(1)}, u32[]{:S(2)}, u32[]{:S(2)}) collective-permute-start(f32[2,128,128]{2,1,0:T(8,128)S(1)} %get-tuple-element.56.refs_0_), channel_id=1, source_target_pairs={{0,4},{4,0},{8,12},{12,8},{16,20},{20,16},{24,28},{28,24},{1,5},{5... | collective-permute-start | bytes 393224 | tf_op jit(solution)/shard_map/ppermute | solution.py:18
  57.2 9.1 %collective-permute-start.13 = (f32[2,128,128]{2,1,0:T(8,128)S(1)}, f32[2,128,128]{2,1,0:T(8,128)S(1)}, u32[]{:S(2)}, u32[]{:S(2)}) collective-permute-start(f32[2,128,128]{2,1,0:T(8,128)S(1)} %collective-permute-done.11.refs_1_), channel_id=1, source_target_pairs={{0,8},{4,12},{8,0},{12,4},{16,24},{20,28},{24,16},{28,20},{1,9},{5... | collective-permute-start | bytes 393224 | tf_op jit(solution)/shard_map/ppermute | solution.py:18
  59.3 7.1 %collective-permute-start.16 = (f32[2,128,128]{2,1,0:T(8,128)S(1)}, f32[2,128,128]{2,1,0:T(8,128)S(1)}, u32[]{:S(2)}, u32[]{:S(2)}) collective-permute-start(f32[2,128,128]{2,1,0:T(8,128)S(1)} %collective-permute-done.12.refs_2_), channel_id=1, source_target_pairs={{0,4},{4,0},{8,12},{12,8},{16,20},{20,16},{24,28},{28,24},{1,5},{5... | collective-permute-start | bytes 393224 | tf_op jit(solution)/shard_map/ppermute | solution.py:18
  61.5 5.0 %collective-permute-start.17 = (f32[2,128,128]{2,1,0:T(8,128)S(1)}, f32[2,128,128]{2,1,0:T(8,128)S(1)}, u32[]{:S(2)}, u32[]{:S(2)}) collective-permute-start(f32[2,128,128]{2,1,0:T(8,128)S(1)} %collective-permute-done.15.refs_5_), channel_id=1, source_target_pairs={{0,8},{4,12},{8,0},{12,4},{16,24},{20,28},{24,16},{28,20},{1,9},{5... | collective-permute-start | bytes 393224 | tf_op jit(solution)/shard_map/ppermute | solution.py:18

commit v3 on v2

--- a/solution.py
+++ b/solution.py
@@ -169,83 +169,72 @@
 
 
 def turn_kernel(
-    shi_ref, slo_ref, own_ref, core_ref, far_ref, far_core_ref, even_ref, odd_ref, thi_ref, tlo_ref, hi_ref, lo_ref
+    shi_ref, slo_ref, own_ref, core_ref, far_ref, far_core_ref, even_ref, odd_ref, even_in,
+    thi_ref, tlo_ref, hi_ref, lo_ref,
 ):
     pairs, piece, width = core_ref.shape
     half, last = width // 2, pairs - 1
-    side = lax.axis_index("loop") % 2
+    l, loops = lax.axis_index("loop"), lax.axis_size("loop")
     for p in range(pairs):
         cols = slice(0, half) if p == 0 else slice(half, width) if p == last else slice(0, width)
         at = 0 if p == 0 else half + (p - 1) * width
         here = slice(at, at + cols.stop - cols.start)
         stack_parts(hi_ref, lo_ref, p, (own_ref[:, here], core_ref[p, :, cols], far_ref[:, here], far_core_ref[:, here]))
 
-    def put(block, n):
+    def put(block, k):
         hi, lo = split(block)
-        thi_ref[n] = hi
-        tlo_ref[n] = lo
-
-    for p in range(pairs):
+        thi_ref[:, k * half : (k + 1) * half] = hi
+        tlo_ref[:, k * half : (k + 1) * half] = lo
+
+    for p in range(1, last):
         a_hi, a_lo = (ref[:, p * width : (p + 1) * width] for ref in (shi_ref, slo_ref))
-        if p == 0:
-            put(dot3(a_hi, a_lo, hi_ref[p, :, :half], lo_ref[p, :, :half]), 0)
-        elif p == last:
-            put(dot3(a_hi, a_lo, hi_ref[p, :, :half], lo_ref[p, :, :half]), 2 * p + 1)
-        else:
-            made = dot3(a_hi, a_lo, hi_ref[p], lo_ref[p])
-            put(made[:, :half], 2 * p)
-            put(made[:, half:], 2 * p + 1)
-
-    @pl.when(side == 0)
-    def _():
-        put(odd_ref[...], 1)
-        put(even_ref[...], 2 * last)
-
-    @pl.when(side == 1)
-    def _():
-        put(even_ref[...], 1)
-        put(odd_ref[...], 2 * last)
-
-
-def left_kernel(*refs):
-    pieces, (thi_ref, tlo_ref, even_ref, odd_ref, out_ref, rot_ref, hi_ref, lo_ref) = refs[:8], refs[8:]
-    k = pl.program_id(0)
-    blocks = thi_ref.shape[0]
+        made = dot3(a_hi, a_lo, hi_ref[p], lo_ref[p])
+        put(made[:, :half], 2 * (p + 1))
+        put(made[:, half:], 2 * (p - 1) + 1)
+    a_hi, a_lo = (ref[:, last * width :] for ref in (shi_ref, slo_ref))
+    put(dot3(a_hi, a_lo, hi_ref[last, :, :half], lo_ref[last, :, :half]), 2 * (last - 1) + 1)
+    a_hi, a_lo = (ref[:, :width] for ref in (shi_ref, slo_ref))
+    top = dot3(a_hi, a_lo, hi_ref[0, :, :half], lo_ref[0, :, :half])
+    put(jnp.where(l == 0, top, even_in[...]), 0)
+    put(jnp.where(l == 0, odd_ref[...], top), 2)
+    put(jnp.where(l == loops - 1, odd_ref[...], even_in[...]), 2 * pairs - 1)
+
+
+def left_kernel(offsets, aliased, *refs):
+    count = 2 * len(offsets)
+    pieces, (thi_ref, tlo_ref, odd_ref) = refs[:count], refs[count : count + 3]
+    out_ref, made_ref, rot_ref, hi_ref, lo_ref, sem = refs[count + 3 + aliased :]
     _, piece, quarter = pieces[0].shape
-    l, loops = lax.axis_index("loop"), lax.axis_size("loop")
-    r = lax.axis_index("row")
-
-    @pl.when(k == 0)
-    def _():
-        mine = 2 * (l % 2) + (l // 2) % 2
-        for place, block in enumerate(pieces):
-            which, core = divmod(place, 2)
-            cols = pl.ds(pl.multiple_of((mine ^ which) * quarter, quarter), quarter)
-            for n in range(2):
-                rows = pl.ds(pl.multiple_of((r ^ (2 * n + core)) * piece, piece), piece)
-                rot_ref[rows, cols] = block[n]
-        hi_ref[...], lo_ref[...] = split(rot_ref[...].T)
-
-    from_left = (k == 0) & (l > 0)
-    from_right = (k == blocks - 1) & (l < loops - 1)
-    src = jnp.where(k % 2 == 0, k - 2, k + 2)
-    src = jnp.where(l == 0, jnp.where(k == 0, 0, jnp.where(k == 2, 1, src)), src)
-    src = jnp.where((l == loops - 1) & (k == blocks - 1), blocks - 2, src)
-
-    @pl.when(jnp.logical_not(from_left | from_right))
-    def _():
-        out_ref[...] = dot3(hi_ref[...], lo_ref[...], thi_ref[src], tlo_ref[src])
-
-    by_even = (from_left & (l % 2 == 1)) | (from_right & (l % 2 == 0))
-    by_odd = (from_left & (l % 2 == 0)) | (from_right & (l % 2 == 1))
-
-    @pl.when(by_even)
-    def _():
-        out_ref[...] = dot3(hi_ref[...], lo_ref[...], *split(even_ref[...]))
-
-    @pl.when(by_odd)
-    def _():
-        out_ref[...] = dot3(hi_ref[...], lo_ref[...], *split(odd_ref[...]))
+    width = thi_ref.shape[0]
+    l, r = lax.axis_index("loop"), lax.axis_index("row")
+    mine = 2 * (l % 2) + (l // 2) % 2
+    for place, block in enumerate(pieces):
+        n, core = divmod(place, 2)
+        for m in range(2):
+            rows = pl.ds(pl.multiple_of((r ^ (2 * m + core)) * piece, piece), piece)
+            rot_ref[rows, n * quarter : (n + 1) * quarter] = block[m]
+    hi_ref[...], lo_ref[...] = split(rot_ref[...].T)
+    wide = width // 2
+    blocks = made_ref.shape[1] // wide
+    loops = lax.axis_size("loop")
+    by_odd = {0: (l % 2 == 0) & (l > 0), blocks - 1: (l % 2 == 1) & (l < loops - 1)}
+    copies = []
+    for k in (*range(1, blocks - 1), 0, blocks - 1):
+        cols = slice(k * wide, (k + 1) * wide)
+        t_hi, t_lo = thi_ref[:, cols], tlo_ref[:, cols]
+        if k in by_odd:
+            came_hi, came_lo = split(odd_ref[...])
+            t_hi, t_lo = jnp.where(by_odd[k], came_hi, t_hi), jnp.where(by_odd[k], came_lo, t_lo)
+        made_ref[:, cols] = dot3(hi_ref[...], lo_ref[...], t_hi, t_lo)
+        for n, offset in enumerate(offsets):
+            rows = pl.ds(pl.multiple_of((mine ^ offset) * quarter, quarter), quarter)
+            copy = pltpu.make_async_copy(
+                made_ref.at[n * quarter : (n + 1) * quarter, cols], out_ref.at[rows, cols], sem.at[n, k]
+            )
+            copy.start()
+            copies.append(copy)
+    for copy in copies:
+        copy.wait()
 
 
 def per_device(slab, rotations, slab_pair):
@@ -282,9 +271,7 @@
     a_give, b_give = copied(partial(candidate_kernel, False), (chunks, chunks), 3 * teams, pair=True)(
         slab_pair, transforms
     )
-    edge, rest = copied(cut_kernel, ((2, piece, half), (piece, last * width)), pairs + 2)(
-        after(transforms, a_give)
-    )
+    edge, rest = copied(cut_kernel, ((2, piece, half), (piece, last * width)), pairs + 2)(after(transforms, a_give))
     a_keep, b_keep = copied(partial(candidate_kernel, True), (chunks, chunks), 3 * teams, pair=True)(
         slab_pair, after(transforms, edge)
     )
@@ -306,15 +293,14 @@
 
     fine = (teams, piece // 2, quarter)
     a_give, b_give, a_keep, b_keep = glue(
-        partial(halve_kernel, pairs), (fine,) * 4, a_keep, b_keep, a_got, b_got, pair=True
+        partial(halve_kernel, pairs), (fine,) * 4, a_keep, b_keep, after(a_got, slab_hi), b_got, pair=True
     )
     a_got = flip(a_give, "loop", 2)
     b_got = flip(b_give, "loop", 1)
-    far_edge = after(far_edge, slab_hi, a_got, b_got)
-    quarters = (teams, piece, quarter)
-    (held,) = glue(partial(meet_kernel, pairs), (quarters,), a_keep, b_keep, a_got, b_got, pair=True)
-    far_core_edge = after(flip(far_edge, "row", 1), held)
-    far = flip(after(rest, far_edge), "row", 2)
+
+    far_edge = after(far_edge, a_give)
+    far_core_edge = flip(far_edge, "row", 1)
+    far = flip(after(rest, far_edge, a_got, b_got), "row", 2)
 
     even, odd = pl.pallas_call(
         edge_kernel,
@@ -336,6 +322,8 @@
         compiler_params=params(20),
         cost_estimate=cost(0, 0),
     )(slab_hi, slab_lo, slab_hi, slab_lo, edge, core, core, far_edge, far_core_edge)
+    quarters = (teams, piece, quarter)
+    (held,) = glue(partial(meet_kernel, pairs), (quarters,), a_keep, b_keep, after(a_got, even), b_got, pair=True)
     even_in = trade(even, 0)
     odd_in = trade(after(odd, even_in), 1)
 
@@ -345,36 +333,49 @@
         (held,) = glue(partial(pick_kernel, pairs, bit), (quarters,), held, got, pair=True)
         got = flip(held, "loop", 2 * bit)
     far_core = flip(after(far, even_in, got), "row", 1)
-    blocks = array((2 * pairs, rows, half), BF16)
+    blocks = array((rows, columns), BF16)
     turned_hi, turned_lo = pl.pallas_call(
         turn_kernel,
         out_shape=(blocks, blocks),
-        in_specs=[VMEM] * 8,
+        in_specs=[VMEM] * 9,
         out_specs=(VMEM, VMEM),
         scratch_shapes=[pltpu.VMEM((pairs, width, width), BF16)] * 2,
         compiler_params=params(28),
         cost_estimate=cost(0, 0),
-    )(slab_hi, slab_lo, rest, core, far, far_core, even, odd)
+    )(slab_hi, slab_lo, rest, core, far, far_core, even, odd, even_in)
 
     pieces = (2, piece, quarter)
     give, held = glue(partial(last_pick_kernel, pairs, bits[-1]), (pieces, pieces), held, got, pair=True)
-    give, held = glue(cross_kernel, (pieces, pieces), held, after(flip(give, "row", 2), odd_in))
+    give, held = glue(cross_kernel, (pieces, pieces), held, after(flip(give, "row", 2), turned_hi, odd_in))
     more = flip(give, "row", 1)
 
     near = flip(held, "loop", 2), flip(more, "loop", 2)
     side = flip(held, "loop", 1), flip(more, "loop", 1)
     across = flip(near[0], "loop", 1), flip(side[1], "loop", 2)
 
-    return pl.pallas_call(
-        left_kernel,
-        grid=(2 * pairs,),
-        out_shape=array((rows, columns), F32),
-        in_specs=[VMEM] * 12,
-        out_specs=pl.BlockSpec((rows, half), lambda k: (0, k)),
-        scratch_shapes=[pltpu.VMEM((width, width), F32)] + [pltpu.VMEM((width, width), BF16)] * 2,
-        compiler_params=params(28),
-        cost_estimate=cost(0, 0),
-    )(held, more, *near, *side, *across, turned_hi, turned_lo, even_in, odd_in)
+    def left(offsets, pieces, out=None):
+        tall = len(offsets) * quarter
+        aliased = out is not None
+        return pl.pallas_call(
+            partial(left_kernel, offsets, int(aliased)),
+            out_shape=array((rows, columns), F32),
+            in_specs=[VMEM] * (len(pieces) + 3) + [HBM] * aliased,
+            out_specs=HBM,
+            input_output_aliases={len(pieces) + 3: 0} if aliased else {},
+            scratch_shapes=[
+                pltpu.VMEM((tall, columns), F32),
+                pltpu.VMEM((width, tall), F32),
+                pltpu.VMEM((tall, width), BF16),
+                pltpu.VMEM((tall, width), BF16),
+                pltpu.SemaphoreType.DMA((len(offsets), 2 * pairs)),
+            ],
+            compiler_params=params(20),
+            cost_estimate=cost(0, 0),
+        )(*pieces, turned_hi, turned_lo, odd_in, *([out] * aliased))
+
+    out = left((0,), (held, more))
+    out = left((1, 2), (*near, *side), out)
+    return left((3,), across, out)
 
 
 def solution(mesh):

time: 73.5 us -> 72.3 us (0.984)
  waiting for transfers between devices: 22.1 us -> 19.1 us
  starting transfers between devices: 29.2 us -> 31.1 us
    ppermute x2, waiting for transfers between devices: 11 us -> 0.01 us  [trade(): return lax.ppermute(x, 'loop', pairs)]
    ppermute x18, waiting for transfers between devices: 11.1 us -> 19.1 us  [flip(): return lax.ppermute(x, axis, [(i, i ^ bit) for i in range(n)])]
    ppermute x18, starting transfers between devices: 28 us -> 29.8 us  [flip(): return lax.ppermute(x, axis, [(i, i ^ bit) for i in range(n)])]
    pallas_call x1 -> x3, Pallas kernels: 6.67 us -> 6.56 us  [left(): pl.pallas_call(partial(left_kernel, offsets, int(aliased)), out_shape=arr...]
  transfers between devices with their start and end apart: 20 -> 20, of which waited for: 11 -> 6; matrix products, arithmetic and copies ran while one was open for 0% -> 0% of each run, Pallas kernels for 20% -> 27%
where the time goes in v3:
time: 72.3 us; the launch traced here: 72 us
  starting transfers between devices  31.1 us (43%)
  Pallas kernels  21 us (29%)
  waiting for transfers between devices  19.1 us (26%)
    ppermute x18, starting transfers between devices, flip(): return lax.ppermute(x, axis, [(i, i ^ bit) for i in range(n)])  29.8 us
    ppermute x18, waiting for transfers between devices, flip(): return lax.ppermute(x, axis, [(i, i ^ bit) for i in range(n)])  19.1 us
    pallas_call x3, Pallas kernels, left(): pl.pallas_call(partial(left_kernel, offsets, int(aliased)), out_shape=arr...  6.56 us
    pallas_call x1, Pallas kernels, per_device(): pl.pallas_call(turn_kernel, out_shape=(blocks, blocks), in_specs=[VMEM] *...  3.47 us
    pallas_call x1, Pallas kernels, per_device(): pl.pallas_call(split_kernel, grid=(4,), out_shape=(array((rows, columns),...  3.15 us
    pallas_call x4, Pallas kernels, glue(): pl.pallas_call(kernel, out_shape=tuple((array(shape, F32) for shape in sh...  1.84 us
    pallas_call x1, Pallas kernels, per_device(): copied(partial(candidate_kernel, False), (chunks, chunks), 3 * teams, pai...  1.71 us
    pallas_call x1, Pallas kernels, per_device(): copied(partial(candidate_kernel, True), (chunks, chunks), 3 * teams, pair...  1.71 us
  transfers between devices with their start and end apart: 20, of which 6 were waited for; matrix products, arithmetic and copies ran while one was open for 0% of the time, Pallas kernels for 27%

profile of v3, /device:TPU:0, one launch (start us, length us, event | category | flops | bytes accessed | tf_op | source)
XLA Modules:
  0.0 72.0 jit_solution(17518002300815641639)
XLA Ops:
  0.0 0.5 collective-permute-start.3
  0.5 0.0 copy-start
  0.5 0.7 copy-done
  1.1 0.0 copy-start.1
  1.1 1.7 %shard_map.37 = (f32[4,64,256]{2,1,0:T(8,128)S(1)}, f32[4,64,256]{2,1,0:T(8,128)S(1)}) custom-call(s32[4]{0:T(128)S(1)} %copy-done, f32[4,128,512]{2,1,0:T(8,128)} %rot_ref.3), custom_call_target="tpu_custom_call" | custom-call | tf_op jit(solution)/shard_map/pallas_call | solution.py:271
  2.8 2.6 %collective-permute-start = (f32[4,64,256]{2,1,0:T(8,128)S(1)}, f32[4,64,256]{2,1,0:T(8,128)S(1)}, u32[]{:S(2)}, u32[]{:S(2)}) collective-permute-start(f32[4,64,256]{2,1,0:T(8,128)S(1)} %get-tuple-element.35), channel_id=1, source_target_pairs={{0,4},{4,0},{8,12},{12,8},{16,20},{20,16},{24,28},{28,24},{1,5},{5... | collective-permute-start | bytes 786440 | tf_op jit(solution)/shard_map/ppermute | solution.py:18
  5.4 1.6 %collective-permute-start.1 = (f32[4,64,256]{2,1,0:T(8,128)S(1)}, f32[4,64,256]{2,1,0:T(8,128)S(1)}, u32[]{:S(2)}, u32[]{:S(2)}) collective-permute-start(f32[4,64,256]{2,1,0:T(8,128)S(1)} %get-tuple-element.44), channel_id=1, source_target_pairs={{0,8},{4,12},{8,0},{12,4},{16,24},{20,28},{24,16},{28,20},{1,9},{5... | collective-permute-start | bytes 786440 | tf_op jit(solution)/shard_map/ppermute | solution.py:18
  7.0 1.3 %shard_map.38 = (f32[2,128,256]{2,1,0:T(8,128)S(1)}, f32[128,1536]{1,0:T(8,128)S(1)}) custom-call(f32[4,128,512]{2,1,0:T(8,128)} %rot_ref.3), custom_call_target="tpu_custom_call" | custom-call | tf_op jit(solution)/shard_map/pallas_call | solution.py:274
  8.3 1.6 %collective-permute-start.4 = (f32[2,128,256]{2,1,0:T(8,128)S(1)}, f32[2,128,256]{2,1,0:T(8,128)S(1)}, u32[]{:S(2)}, u32[]{:S(2)}) collective-permute-start(f32[2,128,256]{2,1,0:T(8,128)S(1)} %get-tuple-element.37.own_ref), channel_id=1, source_target_pairs={{0,2},{1,3},{2,0},{3,1},{4,6},{5,7},{6,4},{7,5},{8,10},{9,11},{10,... | collective-permute-start | bytes 786440 | tf_op jit(solution)/shard_map/ppermute | solution.py:18
  9.9 1.7 %shard_map.39 = (f32[4,64,256]{2,1,0:T(8,128)S(1)}, f32[4,64,256]{2,1,0:T(8,128)S(1)}) custom-call(s32[4]{0:T(128)S(1)} %copy-done, f32[4,128,512]{2,1,0:T(8,128)} %rot_ref.3), custom_call_target="tpu_custom_call" | custom-call | tf_op jit(solution)/shard_map/pallas_call | solution.py:275
  11.6 3.2 %shard_map.40 = (bf16[512,2048]{1,0:T(8,128)(2,1)S(1)}, bf16[512,2048]{1,0:T(8,128)(2,1)S(1)}) custom-call(f32[512,2048]{1,0:T(8,128)} %slab_ref), custom_call_target="tpu_custom_call" | custom-call | tf_op jit(solution)/shard_map/pallas_call | solution.py:284
  14.8 0.0 collective-permute-done.a_got
  14.8 0.0 collective-permute-done.1.b_got
  14.8 0.0 copy-done.1
  14.8 0.6 shard_map.41
  15.4 0.7 collective-permute-start.2
  16.1 0.5 collective-permute-start.6
  16.7 0.0 collective-permute-done.4.far_ref
  16.7 0.0 collective-permute-start.5
  16.7 3.9 %collective-permute-done.2.a_got = f32[4,64,128]{2,1,0:T(8,128)S(1)} collective-permute-done((f32[4,64,128]{2,1,0:T(8,128)S(1)}, f32[4,64,128]{2,1,0:T(8,128)S(1)}, u32[]{:S(2)}, u32[]{:S(2)}) %collective-permute-start.2) | collective-permute-done | bytes 131104 | tf_op jit(solution)/shard_map/ppermute | solution.py:18
  20.6 0.5 collective-permute-done.6.b_got
  21.1 1.5 %collective-permute-start.9 = (f32[128,1536]{1,0:T(8,128)S(1)}, f32[128,1536]{1,0:T(8,128)S(1)}, u32[]{:S(2)}, u32[]{:S(2)}) collective-permute-start(f32[128,1536]{1,0:T(8,128)S(1)} %get-tuple-element.56.own_ref), channel_id=1, source_target_pairs={{0,2},{1,3},{2,0},{3,1},{4,6},{5,7},{6,4},{7,5},{8,10},{9,11},{10,... | collective-permute-start | bytes 2359304 | tf_op jit(solution)/shard_map/ppermute | solution.py:18
  22.6 0.0 collective-permute-done.5.far_core_ref
  22.6 0.0 collective-permute-done.3.core0.core1.core_ref
  22.6 1.2 %shard_map.42 = (f32[512,256]{1,0:T(8,128)S(1)}, f32[512,256]{1,0:T(8,128)S(1)}) custom-call(bf16[512,2048]{1,0:T(8,128)(2,1)S(1)} %get-tuple-element.42.shi0.shi1.shi_ref, bf16[512,2048]{1,0:T(8,128)(2,1)S(1)} %get-tuple-element.48.slo0.slo1.slo_ref, bf16[512,2048]{1,0:T(8,128)(2,1)S(1)} %get-tuple-element.42.shi0.shi1.shi_ref, ...), custom_call_target="tpu_custom_call" | custom-call | tf_op jit(solution)/shard_map/pallas_call | solution.py:305
  23.8 0.6 collective-permute-start.10
  24.4 0.6 shard_map.43.kept_ref
  25.0 2.7 %collective-permute-start.7 = (f32[4,128,128]{2,1,0:T(8,128)S(1)}, f32[4,128,128]{2,1,0:T(8,128)S(1)}, u32[]{:S(2)}, u32[]{:S(2)}) collective-permute-start(f32[4,128,128]{2,1,0:T(8,128)S(1)} %shard_map.43.kept_ref), channel_id=1, source_target_pairs={{0,16},{4,20},{8,24},{12,28},{16,0},{20,4},{24,8},{28,12},{1,17},{... | collective-permute-start | bytes 786440 | tf_op jit(solution)/shard_map/ppermute | solution.py:18
  27.6 11.3 %collective-permute-done.9.far_ref = f32[128,1536]{1,0:T(8,128)S(1)} collective-permute-done((f32[128,1536]{1,0:T(8,128)S(1)}, f32[128,1536]{1,0:T(8,128)S(1)}, u32[]{:S(2)}, u32[]{:S(2)}) %collective-permute-start.9) | collective-permute-done | bytes 786464 | tf_op jit(solution)/shard_map/ppermute | solution.py:18
  38.9 0.0 collective-permute-done.7.got_ref
  38.9 0.0 collective-permute-done.10.even_in
  38.9 0.0 collective-permute-start.11
  38.9 0.7 collective-permute-start.12
  39.6 0.6 shard_map.44
  40.2 1.5 %collective-permute-start.8 = (f32[2,128,128]{2,1,0:T(8,128)S(1)}, f32[2,128,128]{2,1,0:T(8,128)S(1)}, u32[]{:S(2)}, u32[]{:S(2)}) collective-permute-start(f32[2,128,128]{2,1,0:T(8,128)S(1)} %get-tuple-element.54), channel_id=1, source_target_pairs={{0,2},{1,3},{2,0},{3,1},{4,6},{5,7},{6,4},{7,5},{8,10},{9,11},{10,... | collective-permute-start | bytes 393224 | tf_op jit(solution)/shard_map/ppermute | solution.py:18
  41.7 0.0 collective-permute-done.11.far_core_ref
  41.7 3.5 %shard_map.45 = (bf16[512,2048]{1,0:T(8,128)(2,1)S(1)}, bf16[512,2048]{1,0:T(8,128)(2,1)S(1)}) custom-call(bf16[512,2048]{1,0:T(8,128)(2,1)S(1)} %get-tuple-element.42.shi0.shi1.shi_ref, bf16[512,2048]{1,0:T(8,128)(2,1)S(1)} %get-tuple-element.48.slo0.slo1.slo_ref, f32[128,1536]{1,0:T(8,128)S(1)} %get-tuple-element.56.own_ref, ...), custom_call_target="tpu_custom_call" | custom-call | tf_op jit(solution)/shard_map/pallas_call | solution.py:337
  45.2 1.0 %collective-permute-done.8.got_ref = f32[2,128,128]{2,1,0:T(8,128)S(1)} collective-permute-done((f32[2,128,128]{2,1,0:T(8,128)S(1)}, f32[2,128,128]{2,1,0:T(8,128)S(1)}, u32[]{:S(2)}, u32[]{:S(2)}) %collective-permute-start.8) | collective-permute-done | bytes 131104 | tf_op jit(solution)/shard_map/ppermute | solution.py:18
  46.2 0.0 collective-permute-done.12.refs_4_.refs_6_
  46.2 0.1 collective-permute-start.15
  46.3 11.5 %collective-permute-start.13 = (f32[2,128,128]{2,1,0:T(8,128)S(1)}, f32[2,128,128]{2,1,0:T(8,128)S(1)}, u32[]{:S(2)}, u32[]{:S(2)}) collective-permute-start(f32[2,128,128]{2,1,0:T(8,128)S(1)} %get-tuple-element.62.refs_0_), channel_id=1, source_target_pairs={{0,8},{4,12},{8,0},{12,4},{16,24},{20,28},{24,16},{28,20},{1,9},{5... | collective-permute-start | bytes 393224 | tf_op jit(solution)/shard_map/ppermute | solution.py:18
  57.8 0.0 collective-permute-done.15.refs_1_
  57.8 0.5 collective-permute-start.16
  58.3 1.5 %collective-permute-start.19 = (f32[2,128,128]{2,1,0:T(8,128)S(1)}, f32[2,128,128]{2,1,0:T(8,128)S(1)}, u32[]{:S(2)}, u32[]{:S(2)}) collective-permute-start(f32[2,128,128]{2,1,0:T(8,128)S(1)} %get-tuple-element.62.refs_0_), channel_id=1, source_target_pairs={{0,4},{4,0},{8,12},{12,8},{16,20},{20,16},{24,28},{28,24},{1,5},{5... | collective-permute-start | bytes 393224 | tf_op jit(solution)/shard_map/ppermute | solution.py:18
  59.8 1.3 %collective-permute-start.18 = (f32[2,128,128]{2,1,0:T(8,128)S(1)}, f32[2,128,128]{2,1,0:T(8,128)S(1)}, u32[]{:S(2)}, u32[]{:S(2)}) collective-permute-start(f32[2,128,128]{2,1,0:T(8,128)S(1)} %collective-permute-done.15.refs_1_), channel_id=1, source_target_pairs={{0,8},{4,12},{8,0},{12,4},{16,24},{20,28},{24,16},{28,20},{1,9},{5... | collective-permute-start | bytes 393224 | tf_op jit(solution)/shard_map/ppermute | solution.py:18
  61.1 0.8 %collective-permute-done.13.refs_0_ = f32[2,128,128]{2,1,0:T(8,128)S(1)} collective-permute-done((f32[2,128,128]{2,1,0:T(8,128)S(1)}, f32[2,128,128]{2,1,0:T(8,128)S(1)}, u32[]{:S(2)}, u32[]{:S(2)}) %collective-permute-start.13) | collective-permute-done | bytes 131104 | tf_op jit(solution)/shard_map/ppermute | solution.py:18
  61.9 0.7 collective-permute-start.14
  62.6 1.6 %collective-permute-done.16.refs_3_ = f32[2,128,128]{2,1,0:T(8,128)S(1)} collective-permute-done((f32[2,128,128]{2,1,0:T(8,128)S(1)}, f32[2,128,128]{2,1,0:T(8,128)S(1)}, u32[]{:S(2)}, u32[]{:S(2)}) %collective-permute-start.16) | collective-permute-done | bytes 131104 | tf_op jit(solution)/shard_map/ppermute | solution.py:18
  64.1 1.3 %collective-permute-start.17 = (f32[2,128,128]{2,1,0:T(8,128)S(1)}, f32[2,128,128]{2,1,0:T(8,128)S(1)}, u32[]{:S(2)}, u32[]{:S(2)}) collective-permute-start(f32[2,128,128]{2,1,0:T(8,128)S(1)} %collective-permute-done.16.refs_3_), channel_id=1, source_target_pairs={{0,8},{4,12},{8,0},{12,4},{16,24},{20,28},{24,16},{28,20},{1,9},{5... | collective-permute-start | bytes 393224 | tf_op jit(solution)/shard_map/ppermute | solution.py:18
  65.4 1.8 %shard_map.47.refs_7_ = f32[512,2048]{1,0:T(8,128)} custom-call(f32[2,128,128]{2,1,0:T(8,128)S(1)} %get-tuple-element.62.refs_0_, f32[2,128,128]{2,1,0:T(8,128)S(1)} %collective-permute-done.15.refs_1_, bf16[512,2048]{1,0:T(8,128)(2,1)S(1)} %get-tuple-element.59.refs_2_.refs_4_, bf16[512,2048]{1,0:T(8,128)(2,1)S(1)} %get-tuple-element.64.refs_3_.refs_5_, ...), custom_call_target="tpu_custom_call" | custom-call | tf_op jit(solution)/shard_map/pallas_call | solution.py:359
  67.2 0.0 collective-permute-done.19.refs_2_
  67.3 0.0 collective-permute-done.18.refs_1_
  67.3 2.9 %shard_map.48.refs_5_ = f32[512,2048]{1,0:T(8,128)} custom-call(f32[2,128,128]{2,1,0:T(8,128)S(1)} %collective-permute-done.13.refs_0_, f32[2,128,128]{2,1,0:T(8,128)S(1)} %collective-permute-done.18.refs_1_, f32[2,128,128]{2,1,0:T(8,128)S(1)} %collective-permute-done.19.refs_2_, ...), custom_call_target="tpu_custom_call", output_to_operand_aliasing={{}: (7, {})} | custom-call | tf_op jit(solution)/shard_map/pallas_call | solution.py:359
  70.1 0.0 collective-permute-done.14.refs_0_
  70.1 0.0 collective-permute-done.17.refs_1_
  70.2 1.9 %shard_map.49 = f32[512,2048]{1,0:T(8,128)} custom-call(f32[2,128,128]{2,1,0:T(8,128)S(1)} %collective-permute-done.14.refs_0_, f32[2,128,128]{2,1,0:T(8,128)S(1)} %collective-permute-done.17.refs_1_, bf16[512,2048]{1,0:T(8,128)(2,1)S(1)} %get-tuple-element.59.refs_2_.refs_4_, ...), custom_call_target="tpu_custom_call", output_to_operand_aliasing={{}: (5, {})} | custom-call | tf_op jit(solution)/shard_map/pallas_call | solution.py:359
  (1 shorter events, 0.0 us)
Async XLA Ops:
  0.0 22.6 %collective-permute-start.3 = (f32[4,128,512]{2,1,0:T(8,128)}, f32[4,128,512]{2,1,0:T(8,128)S(1)}, u32[]{:S(2)}, u32[]{:S(2)}) collective-permute-start(f32[4,128,512]{2,1,0:T(8,128)} %rot_ref.3), channel_id=1, source_target_pairs={{0,1},{1,0},{2,3},{3,2},{4,5},{5,4},{6,7},{7,6},{8,9},{9,8},{10,11... | collective-permute-start | bytes 3145736 | tf_op jit(solution)/shard_map/ppermute | solution.py:18
  0.5 0.7 copy-start
  1.1 13.7 %copy-start.1 = (s32[4]{0:T(128)S(1)}, s32[4]{0:T(128)}, u32[]{:S(2)}) copy-start(s32[4]{0:T(128)} %pair_ref.9) | copy-start | bytes 52
  2.8 11.9 %collective-permute-start = (f32[4,64,256]{2,1,0:T(8,128)S(1)}, f32[4,64,256]{2,1,0:T(8,128)S(1)}, u32[]{:S(2)}, u32[]{:S(2)}) collective-permute-start(f32[4,64,256]{2,1,0:T(8,128)S(1)} %get-tuple-element.35), channel_id=1, source_target_pairs={{0,4},{4,0},{8,12},{12,8},{16,20},{20,16},{24,28},{28,24},{1,5},{5... | collective-permute-start | bytes 786440 | tf_op jit(solution)/shard_map/ppermute | solution.py:18
  5.4 9.4 %collective-permute-start.1 = (f32[4,64,256]{2,1,0:T(8,128)S(1)}, f32[4,64,256]{2,1,0:T(8,128)S(1)}, u32[]{:S(2)}, u32[]{:S(2)}) collective-permute-start(f32[4,64,256]{2,1,0:T(8,128)S(1)} %get-tuple-element.44), channel_id=1, source_target_pairs={{0,8},{4,12},{8,0},{12,4},{16,24},{20,28},{24,16},{28,20},{1,9},{5... | collective-permute-start | bytes 786440 | tf_op jit(solution)/shard_map/ppermute | solution.py:18
  8.3 8.3 %collective-permute-start.4 = (f32[2,128,256]{2,1,0:T(8,128)S(1)}, f32[2,128,256]{2,1,0:T(8,128)S(1)}, u32[]{:S(2)}, u32[]{:S(2)}) collective-permute-start(f32[2,128,256]{2,1,0:T(8,128)S(1)} %get-tuple-element.37.own_ref), channel_id=1, source_target_pairs={{0,2},{1,3},{2,0},{3,1},{4,6},{5,7},{6,4},{7,5},{8,10},{9,11},{10,... | collective-permute-start | bytes 786440 | tf_op jit(solution)/shard_map/ppermute | solution.py:18
  15.4 5.1 %collective-permute-start.2 = (f32[4,64,128]{2,1,0:T(8,128)S(1)}, f32[4,64,128]{2,1,0:T(8,128)S(1)}, u32[]{:S(2)}, u32[]{:S(2)}) collective-permute-start(f32[4,64,128]{2,1,0:T(8,128)S(1)} %get-tuple-element.47), channel_id=1, source_target_pairs={{0,8},{4,12},{8,0},{12,4},{16,24},{20,28},{24,16},{28,20},{1,9},{5... | collective-permute-start | bytes 393224 | tf_op jit(solution)/shard_map/ppermute | solution.py:18
  16.1 5.0 %collective-permute-start.6 = (f32[4,64,128]{2,1,0:T(8,128)S(1)}, f32[4,64,128]{2,1,0:T(8,128)S(1)}, u32[]{:S(2)}, u32[]{:S(2)}) collective-permute-start(f32[4,64,128]{2,1,0:T(8,128)S(1)} %get-tuple-element.52), channel_id=1, source_target_pairs={{0,4},{4,0},{8,12},{12,8},{16,20},{20,16},{24,28},{28,24},{1,5},{5... | collective-permute-start | bytes 393224 | tf_op jit(solution)/shard_map/ppermute | solution.py:18
  16.7 5.9 %collective-permute-start.5 = (f32[2,128,256]{2,1,0:T(8,128)S(1)}, f32[2,128,256]{2,1,0:T(8,128)S(1)}, u32[]{:S(2)}, u32[]{:S(2)}) collective-permute-start(f32[2,128,256]{2,1,0:T(8,128)S(1)} %collective-permute-done.4.far_ref), channel_id=1, source_target_pairs={{0,1},{1,0},{2,3},{3,2},{4,5},{5,4},{6,7},{7,6},{8,9},{9,8},{10,11... | collective-permute-start | bytes 786440 | tf_op jit(solution)/shard_map/ppermute | solution.py:18
  21.1 17.8 %collective-permute-start.9 = (f32[128,1536]{1,0:T(8,128)S(1)}, f32[128,1536]{1,0:T(8,128)S(1)}, u32[]{:S(2)}, u32[]{:S(2)}) collective-permute-start(f32[128,1536]{1,0:T(8,128)S(1)} %get-tuple-element.56.own_ref), channel_id=1, source_target_pairs={{0,2},{1,3},{2,0},{3,1},{4,6},{5,7},{6,4},{7,5},{8,10},{9,11},{10,... | collective-permute-start | bytes 2359304 | tf_op jit(solution)/shard_map/ppermute | solution.py:18
  23.8 15.1 %collective-permute-start.10 = (f32[512,256]{1,0:T(8,128)S(1)}, f32[512,256]{1,0:T(8,128)S(1)}, u32[]{:S(2)}, u32[]{:S(2)}) collective-permute-start(f32[512,256]{1,0:T(8,128)S(1)} %get-tuple-element.50.even_ref), channel_id=1, source_target_pairs={{0,4},{4,0},{8,12},{12,8},{16,20},{20,16},{24,28},{28,24},{1,5},{5... | collective-permute-start | bytes 1572872 | tf_op jit(solution)/shard_map/ppermute | solution.py:26
  25.0 13.9 %collective-permute-start.7 = (f32[4,128,128]{2,1,0:T(8,128)S(1)}, f32[4,128,128]{2,1,0:T(8,128)S(1)}, u32[]{:S(2)}, u32[]{:S(2)}) collective-permute-start(f32[4,128,128]{2,1,0:T(8,128)S(1)} %shard_map.43.kept_ref), channel_id=1, source_target_pairs={{0,16},{4,20},{8,24},{12,28},{16,0},{20,4},{24,8},{28,12},{1,17},{... | collective-permute-start | bytes 786440 | tf_op jit(solution)/shard_map/ppermute | solution.py:18
  38.9 2.8 %collective-permute-start.11 = (f32[128,1536]{1,0:T(8,128)S(1)}, f32[128,1536]{1,0:T(8,128)S(1)}, u32[]{:S(2)}, u32[]{:S(2)}) collective-permute-start(f32[128,1536]{1,0:T(8,128)S(1)} %collective-permute-done.9.far_ref), channel_id=1, source_target_pairs={{0,1},{1,0},{2,3},{3,2},{4,5},{5,4},{6,7},{7,6},{8,9},{9,8},{10,11... | collective-permute-start | bytes 2359304 | tf_op jit(solution)/shard_map/ppermute | solution.py:18
  38.9 7.3 %collective-permute-start.12 = (f32[512,256]{1,0:T(8,128)S(1)}, f32[512,256]{1,0:T(8,128)S(1)}, u32[]{:S(2)}, u32[]{:S(2)}) collective-permute-start(f32[512,256]{1,0:T(8,128)S(1)} %get-tuple-element.60.odd_ref), channel_id=1, source_target_pairs={{4,8},{8,4},{12,16},{16,12},{20,24},{24,20},{5,9},{9,5},{13,17},{1... | collective-permute-start | bytes 1572872 | tf_op jit(solution)/shard_map/ppermute | solution.py:26
  40.2 6.0 %collective-permute-start.8 = (f32[2,128,128]{2,1,0:T(8,128)S(1)}, f32[2,128,128]{2,1,0:T(8,128)S(1)}, u32[]{:S(2)}, u32[]{:S(2)}) collective-permute-start(f32[2,128,128]{2,1,0:T(8,128)S(1)} %get-tuple-element.54), channel_id=1, source_target_pairs={{0,2},{1,3},{2,0},{3,1},{4,6},{5,7},{6,4},{7,5},{8,10},{9,11},{10,... | collective-permute-start | bytes 393224 | tf_op jit(solution)/shard_map/ppermute | solution.py:18
  46.2 11.6 %collective-permute-start.15 = (f32[2,128,128]{2,1,0:T(8,128)S(1)}, f32[2,128,128]{2,1,0:T(8,128)S(1)}, u32[]{:S(2)}, u32[]{:S(2)}) collective-permute-start(f32[2,128,128]{2,1,0:T(8,128)S(1)} %get-tuple-element.63), channel_id=1, source_target_pairs={{0,1},{1,0},{2,3},{3,2},{4,5},{5,4},{6,7},{7,6},{8,9},{9,8},{10,11... | collective-permute-start | bytes 393224 | tf_op jit(solution)/shard_map/ppermute | solution.py:18
  46.3 15.6 %collective-permute-start.13 = (f32[2,128,128]{2,1,0:T(8,128)S(1)}, f32[2,128,128]{2,1,0:T(8,128)S(1)}, u32[]{:S(2)}, u32[]{:S(2)}) collective-permute-start(f32[2,128,128]{2,1,0:T(8,128)S(1)} %get-tuple-element.62.refs_0_), channel_id=1, source_target_pairs={{0,8},{4,12},{8,0},{12,4},{16,24},{20,28},{24,16},{28,20},{1,9},{5... | collective-permute-start | bytes 393224 | tf_op jit(solution)/shard_map/ppermute | solution.py:18
  57.8 6.3 %collective-permute-start.16 = (f32[2,128,128]{2,1,0:T(8,128)S(1)}, f32[2,128,128]{2,1,0:T(8,128)S(1)}, u32[]{:S(2)}, u32[]{:S(2)}) collective-permute-start(f32[2,128,128]{2,1,0:T(8,128)S(1)} %collective-permute-done.15.refs_1_), channel_id=1, source_target_pairs={{0,4},{4,0},{8,12},{12,8},{16,20},{20,16},{24,28},{28,24},{1,5},{5... | collective-permute-start | bytes 393224 | tf_op jit(solution)/shard_map/ppermute | solution.py:18
  58.3 8.9 %collective-permute-start.19 = (f32[2,128,128]{2,1,0:T(8,128)S(1)}, f32[2,128,128]{2,1,0:T(8,128)S(1)}, u32[]{:S(2)}, u32[]{:S(2)}) collective-permute-start(f32[2,128,128]{2,1,0:T(8,128)S(1)} %get-tuple-element.62.refs_0_), channel_id=1, source_target_pairs={{0,4},{4,0},{8,12},{12,8},{16,20},{20,16},{24,28},{28,24},{1,5},{5... | collective-permute-start | bytes 393224 | tf_op jit(solution)/shard_map/ppermute | solution.py:18
  59.8 7.5 %collective-permute-start.18 = (f32[2,128,128]{2,1,0:T(8,128)S(1)}, f32[2,128,128]{2,1,0:T(8,128)S(1)}, u32[]{:S(2)}, u32[]{:S(2)}) collective-permute-start(f32[2,128,128]{2,1,0:T(8,128)S(1)} %collective-permute-done.15.refs_1_), channel_id=1, source_target_pairs={{0,8},{4,12},{8,0},{12,4},{16,24},{20,28},{24,16},{28,20},{1,9},{5... | collective-permute-start | bytes 393224 | tf_op jit(solution)/shard_map/ppermute | solution.py:18
  61.9 8.3 %collective-permute-start.14 = (f32[2,128,128]{2,1,0:T(8,128)S(1)}, f32[2,128,128]{2,1,0:T(8,128)S(1)}, u32[]{:S(2)}, u32[]{:S(2)}) collective-permute-start(f32[2,128,128]{2,1,0:T(8,128)S(1)} %collective-permute-done.13.refs_0_), channel_id=1, source_target_pairs={{0,4},{4,0},{8,12},{12,8},{16,20},{20,16},{24,28},{28,24},{1,5},{5... | collective-permute-start | bytes 393224 | tf_op jit(solution)/shard_map/ppermute | solution.py:18
  64.1 6.0 %collective-permute-start.17 = (f32[2,128,128]{2,1,0:T(8,128)S(1)}, f32[2,128,128]{2,1,0:T(8,128)S(1)}, u32[]{:S(2)}, u32[]{:S(2)}) collective-permute-start(f32[2,128,128]{2,1,0:T(8,128)S(1)} %collective-permute-done.16.refs_3_), channel_id=1, source_target_pairs={{0,8},{4,12},{8,0},{12,4},{16,24},{20,28},{24,16},{28,20},{1,9},{5... | collective-permute-start | bytes 393224 | tf_op jit(solution)/shard_map/ppermute | solution.py:18

commit v4 on v3

--- a/solution.py
+++ b/solution.py
@@ -346,10 +346,10 @@
 
     pieces = (2, piece, quarter)
     give, held = glue(partial(last_pick_kernel, pairs, bits[-1]), (pieces, pieces), held, got, pair=True)
-    give, held = glue(cross_kernel, (pieces, pieces), held, after(flip(give, "row", 2), turned_hi, odd_in))
+    give, held = glue(cross_kernel, (pieces, pieces), held, after(flip(give, "row", 2), turned_hi))
     more = flip(give, "row", 1)
 
-    near = flip(held, "loop", 2), flip(more, "loop", 2)
+    near = after(flip(held, "loop", 2), odd_in), flip(more, "loop", 2)
     side = flip(held, "loop", 1), flip(more, "loop", 1)
     across = flip(near[0], "loop", 1), flip(side[1], "loop", 2)
 

time: 72.3 us -> 68.3 us (0.945)
  starting transfers between devices: 31.1 us -> 23.1 us
  waiting for transfers between devices: 19.1 us -> 23 us
    ppermute x18, starting transfers between devices: 29.8 us -> 21.8 us  [flip(): return lax.ppermute(x, axis, [(i, i ^ bit) for i in range(n)])]
    ppermute x18, waiting for transfers between devices: 19.1 us -> 23 us  [flip(): return lax.ppermute(x, axis, [(i, i ^ bit) for i in range(n)])]
  transfers between devices with their start and end apart: 20 -> 20, of which waited for: 6 -> 6; matrix products, arithmetic and copies ran while one was open for 0% -> 0% of each run, Pallas kernels for 27% -> 28%
where the time goes in v4:
time: 68.3 us; the launch traced here: 67.9 us
  starting transfers between devices  23.1 us (34%)
  waiting for transfers between devices  23 us (34%)
  Pallas kernels  21 us (31%)
    ppermute x18, waiting for transfers between devices, flip(): return lax.ppermute(x, axis, [(i, i ^ bit) for i in range(n)])  23 us
    ppermute x18, starting transfers between devices, flip(): return lax.ppermute(x, axis, [(i, i ^ bit) for i in range(n)])  21.8 us
    pallas_call x3, Pallas kernels, left(): pl.pallas_call(partial(left_kernel, offsets, int(aliased)), out_shape=arr...  6.56 us
    pallas_call x1, Pallas kernels, per_device(): pl.pallas_call(turn_kernel, out_shape=(blocks, blocks), in_specs=[VMEM] *...  3.47 us
    pallas_call x1, Pallas kernels, per_device(): pl.pallas_call(split_kernel, grid=(4,), out_shape=(array((rows, columns),...  3.15 us
    pallas_call x4, Pallas kernels, glue(): pl.pallas_call(kernel, out_shape=tuple((array(shape, F32) for shape in sh...  1.84 us
    pallas_call x1, Pallas kernels, per_device(): copied(partial(candidate_kernel, False), (chunks, chunks), 3 * teams, pai...  1.71 us
    pallas_call x1, Pallas kernels, per_device(): copied(partial(candidate_kernel, True), (chunks, chunks), 3 * teams, pair...  1.71 us
  transfers between devices with their start and end apart: 20, of which 6 were waited for; matrix products, arithmetic and copies ran while one was open for 0% of the time, Pallas kernels for 28%

profile of v4, /device:TPU:0, one launch (start us, length us, event | category | flops | bytes accessed | tf_op | source)
XLA Modules:
  0.0 67.9 jit_solution(6178563334125863221)
XLA Ops:
  0.0 0.5 collective-permute-start.3
  0.5 0.0 copy-start
  0.5 0.7 copy-done
  1.1 0.0 copy-start.1
  1.1 1.7 %shard_map.37 = (f32[4,64,256]{2,1,0:T(8,128)S(1)}, f32[4,64,256]{2,1,0:T(8,128)S(1)}) custom-call(s32[4]{0:T(128)S(1)} %copy-done, f32[4,128,512]{2,1,0:T(8,128)} %rot_ref.3), custom_call_target="tpu_custom_call" | custom-call | tf_op jit(solution)/shard_map/pallas_call | solution.py:271
  2.8 2.6 %collective-permute-start = (f32[4,64,256]{2,1,0:T(8,128)S(1)}, f32[4,64,256]{2,1,0:T(8,128)S(1)}, u32[]{:S(2)}, u32[]{:S(2)}) collective-permute-start(f32[4,64,256]{2,1,0:T(8,128)S(1)} %get-tuple-element.36), channel_id=1, source_target_pairs={{0,4},{4,0},{8,12},{12,8},{16,20},{20,16},{24,28},{28,24},{1,5},{5... | collective-permute-start | bytes 786440 | tf_op jit(solution)/shard_map/ppermute | solution.py:18
  5.4 1.6 %collective-permute-start.1 = (f32[4,64,256]{2,1,0:T(8,128)S(1)}, f32[4,64,256]{2,1,0:T(8,128)S(1)}, u32[]{:S(2)}, u32[]{:S(2)}) collective-permute-start(f32[4,64,256]{2,1,0:T(8,128)S(1)} %get-tuple-element.45), channel_id=1, source_target_pairs={{0,8},{4,12},{8,0},{12,4},{16,24},{20,28},{24,16},{28,20},{1,9},{5... | collective-permute-start | bytes 786440 | tf_op jit(solution)/shard_map/ppermute | solution.py:18
  7.0 1.3 %shard_map.38 = (f32[2,128,256]{2,1,0:T(8,128)S(1)}, f32[128,1536]{1,0:T(8,128)S(1)}) custom-call(f32[4,128,512]{2,1,0:T(8,128)} %rot_ref.3), custom_call_target="tpu_custom_call" | custom-call | tf_op jit(solution)/shard_map/pallas_call | solution.py:274
  8.3 1.6 %collective-permute-start.4 = (f32[2,128,256]{2,1,0:T(8,128)S(1)}, f32[2,128,256]{2,1,0:T(8,128)S(1)}, u32[]{:S(2)}, u32[]{:S(2)}) collective-permute-start(f32[2,128,256]{2,1,0:T(8,128)S(1)} %get-tuple-element.38.own_ref), channel_id=1, source_target_pairs={{0,2},{1,3},{2,0},{3,1},{4,6},{5,7},{6,4},{7,5},{8,10},{9,11},{10,... | collective-permute-start | bytes 786440 | tf_op jit(solution)/shard_map/ppermute | solution.py:18
  9.9 1.7 %shard_map.39 = (f32[4,64,256]{2,1,0:T(8,128)S(1)}, f32[4,64,256]{2,1,0:T(8,128)S(1)}) custom-call(s32[4]{0:T(128)S(1)} %copy-done, f32[4,128,512]{2,1,0:T(8,128)} %rot_ref.3), custom_call_target="tpu_custom_call" | custom-call | tf_op jit(solution)/shard_map/pallas_call | solution.py:275
  11.6 3.2 %shard_map.40 = (bf16[512,2048]{1,0:T(8,128)(2,1)S(1)}, bf16[512,2048]{1,0:T(8,128)(2,1)S(1)}) custom-call(f32[512,2048]{1,0:T(8,128)} %slab_ref), custom_call_target="tpu_custom_call" | custom-call | tf_op jit(solution)/shard_map/pallas_call | solution.py:284
  14.8 0.0 collective-permute-done.a_got
  14.8 0.0 collective-permute-done.1.b_got
  14.8 0.0 copy-done.1
  14.8 0.6 shard_map.41
  15.4 0.7 %collective-permute-start.2 = (f32[4,64,128]{2,1,0:T(8,128)S(1)}, f32[4,64,128]{2,1,0:T(8,128)S(1)}, u32[]{:S(2)}, u32[]{:S(2)}) collective-permute-start(f32[4,64,128]{2,1,0:T(8,128)S(1)} %get-tuple-element.48), channel_id=1, source_target_pairs={{0,8},{4,12},{8,0},{12,4},{16,24},{20,28},{24,16},{28,20},{1,9},{5... | collective-permute-start | bytes 393224 | tf_op jit(solution)/shard_map/ppermute | solution.py:18
  16.1 0.5 collective-permute-start.6
  16.6 0.0 collective-permute-done.4.far_ref
  16.6 0.0 collective-permute-start.5
  16.6 3.9 %collective-permute-done.2.a_got = f32[4,64,128]{2,1,0:T(8,128)S(1)} collective-permute-done((f32[4,64,128]{2,1,0:T(8,128)S(1)}, f32[4,64,128]{2,1,0:T(8,128)S(1)}, u32[]{:S(2)}, u32[]{:S(2)}) %collective-permute-start.2) | collective-permute-done | bytes 131104 | tf_op jit(solution)/shard_map/ppermute | solution.py:18
  20.6 0.5 collective-permute-done.6.b_got
  21.1 1.5 %collective-permute-start.9 = (f32[128,1536]{1,0:T(8,128)S(1)}, f32[128,1536]{1,0:T(8,128)S(1)}, u32[]{:S(2)}, u32[]{:S(2)}) collective-permute-start(f32[128,1536]{1,0:T(8,128)S(1)} %get-tuple-element.57.own_ref), channel_id=1, source_target_pairs={{0,2},{1,3},{2,0},{3,1},{4,6},{5,7},{6,4},{7,5},{8,10},{9,11},{10,... | collective-permute-start | bytes 2359304 | tf_op jit(solution)/shard_map/ppermute | solution.py:18
  22.6 0.0 collective-permute-done.5.far_core_ref
  22.6 0.0 collective-permute-done.3.core0.core1.core_ref
  22.6 1.2 %shard_map.42 = (f32[512,256]{1,0:T(8,128)S(1)}, f32[512,256]{1,0:T(8,128)S(1)}) custom-call(bf16[512,2048]{1,0:T(8,128)(2,1)S(1)} %get-tuple-element.43.shi0.shi1.shi_ref, bf16[512,2048]{1,0:T(8,128)(2,1)S(1)} %get-tuple-element.49.slo0.slo1.slo_ref, bf16[512,2048]{1,0:T(8,128)(2,1)S(1)} %get-tuple-element.43.shi0.shi1.shi_ref, ...), custom_call_target="tpu_custom_call" | custom-call | tf_op jit(solution)/shard_map/pallas_call | solution.py:305
  23.8 0.6 collective-permute-start.10
  24.4 0.6 shard_map.43.kept_ref
  25.0 2.7 %collective-permute-start.7 = (f32[4,128,128]{2,1,0:T(8,128)S(1)}, f32[4,128,128]{2,1,0:T(8,128)S(1)}, u32[]{:S(2)}, u32[]{:S(2)}) collective-permute-start(f32[4,128,128]{2,1,0:T(8,128)S(1)} %shard_map.43.kept_ref), channel_id=1, source_target_pairs={{0,16},{4,20},{8,24},{12,28},{16,0},{20,4},{24,8},{28,12},{1,17},{... | collective-permute-start | bytes 786440 | tf_op jit(solution)/shard_map/ppermute | solution.py:18
  27.6 11.3 %collective-permute-done.9.far_ref = f32[128,1536]{1,0:T(8,128)S(1)} collective-permute-done((f32[128,1536]{1,0:T(8,128)S(1)}, f32[128,1536]{1,0:T(8,128)S(1)}, u32[]{:S(2)}, u32[]{:S(2)}) %collective-permute-start.9) | collective-permute-done | bytes 786464 | tf_op jit(solution)/shard_map/ppermute | solution.py:18
  38.9 0.0 collective-permute-done.7.got_ref
  38.9 0.0 collective-permute-done.10.even_in
  38.9 0.0 collective-permute-start.11
  38.9 0.7 %collective-permute-start.13 = (f32[512,256]{1,0:T(8,128)S(1)}, f32[512,256]{1,0:T(8,128)S(1)}, u32[]{:S(2)}, u32[]{:S(2)}) collective-permute-start(f32[512,256]{1,0:T(8,128)S(1)} %get-tuple-element.63.odd_ref), channel_id=1, source_target_pairs={{4,8},{8,4},{12,16},{16,12},{20,24},{24,20},{5,9},{9,5},{13,17},{1... | collective-permute-start | bytes 1572872 | tf_op jit(solution)/shard_map/ppermute | solution.py:26
  39.6 0.6 shard_map.44
  40.2 1.5 %collective-permute-start.8 = (f32[2,128,128]{2,1,0:T(8,128)S(1)}, f32[2,128,128]{2,1,0:T(8,128)S(1)}, u32[]{:S(2)}, u32[]{:S(2)}) collective-permute-start(f32[2,128,128]{2,1,0:T(8,128)S(1)} %get-tuple-element.55), channel_id=1, source_target_pairs={{0,2},{1,3},{2,0},{3,1},{4,6},{5,7},{6,4},{7,5},{8,10},{9,11},{10,... | collective-permute-start | bytes 393224 | tf_op jit(solution)/shard_map/ppermute | solution.py:18
  41.7 0.0 collective-permute-done.11.far_core_ref
  41.7 3.5 %shard_map.45 = (bf16[512,2048]{1,0:T(8,128)(2,1)S(1)}, bf16[512,2048]{1,0:T(8,128)(2,1)S(1)}) custom-call(bf16[512,2048]{1,0:T(8,128)(2,1)S(1)} %get-tuple-element.43.shi0.shi1.shi_ref, bf16[512,2048]{1,0:T(8,128)(2,1)S(1)} %get-tuple-element.49.slo0.slo1.slo_ref, f32[128,1536]{1,0:T(8,128)S(1)} %get-tuple-element.57.own_ref, ...), custom_call_target="tpu_custom_call" | custom-call | tf_op jit(solution)/shard_map/pallas_call | solution.py:337
  45.2 1.0 %collective-permute-done.8.got_ref = f32[2,128,128]{2,1,0:T(8,128)S(1)} collective-permute-done((f32[2,128,128]{2,1,0:T(8,128)S(1)}, f32[2,128,128]{2,1,0:T(8,128)S(1)}, u32[]{:S(2)}, u32[]{:S(2)}) %collective-permute-start.8) | collective-permute-done | bytes 131104 | tf_op jit(solution)/shard_map/ppermute | solution.py:18
  46.2 0.1 collective-permute-start.15
  46.3 3.0 %collective-permute-start.12 = (f32[2,128,128]{2,1,0:T(8,128)S(1)}, f32[2,128,128]{2,1,0:T(8,128)S(1)}, u32[]{:S(2)}, u32[]{:S(2)}) collective-permute-start(f32[2,128,128]{2,1,0:T(8,128)S(1)} %get-tuple-element.62.refs_0_), channel_id=1, source_target_pairs={{0,8},{4,12},{8,0},{12,4},{16,24},{20,28},{24,16},{28,20},{1,9},{5... | collective-permute-start | bytes 393224 | tf_op jit(solution)/shard_map/ppermute | solution.py:18
  49.3 0.0 collective-permute-done.15.refs_1_
  49.3 2.6 %collective-permute-start.16 = (f32[2,128,128]{2,1,0:T(8,128)S(1)}, f32[2,128,128]{2,1,0:T(8,128)S(1)}, u32[]{:S(2)}, u32[]{:S(2)}) collective-permute-start(f32[2,128,128]{2,1,0:T(8,128)S(1)} %collective-permute-done.15.refs_1_), channel_id=1, source_target_pairs={{0,4},{4,0},{8,12},{12,8},{16,20},{20,16},{24,28},{28,24},{1,5},{5... | collective-permute-start | bytes 393224 | tf_op jit(solution)/shard_map/ppermute | solution.py:18
  51.9 0.0 collective-permute-start.19
  51.9 0.0 collective-permute-done.13.refs_4_.refs_6_
  51.9 6.0 %collective-permute-done.12.refs_0_ = f32[2,128,128]{2,1,0:T(8,128)S(1)} collective-permute-done((f32[2,128,128]{2,1,0:T(8,128)S(1)}, f32[2,128,128]{2,1,0:T(8,128)S(1)}, u32[]{:S(2)}, u32[]{:S(2)}) %collective-permute-start.12) | collective-permute-done | bytes 131104 | tf_op jit(solution)/shard_map/ppermute | solution.py:18
  57.9 0.2 collective-permute-start.18
  58.1 3.0 %collective-permute-start.14 = (f32[2,128,128]{2,1,0:T(8,128)S(1)}, f32[2,128,128]{2,1,0:T(8,128)S(1)}, u32[]{:S(2)}, u32[]{:S(2)}) collective-permute-start(f32[2,128,128]{2,1,0:T(8,128)S(1)} %collective-permute-done.12.refs_0_), channel_id=1, source_target_pairs={{0,4},{4,0},{8,12},{12,8},{16,20},{20,16},{24,28},{28,24},{1,5},{5... | collective-permute-start | bytes 393224 | tf_op jit(solution)/shard_map/ppermute | solution.py:18
  61.0 0.0 collective-permute-done.16.refs_3_
  61.0 0.0 collective-permute-start.17
  61.0 1.9 %shard_map.47.refs_7_ = f32[512,2048]{1,0:T(8,128)} custom-call(f32[2,128,128]{2,1,0:T(8,128)S(1)} %get-tuple-element.62.refs_0_, f32[2,128,128]{2,1,0:T(8,128)S(1)} %collective-permute-done.15.refs_1_, bf16[512,2048]{1,0:T(8,128)(2,1)S(1)} %get-tuple-element.60.refs_2_.refs_4_, bf16[512,2048]{1,0:T(8,128)(2,1)S(1)} %get-tuple-element.66.refs_3_.refs_5_, ...), custom_call_target="tpu_custom_call" | custom-call | tf_op jit(solution)/shard_map/pallas_call | solution.py:359
  62.9 0.0 collective-permute-done.19.refs_2_
  62.9 0.3 collective-permute-done.18.refs_1_
  63.2 2.8 %shard_map.48.refs_5_ = f32[512,2048]{1,0:T(8,128)} custom-call(f32[2,128,128]{2,1,0:T(8,128)S(1)} %collective-permute-done.12.refs_0_, f32[2,128,128]{2,1,0:T(8,128)S(1)} %collective-permute-done.18.refs_1_, f32[2,128,128]{2,1,0:T(8,128)S(1)} %collective-permute-done.19.refs_2_, ...), custom_call_target="tpu_custom_call", output_to_operand_aliasing={{}: (7, {})} | custom-call | tf_op jit(solution)/shard_map/pallas_call | solution.py:359
  66.1 0.0 collective-permute-done.14.refs_0_
  66.1 0.0 collective-permute-done.17.refs_1_
  66.1 1.9 %shard_map.49 = f32[512,2048]{1,0:T(8,128)} custom-call(f32[2,128,128]{2,1,0:T(8,128)S(1)} %collective-permute-done.14.refs_0_, f32[2,128,128]{2,1,0:T(8,128)S(1)} %collective-permute-done.17.refs_1_, bf16[512,2048]{1,0:T(8,128)(2,1)S(1)} %get-tuple-element.60.refs_2_.refs_4_, ...), custom_call_target="tpu_custom_call", output_to_operand_aliasing={{}: (5, {})} | custom-call | tf_op jit(solution)/shard_map/pallas_call | solution.py:359
  (1 shorter events, 0.0 us)
Async XLA Ops:
  0.0 22.6 %collective-permute-start.3 = (f32[4,128,512]{2,1,0:T(8,128)}, f32[4,128,512]{2,1,0:T(8,128)S(1)}, u32[]{:S(2)}, u32[]{:S(2)}) collective-permute-start(f32[4,128,512]{2,1,0:T(8,128)} %rot_ref.3), channel_id=1, source_target_pairs={{0,1},{1,0},{2,3},{3,2},{4,5},{5,4},{6,7},{7,6},{8,9},{9,8},{10,11... | collective-permute-start | bytes 3145736 | tf_op jit(solution)/shard_map/ppermute | solution.py:18
  0.5 0.7 copy-start
  1.1 13.7 %copy-start.1 = (s32[4]{0:T(128)S(1)}, s32[4]{0:T(128)}, u32[]{:S(2)}) copy-start(s32[4]{0:T(128)} %pair_ref.9) | copy-start | bytes 52
  2.8 11.9 %collective-permute-start = (f32[4,64,256]{2,1,0:T(8,128)S(1)}, f32[4,64,256]{2,1,0:T(8,128)S(1)}, u32[]{:S(2)}, u32[]{:S(2)}) collective-permute-start(f32[4,64,256]{2,1,0:T(8,128)S(1)} %get-tuple-element.36), channel_id=1, source_target_pairs={{0,4},{4,0},{8,12},{12,8},{16,20},{20,16},{24,28},{28,24},{1,5},{5... | collective-permute-start | bytes 786440 | tf_op jit(solution)/shard_map/ppermute | solution.py:18
  5.4 9.4 %collective-permute-start.1 = (f32[4,64,256]{2,1,0:T(8,128)S(1)}, f32[4,64,256]{2,1,0:T(8,128)S(1)}, u32[]{:S(2)}, u32[]{:S(2)}) collective-permute-start(f32[4,64,256]{2,1,0:T(8,128)S(1)} %get-tuple-element.45), channel_id=1, source_target_pairs={{0,8},{4,12},{8,0},{12,4},{16,24},{20,28},{24,16},{28,20},{1,9},{5... | collective-permute-start | bytes 786440 | tf_op jit(solution)/shard_map/ppermute | solution.py:18
  8.3 8.3 %collective-permute-start.4 = (f32[2,128,256]{2,1,0:T(8,128)S(1)}, f32[2,128,256]{2,1,0:T(8,128)S(1)}, u32[]{:S(2)}, u32[]{:S(2)}) collective-permute-start(f32[2,128,256]{2,1,0:T(8,128)S(1)} %get-tuple-element.38.own_ref), channel_id=1, source_target_pairs={{0,2},{1,3},{2,0},{3,1},{4,6},{5,7},{6,4},{7,5},{8,10},{9,11},{10,... | collective-permute-start | bytes 786440 | tf_op jit(solution)/shard_map/ppermute | solution.py:18
  15.4 5.1 %collective-permute-start.2 = (f32[4,64,128]{2,1,0:T(8,128)S(1)}, f32[4,64,128]{2,1,0:T(8,128)S(1)}, u32[]{:S(2)}, u32[]{:S(2)}) collective-permute-start(f32[4,64,128]{2,1,0:T(8,128)S(1)} %get-tuple-element.48), channel_id=1, source_target_pairs={{0,8},{4,12},{8,0},{12,4},{16,24},{20,28},{24,16},{28,20},{1,9},{5... | collective-permute-start | bytes 393224 | tf_op jit(solution)/shard_map/ppermute | solution.py:18
  16.1 5.0 %collective-permute-start.6 = (f32[4,64,128]{2,1,0:T(8,128)S(1)}, f32[4,64,128]{2,1,0:T(8,128)S(1)}, u32[]{:S(2)}, u32[]{:S(2)}) collective-permute-start(f32[4,64,128]{2,1,0:T(8,128)S(1)} %get-tuple-element.53), channel_id=1, source_target_pairs={{0,4},{4,0},{8,12},{12,8},{16,20},{20,16},{24,28},{28,24},{1,5},{5... | collective-permute-start | bytes 393224 | tf_op jit(solution)/shard_map/ppermute | solution.py:18
  16.6 6.0 %collective-permute-start.5 = (f32[2,128,256]{2,1,0:T(8,128)S(1)}, f32[2,128,256]{2,1,0:T(8,128)S(1)}, u32[]{:S(2)}, u32[]{:S(2)}) collective-permute-start(f32[2,128,256]{2,1,0:T(8,128)S(1)} %collective-permute-done.4.far_ref), channel_id=1, source_target_pairs={{0,1},{1,0},{2,3},{3,2},{4,5},{5,4},{6,7},{7,6},{8,9},{9,8},{10,11... | collective-permute-start | bytes 786440 | tf_op jit(solution)/shard_map/ppermute | solution.py:18
  21.1 17.8 %collective-permute-start.9 = (f32[128,1536]{1,0:T(8,128)S(1)}, f32[128,1536]{1,0:T(8,128)S(1)}, u32[]{:S(2)}, u32[]{:S(2)}) collective-permute-start(f32[128,1536]{1,0:T(8,128)S(1)} %get-tuple-element.57.own_ref), channel_id=1, source_target_pairs={{0,2},{1,3},{2,0},{3,1},{4,6},{5,7},{6,4},{7,5},{8,10},{9,11},{10,... | collective-permute-start | bytes 2359304 | tf_op jit(solution)/shard_map/ppermute | solution.py:18
  23.8 15.1 %collective-permute-start.10 = (f32[512,256]{1,0:T(8,128)S(1)}, f32[512,256]{1,0:T(8,128)S(1)}, u32[]{:S(2)}, u32[]{:S(2)}) collective-permute-start(f32[512,256]{1,0:T(8,128)S(1)} %get-tuple-element.51.even_ref), channel_id=1, source_target_pairs={{0,4},{4,0},{8,12},{12,8},{16,20},{20,16},{24,28},{28,24},{1,5},{5... | collective-permute-start | bytes 1572872 | tf_op jit(solution)/shard_map/ppermute | solution.py:26
  25.0 14.0 %collective-permute-start.7 = (f32[4,128,128]{2,1,0:T(8,128)S(1)}, f32[4,128,128]{2,1,0:T(8,128)S(1)}, u32[]{:S(2)}, u32[]{:S(2)}) collective-permute-start(f32[4,128,128]{2,1,0:T(8,128)S(1)} %shard_map.43.kept_ref), channel_id=1, source_target_pairs={{0,16},{4,20},{8,24},{12,28},{16,0},{20,4},{24,8},{28,12},{1,17},{... | collective-permute-start | bytes 786440 | tf_op jit(solution)/shard_map/ppermute | solution.py:18
  38.9 2.8 %collective-permute-start.11 = (f32[128,1536]{1,0:T(8,128)S(1)}, f32[128,1536]{1,0:T(8,128)S(1)}, u32[]{:S(2)}, u32[]{:S(2)}) collective-permute-start(f32[128,1536]{1,0:T(8,128)S(1)} %collective-permute-done.9.far_ref), channel_id=1, source_target_pairs={{0,1},{1,0},{2,3},{3,2},{4,5},{5,4},{6,7},{7,6},{8,9},{9,8},{10,11... | collective-permute-start | bytes 2359304 | tf_op jit(solution)/shard_map/ppermute | solution.py:18
  38.9 13.0 %collective-permute-start.13 = (f32[512,256]{1,0:T(8,128)S(1)}, f32[512,256]{1,0:T(8,128)S(1)}, u32[]{:S(2)}, u32[]{:S(2)}) collective-permute-start(f32[512,256]{1,0:T(8,128)S(1)} %get-tuple-element.63.odd_ref), channel_id=1, source_target_pairs={{4,8},{8,4},{12,16},{16,12},{20,24},{24,20},{5,9},{9,5},{13,17},{1... | collective-permute-start | bytes 1572872 | tf_op jit(solution)/shard_map/ppermute | solution.py:26
  40.2 6.0 %collective-permute-start.8 = (f32[2,128,128]{2,1,0:T(8,128)S(1)}, f32[2,128,128]{2,1,0:T(8,128)S(1)}, u32[]{:S(2)}, u32[]{:S(2)}) collective-permute-start(f32[2,128,128]{2,1,0:T(8,128)S(1)} %get-tuple-element.55), channel_id=1, source_target_pairs={{0,2},{1,3},{2,0},{3,1},{4,6},{5,7},{6,4},{7,5},{8,10},{9,11},{10,... | collective-permute-start | bytes 393224 | tf_op jit(solution)/shard_map/ppermute | solution.py:18
  46.2 3.1 %collective-permute-start.15 = (f32[2,128,128]{2,1,0:T(8,128)S(1)}, f32[2,128,128]{2,1,0:T(8,128)S(1)}, u32[]{:S(2)}, u32[]{:S(2)}) collective-permute-start(f32[2,128,128]{2,1,0:T(8,128)S(1)} %get-tuple-element.65), channel_id=1, source_target_pairs={{0,1},{1,0},{2,3},{3,2},{4,5},{5,4},{6,7},{7,6},{8,9},{9,8},{10,11... | collective-permute-start | bytes 393224 | tf_op jit(solution)/shard_map/ppermute | solution.py:18
  46.3 11.6 %collective-permute-start.12 = (f32[2,128,128]{2,1,0:T(8,128)S(1)}, f32[2,128,128]{2,1,0:T(8,128)S(1)}, u32[]{:S(2)}, u32[]{:S(2)}) collective-permute-start(f32[2,128,128]{2,1,0:T(8,128)S(1)} %get-tuple-element.62.refs_0_), channel_id=1, source_target_pairs={{0,8},{4,12},{8,0},{12,4},{16,24},{20,28},{24,16},{28,20},{1,9},{5... | collective-permute-start | bytes 393224 | tf_op jit(solution)/shard_map/ppermute | solution.py:18
  49.3 11.8 %collective-permute-start.16 = (f32[2,128,128]{2,1,0:T(8,128)S(1)}, f32[2,128,128]{2,1,0:T(8,128)S(1)}, u32[]{:S(2)}, u32[]{:S(2)}) collective-permute-start(f32[2,128,128]{2,1,0:T(8,128)S(1)} %collective-permute-done.15.refs_1_), channel_id=1, source_target_pairs={{0,4},{4,0},{8,12},{12,8},{16,20},{20,16},{24,28},{28,24},{1,5},{5... | collective-permute-start | bytes 393224 | tf_op jit(solution)/shard_map/ppermute | solution.py:18
  51.9 11.0 %collective-permute-start.19 = (f32[2,128,128]{2,1,0:T(8,128)S(1)}, f32[2,128,128]{2,1,0:T(8,128)S(1)}, u32[]{:S(2)}, u32[]{:S(2)}) collective-permute-start(f32[2,128,128]{2,1,0:T(8,128)S(1)} %get-tuple-element.62.refs_0_), channel_id=1, source_target_pairs={{0,4},{4,0},{8,12},{12,8},{16,20},{20,16},{24,28},{28,24},{1,5},{5... | collective-permute-start | bytes 393224 | tf_op jit(solution)/shard_map/ppermute | solution.py:18
  57.9 5.3 %collective-permute-start.18 = (f32[2,128,128]{2,1,0:T(8,128)S(1)}, f32[2,128,128]{2,1,0:T(8,128)S(1)}, u32[]{:S(2)}, u32[]{:S(2)}) collective-permute-start(f32[2,128,128]{2,1,0:T(8,128)S(1)} %collective-permute-done.15.refs_1_), channel_id=1, source_target_pairs={{0,8},{4,12},{8,0},{12,4},{16,24},{20,28},{24,16},{28,20},{1,9},{5... | collective-permute-start | bytes 393224 | tf_op jit(solution)/shard_map/ppermute | solution.py:18
  58.1 8.0 %collective-permute-start.14 = (f32[2,128,128]{2,1,0:T(8,128)S(1)}, f32[2,128,128]{2,1,0:T(8,128)S(1)}, u32[]{:S(2)}, u32[]{:S(2)}) collective-permute-start(f32[2,128,128]{2,1,0:T(8,128)S(1)} %collective-permute-done.12.refs_0_), channel_id=1, source_target_pairs={{0,4},{4,0},{8,12},{12,8},{16,20},{20,16},{24,28},{28,24},{1,5},{5... | collective-permute-start | bytes 393224 | tf_op jit(solution)/shard_map/ppermute | solution.py:18
  61.0 5.0 %collective-permute-start.17 = (f32[2,128,128]{2,1,0:T(8,128)S(1)}, f32[2,128,128]{2,1,0:T(8,128)S(1)}, u32[]{:S(2)}, u32[]{:S(2)}) collective-permute-start(f32[2,128,128]{2,1,0:T(8,128)S(1)} %collective-permute-done.16.refs_3_), channel_id=1, source_target_pairs={{0,8},{4,12},{8,0},{12,4},{16,24},{20,28},{24,16},{28,20},{1,9},{5... | collective-permute-start | bytes 393224 | tf_op jit(solution)/shard_map/ppermute | solution.py:18

commit v5 on v4

--- a/solution.py
+++ b/solution.py
@@ -349,7 +349,7 @@
     give, held = glue(cross_kernel, (pieces, pieces), held, after(flip(give, "row", 2), turned_hi))
     more = flip(give, "row", 1)
 
-    near = after(flip(held, "loop", 2), odd_in), flip(more, "loop", 2)
+    near = flip(held, "loop", 2), after(flip(more, "loop", 2), odd_in)
     side = flip(held, "loop", 1), flip(more, "loop", 1)
     across = flip(near[0], "loop", 1), flip(side[1], "loop", 2)
 

time: 68.3 us -> 69.7 us (1.020)
  waiting for transfers between devices: 23 us -> 24.1 us
    ppermute x18, waiting for transfers between devices: 23 us -> 24.1 us  [flip(): return lax.ppermute(x, axis, [(i, i ^ bit) for i in range(n)])]
  transfers between devices with their start and end apart: 20 -> 20, of which waited for: 6 -> 5; matrix products, arithmetic and copies ran while one was open for 0% -> 0% of each run, Pallas kernels for 28% -> 28%
where the time goes in v5:
time: 69.7 us; the launch traced here: 69.3 us
  waiting for transfers between devices  24.1 us (35%)
  starting transfers between devices  23.3 us (33%)
  Pallas kernels  21 us (30%)
    ppermute x18, waiting for transfers between devices, flip(): return lax.ppermute(x, axis, [(i, i ^ bit) for i in range(n)])  24.1 us
    ppermute x18, starting transfers between devices, flip(): return lax.ppermute(x, axis, [(i, i ^ bit) for i in range(n)])  22.1 us
    pallas_call x3, Pallas kernels, left(): pl.pallas_call(partial(left_kernel, offsets, int(aliased)), out_shape=arr...  6.56 us
    pallas_call x1, Pallas kernels, per_device(): pl.pallas_call(turn_kernel, out_shape=(blocks, blocks), in_specs=[VMEM] *...  3.48 us
    pallas_call x1, Pallas kernels, per_device(): pl.pallas_call(split_kernel, grid=(4,), out_shape=(array((rows, columns),...  3.15 us
    pallas_call x4, Pallas kernels, glue(): pl.pallas_call(kernel, out_shape=tuple((array(shape, F32) for shape in sh...  1.84 us
    pallas_call x1, Pallas kernels, per_device(): copied(partial(candidate_kernel, False), (chunks, chunks), 3 * teams, pai...  1.71 us
    pallas_call x1, Pallas kernels, per_device(): copied(partial(candidate_kernel, True), (chunks, chunks), 3 * teams, pair...  1.71 us
  transfers between devices with their start and end apart: 20, of which 5 were waited for; matrix products, arithmetic and copies ran while one was open for 0% of the time, Pallas kernels for 28%

profile of v5, /device:TPU:0, one launch (start us, length us, event | category | flops | bytes accessed | tf_op | source)
XLA Modules:
  0.0 69.3 jit_solution(2145696099752447976)
XLA Ops:
  0.0 0.5 collective-permute-start.3
  0.5 0.0 copy-start
  0.5 0.7 copy-done
  1.1 0.0 copy-start.1
  1.1 1.7 %shard_map.37 = (f32[4,64,256]{2,1,0:T(8,128)S(1)}, f32[4,64,256]{2,1,0:T(8,128)S(1)}) custom-call(s32[4]{0:T(128)S(1)} %copy-done, f32[4,128,512]{2,1,0:T(8,128)} %rot_ref.3), custom_call_target="tpu_custom_call" | custom-call | tf_op jit(solution)/shard_map/pallas_call | solution.py:271
  2.8 2.6 %collective-permute-start = (f32[4,64,256]{2,1,0:T(8,128)S(1)}, f32[4,64,256]{2,1,0:T(8,128)S(1)}, u32[]{:S(2)}, u32[]{:S(2)}) collective-permute-start(f32[4,64,256]{2,1,0:T(8,128)S(1)} %get-tuple-element.36), channel_id=1, source_target_pairs={{0,4},{4,0},{8,12},{12,8},{16,20},{20,16},{24,28},{28,24},{1,5},{5... | collective-permute-start | bytes 786440 | tf_op jit(solution)/shard_map/ppermute | solution.py:18
  5.4 1.6 %collective-permute-start.1 = (f32[4,64,256]{2,1,0:T(8,128)S(1)}, f32[4,64,256]{2,1,0:T(8,128)S(1)}, u32[]{:S(2)}, u32[]{:S(2)}) collective-permute-start(f32[4,64,256]{2,1,0:T(8,128)S(1)} %get-tuple-element.45), channel_id=1, source_target_pairs={{0,8},{4,12},{8,0},{12,4},{16,24},{20,28},{24,16},{28,20},{1,9},{5... | collective-permute-start | bytes 786440 | tf_op jit(solution)/shard_map/ppermute | solution.py:18
  7.0 1.3 %shard_map.38 = (f32[2,128,256]{2,1,0:T(8,128)S(1)}, f32[128,1536]{1,0:T(8,128)S(1)}) custom-call(f32[4,128,512]{2,1,0:T(8,128)} %rot_ref.3), custom_call_target="tpu_custom_call" | custom-call | tf_op jit(solution)/shard_map/pallas_call | solution.py:274
  8.3 1.6 %collective-permute-start.4 = (f32[2,128,256]{2,1,0:T(8,128)S(1)}, f32[2,128,256]{2,1,0:T(8,128)S(1)}, u32[]{:S(2)}, u32[]{:S(2)}) collective-permute-start(f32[2,128,256]{2,1,0:T(8,128)S(1)} %get-tuple-element.38.own_ref), channel_id=1, source_target_pairs={{0,2},{1,3},{2,0},{3,1},{4,6},{5,7},{6,4},{7,5},{8,10},{9,11},{10,... | collective-permute-start | bytes 786440 | tf_op jit(solution)/shard_map/ppermute | solution.py:18
  9.9 1.7 %shard_map.39 = (f32[4,64,256]{2,1,0:T(8,128)S(1)}, f32[4,64,256]{2,1,0:T(8,128)S(1)}) custom-call(s32[4]{0:T(128)S(1)} %copy-done, f32[4,128,512]{2,1,0:T(8,128)} %rot_ref.3), custom_call_target="tpu_custom_call" | custom-call | tf_op jit(solution)/shard_map/pallas_call | solution.py:275
  11.6 3.2 %shard_map.40 = (bf16[512,2048]{1,0:T(8,128)(2,1)S(1)}, bf16[512,2048]{1,0:T(8,128)(2,1)S(1)}) custom-call(f32[512,2048]{1,0:T(8,128)} %slab_ref), custom_call_target="tpu_custom_call" | custom-call | tf_op jit(solution)/shard_map/pallas_call | solution.py:284
  14.8 0.0 collective-permute-done.a_got
  14.8 0.0 collective-permute-done.1.b_got
  14.8 0.0 copy-done.1
  14.8 0.6 shard_map.41
  15.4 0.7 collective-permute-start.2
  16.1 0.5 collective-permute-start.6
  16.6 0.0 collective-permute-done.4.far_ref
  16.6 0.0 collective-permute-start.5
  16.6 3.9 %collective-permute-done.2.a_got = f32[4,64,128]{2,1,0:T(8,128)S(1)} collective-permute-done((f32[4,64,128]{2,1,0:T(8,128)S(1)}, f32[4,64,128]{2,1,0:T(8,128)S(1)}, u32[]{:S(2)}, u32[]{:S(2)}) %collective-permute-start.2) | collective-permute-done | bytes 131104 | tf_op jit(solution)/shard_map/ppermute | solution.py:18
  20.6 0.5 collective-permute-done.6.b_got
  21.1 1.5 %collective-permute-start.9 = (f32[128,1536]{1,0:T(8,128)S(1)}, f32[128,1536]{1,0:T(8,128)S(1)}, u32[]{:S(2)}, u32[]{:S(2)}) collective-permute-start(f32[128,1536]{1,0:T(8,128)S(1)} %get-tuple-element.57.own_ref), channel_id=1, source_target_pairs={{0,2},{1,3},{2,0},{3,1},{4,6},{5,7},{6,4},{7,5},{8,10},{9,11},{10,... | collective-permute-start | bytes 2359304 | tf_op jit(solution)/shard_map/ppermute | solution.py:18
  22.6 0.0 collective-permute-done.5.far_core_ref
  22.6 0.0 collective-permute-done.3.core0.core1.core_ref
  22.6 1.2 %shard_map.42 = (f32[512,256]{1,0:T(8,128)S(1)}, f32[512,256]{1,0:T(8,128)S(1)}) custom-call(bf16[512,2048]{1,0:T(8,128)(2,1)S(1)} %get-tuple-element.43.shi0.shi1.shi_ref, bf16[512,2048]{1,0:T(8,128)(2,1)S(1)} %get-tuple-element.49.slo0.slo1.slo_ref, bf16[512,2048]{1,0:T(8,128)(2,1)S(1)} %get-tuple-element.43.shi0.shi1.shi_ref, ...), custom_call_target="tpu_custom_call" | custom-call | tf_op jit(solution)/shard_map/pallas_call | solution.py:305
  23.8 0.6 collective-permute-start.10
  24.4 0.6 shard_map.43.kept_ref
  25.0 2.7 %collective-permute-start.7 = (f32[4,128,128]{2,1,0:T(8,128)S(1)}, f32[4,128,128]{2,1,0:T(8,128)S(1)}, u32[]{:S(2)}, u32[]{:S(2)}) collective-permute-start(f32[4,128,128]{2,1,0:T(8,128)S(1)} %shard_map.43.kept_ref), channel_id=1, source_target_pairs={{0,16},{4,20},{8,24},{12,28},{16,0},{20,4},{24,8},{28,12},{1,17},{... | collective-permute-start | bytes 786440 | tf_op jit(solution)/shard_map/ppermute | solution.py:18
  27.6 11.3 %collective-permute-done.9.far_ref = f32[128,1536]{1,0:T(8,128)S(1)} collective-permute-done((f32[128,1536]{1,0:T(8,128)S(1)}, f32[128,1536]{1,0:T(8,128)S(1)}, u32[]{:S(2)}, u32[]{:S(2)}) %collective-permute-start.9) | collective-permute-done | bytes 786464 | tf_op jit(solution)/shard_map/ppermute | solution.py:18
  38.9 0.0 collective-permute-done.7.got_ref
  38.9 0.0 collective-permute-done.10.even_in
  38.9 0.0 collective-permute-start.11
  38.9 0.6 shard_map.44
  39.5 1.5 %collective-permute-start.8 = (f32[2,128,128]{2,1,0:T(8,128)S(1)}, f32[2,128,128]{2,1,0:T(8,128)S(1)}, u32[]{:S(2)}, u32[]{:S(2)}) collective-permute-start(f32[2,128,128]{2,1,0:T(8,128)S(1)} %get-tuple-element.55), channel_id=1, source_target_pairs={{0,2},{1,3},{2,0},{3,1},{4,6},{5,7},{6,4},{7,5},{8,10},{9,11},{10,... | collective-permute-start | bytes 393224 | tf_op jit(solution)/shard_map/ppermute | solution.py:18
  41.0 0.7 collective-permute-start.17
  41.7 0.0 collective-permute-done.11.far_core_ref
  41.7 3.5 %shard_map.45 = (bf16[512,2048]{1,0:T(8,128)(2,1)S(1)}, bf16[512,2048]{1,0:T(8,128)(2,1)S(1)}) custom-call(bf16[512,2048]{1,0:T(8,128)(2,1)S(1)} %get-tuple-element.43.shi0.shi1.shi_ref, bf16[512,2048]{1,0:T(8,128)(2,1)S(1)} %get-tuple-element.49.slo0.slo1.slo_ref, f32[128,1536]{1,0:T(8,128)S(1)} %get-tuple-element.57.own_ref, ...), custom_call_target="tpu_custom_call" | custom-call | tf_op jit(solution)/shard_map/pallas_call | solution.py:337
  45.2 0.3 collective-permute-done.8.got_ref
  45.5 0.1 collective-permute-start.14
  45.6 3.1 %collective-permute-start.12 = (f32[2,128,128]{2,1,0:T(8,128)S(1)}, f32[2,128,128]{2,1,0:T(8,128)S(1)}, u32[]{:S(2)}, u32[]{:S(2)}) collective-permute-start(f32[2,128,128]{2,1,0:T(8,128)S(1)} %get-tuple-element.62.refs_0_), channel_id=1, source_target_pairs={{0,8},{4,12},{8,0},{12,4},{16,24},{20,28},{24,16},{28,20},{1,9},{5... | collective-permute-start | bytes 393224 | tf_op jit(solution)/shard_map/ppermute | solution.py:18
  48.7 0.0 collective-permute-done.14.refs_1_
  48.7 2.6 %collective-permute-start.15 = (f32[2,128,128]{2,1,0:T(8,128)S(1)}, f32[2,128,128]{2,1,0:T(8,128)S(1)}, u32[]{:S(2)}, u32[]{:S(2)}) collective-permute-start(f32[2,128,128]{2,1,0:T(8,128)S(1)} %collective-permute-done.14.refs_1_), channel_id=1, source_target_pairs={{0,4},{4,0},{8,12},{12,8},{16,20},{20,16},{24,28},{28,24},{1,5},{5... | collective-permute-start | bytes 393224 | tf_op jit(solution)/shard_map/ppermute | solution.py:18
  51.2 1.3 %collective-permute-start.18 = (f32[2,128,128]{2,1,0:T(8,128)S(1)}, f32[2,128,128]{2,1,0:T(8,128)S(1)}, u32[]{:S(2)}, u32[]{:S(2)}) collective-permute-start(f32[2,128,128]{2,1,0:T(8,128)S(1)} %collective-permute-done.14.refs_1_), channel_id=1, source_target_pairs={{0,8},{4,12},{8,0},{12,4},{16,24},{20,28},{24,16},{28,20},{1,9},{5... | collective-permute-start | bytes 393224 | tf_op jit(solution)/shard_map/ppermute | solution.py:18
  52.5 0.0 collective-permute-start.19
  52.5 8.0 %collective-permute-done.12.refs_0_ = f32[2,128,128]{2,1,0:T(8,128)S(1)} collective-permute-done((f32[2,128,128]{2,1,0:T(8,128)S(1)}, f32[2,128,128]{2,1,0:T(8,128)S(1)}, u32[]{:S(2)}, u32[]{:S(2)}) %collective-permute-start.12) | collective-permute-done | bytes 131104 | tf_op jit(solution)/shard_map/ppermute | solution.py:18
  60.5 0.0 collective-permute-start.13
  60.5 0.0 collective-permute-done.15.refs_3_
  60.5 2.1 %collective-permute-start.16 = (f32[2,128,128]{2,1,0:T(8,128)S(1)}, f32[2,128,128]{2,1,0:T(8,128)S(1)}, u32[]{:S(2)}, u32[]{:S(2)}) collective-permute-start(f32[2,128,128]{2,1,0:T(8,128)S(1)} %collective-permute-done.15.refs_3_), channel_id=1, source_target_pairs={{0,8},{4,12},{8,0},{12,4},{16,24},{20,28},{24,16},{28,20},{1,9},{5... | collective-permute-start | bytes 393224 | tf_op jit(solution)/shard_map/ppermute | solution.py:18
  62.7 0.0 collective-permute-done.17.refs_4_.refs_6_
  62.7 1.8 %shard_map.47.refs_7_ = f32[512,2048]{1,0:T(8,128)} custom-call(f32[2,128,128]{2,1,0:T(8,128)S(1)} %get-tuple-element.62.refs_0_, f32[2,128,128]{2,1,0:T(8,128)S(1)} %collective-permute-done.14.refs_1_, bf16[512,2048]{1,0:T(8,128)(2,1)S(1)} %get-tuple-element.60.refs_2_.refs_4_, bf16[512,2048]{1,0:T(8,128)(2,1)S(1)} %get-tuple-element.64.refs_3_.refs_5_, ...), custom_call_target="tpu_custom_call" | custom-call | tf_op jit(solution)/shard_map/pallas_call | solution.py:359
  64.5 0.0 collective-permute-done.18.refs_1_
  64.5 0.0 collective-permute-done.19.refs_2_
  64.5 2.9 %shard_map.48.refs_5_ = f32[512,2048]{1,0:T(8,128)} custom-call(f32[2,128,128]{2,1,0:T(8,128)S(1)} %collective-permute-done.12.refs_0_, f32[2,128,128]{2,1,0:T(8,128)S(1)} %collective-permute-done.18.refs_1_, f32[2,128,128]{2,1,0:T(8,128)S(1)} %collective-permute-done.19.refs_2_, ...), custom_call_target="tpu_custom_call", output_to_operand_aliasing={{}: (7, {})} | custom-call | tf_op jit(solution)/shard_map/pallas_call | solution.py:359
  67.4 0.0 collective-permute-done.13.refs_0_
  67.4 0.0 collective-permute-done.16.refs_1_
  67.4 1.9 %shard_map.49 = f32[512,2048]{1,0:T(8,128)} custom-call(f32[2,128,128]{2,1,0:T(8,128)S(1)} %collective-permute-done.13.refs_0_, f32[2,128,128]{2,1,0:T(8,128)S(1)} %collective-permute-done.16.refs_1_, bf16[512,2048]{1,0:T(8,128)(2,1)S(1)} %get-tuple-element.60.refs_2_.refs_4_, ...), custom_call_target="tpu_custom_call", output_to_operand_aliasing={{}: (5, {})} | custom-call | tf_op jit(solution)/shard_map/pallas_call | solution.py:359
  (1 shorter events, 0.0 us)
Async XLA Ops:
  0.0 22.6 %collective-permute-start.3 = (f32[4,128,512]{2,1,0:T(8,128)}, f32[4,128,512]{2,1,0:T(8,128)S(1)}, u32[]{:S(2)}, u32[]{:S(2)}) collective-permute-start(f32[4,128,512]{2,1,0:T(8,128)} %rot_ref.3), channel_id=1, source_target_pairs={{0,1},{1,0},{2,3},{3,2},{4,5},{5,4},{6,7},{7,6},{8,9},{9,8},{10,11... | collective-permute-start | bytes 3145736 | tf_op jit(solution)/shard_map/ppermute | solution.py:18
  0.5 0.7 copy-start
  1.1 13.7 %copy-start.1 = (s32[4]{0:T(128)S(1)}, s32[4]{0:T(128)}, u32[]{:S(2)}) copy-start(s32[4]{0:T(128)} %pair_ref.9) | copy-start | bytes 52
  2.8 11.9 %collective-permute-start = (f32[4,64,256]{2,1,0:T(8,128)S(1)}, f32[4,64,256]{2,1,0:T(8,128)S(1)}, u32[]{:S(2)}, u32[]{:S(2)}) collective-permute-start(f32[4,64,256]{2,1,0:T(8,128)S(1)} %get-tuple-element.36), channel_id=1, source_target_pairs={{0,4},{4,0},{8,12},{12,8},{16,20},{20,16},{24,28},{28,24},{1,5},{5... | collective-permute-start | bytes 786440 | tf_op jit(solution)/shard_map/ppermute | solution.py:18
  5.4 9.4 %collective-permute-start.1 = (f32[4,64,256]{2,1,0:T(8,128)S(1)}, f32[4,64,256]{2,1,0:T(8,128)S(1)}, u32[]{:S(2)}, u32[]{:S(2)}) collective-permute-start(f32[4,64,256]{2,1,0:T(8,128)S(1)} %get-tuple-element.45), channel_id=1, source_target_pairs={{0,8},{4,12},{8,0},{12,4},{16,24},{20,28},{24,16},{28,20},{1,9},{5... | collective-permute-start | bytes 786440 | tf_op jit(solution)/shard_map/ppermute | solution.py:18
  8.3 8.3 %collective-permute-start.4 = (f32[2,128,256]{2,1,0:T(8,128)S(1)}, f32[2,128,256]{2,1,0:T(8,128)S(1)}, u32[]{:S(2)}, u32[]{:S(2)}) collective-permute-start(f32[2,128,256]{2,1,0:T(8,128)S(1)} %get-tuple-element.38.own_ref), channel_id=1, source_target_pairs={{0,2},{1,3},{2,0},{3,1},{4,6},{5,7},{6,4},{7,5},{8,10},{9,11},{10,... | collective-permute-start | bytes 786440 | tf_op jit(solution)/shard_map/ppermute | solution.py:18
  15.4 5.1 %collective-permute-start.2 = (f32[4,64,128]{2,1,0:T(8,128)S(1)}, f32[4,64,128]{2,1,0:T(8,128)S(1)}, u32[]{:S(2)}, u32[]{:S(2)}) collective-permute-start(f32[4,64,128]{2,1,0:T(8,128)S(1)} %get-tuple-element.48), channel_id=1, source_target_pairs={{0,8},{4,12},{8,0},{12,4},{16,24},{20,28},{24,16},{28,20},{1,9},{5... | collective-permute-start | bytes 393224 | tf_op jit(solution)/shard_map/ppermute | solution.py:18
  16.1 5.0 %collective-permute-start.6 = (f32[4,64,128]{2,1,0:T(8,128)S(1)}, f32[4,64,128]{2,1,0:T(8,128)S(1)}, u32[]{:S(2)}, u32[]{:S(2)}) collective-permute-start(f32[4,64,128]{2,1,0:T(8,128)S(1)} %get-tuple-element.53), channel_id=1, source_target_pairs={{0,4},{4,0},{8,12},{12,8},{16,20},{20,16},{24,28},{28,24},{1,5},{5... | collective-permute-start | bytes 393224 | tf_op jit(solution)/shard_map/ppermute | solution.py:18
  16.6 6.0 %collective-permute-start.5 = (f32[2,128,256]{2,1,0:T(8,128)S(1)}, f32[2,128,256]{2,1,0:T(8,128)S(1)}, u32[]{:S(2)}, u32[]{:S(2)}) collective-permute-start(f32[2,128,256]{2,1,0:T(8,128)S(1)} %collective-permute-done.4.far_ref), channel_id=1, source_target_pairs={{0,1},{1,0},{2,3},{3,2},{4,5},{5,4},{6,7},{7,6},{8,9},{9,8},{10,11... | collective-permute-start | bytes 786440 | tf_op jit(solution)/shard_map/ppermute | solution.py:18
  21.1 17.8 %collective-permute-start.9 = (f32[128,1536]{1,0:T(8,128)S(1)}, f32[128,1536]{1,0:T(8,128)S(1)}, u32[]{:S(2)}, u32[]{:S(2)}) collective-permute-start(f32[128,1536]{1,0:T(8,128)S(1)} %get-tuple-element.57.own_ref), channel_id=1, source_target_pairs={{0,2},{1,3},{2,0},{3,1},{4,6},{5,7},{6,4},{7,5},{8,10},{9,11},{10,... | collective-permute-start | bytes 2359304 | tf_op jit(solution)/shard_map/ppermute | solution.py:18
  23.8 15.1 %collective-permute-start.10 = (f32[512,256]{1,0:T(8,128)S(1)}, f32[512,256]{1,0:T(8,128)S(1)}, u32[]{:S(2)}, u32[]{:S(2)}) collective-permute-start(f32[512,256]{1,0:T(8,128)S(1)} %get-tuple-element.51.even_ref), channel_id=1, source_target_pairs={{0,4},{4,0},{8,12},{12,8},{16,20},{20,16},{24,28},{28,24},{1,5},{5... | collective-permute-start | bytes 1572872 | tf_op jit(solution)/shard_map/ppermute | solution.py:26
  25.0 14.0 %collective-permute-start.7 = (f32[4,128,128]{2,1,0:T(8,128)S(1)}, f32[4,128,128]{2,1,0:T(8,128)S(1)}, u32[]{:S(2)}, u32[]{:S(2)}) collective-permute-start(f32[4,128,128]{2,1,0:T(8,128)S(1)} %shard_map.43.kept_ref), channel_id=1, source_target_pairs={{0,16},{4,20},{8,24},{12,28},{16,0},{20,4},{24,8},{28,12},{1,17},{... | collective-permute-start | bytes 786440 | tf_op jit(solution)/shard_map/ppermute | solution.py:18
  38.9 2.8 %collective-permute-start.11 = (f32[128,1536]{1,0:T(8,128)S(1)}, f32[128,1536]{1,0:T(8,128)S(1)}, u32[]{:S(2)}, u32[]{:S(2)}) collective-permute-start(f32[128,1536]{1,0:T(8,128)S(1)} %collective-permute-done.9.far_ref), channel_id=1, source_target_pairs={{0,1},{1,0},{2,3},{3,2},{4,5},{5,4},{6,7},{7,6},{8,9},{9,8},{10,11... | collective-permute-start | bytes 2359304 | tf_op jit(solution)/shard_map/ppermute | solution.py:18
  39.5 6.0 %collective-permute-start.8 = (f32[2,128,128]{2,1,0:T(8,128)S(1)}, f32[2,128,128]{2,1,0:T(8,128)S(1)}, u32[]{:S(2)}, u32[]{:S(2)}) collective-permute-start(f32[2,128,128]{2,1,0:T(8,128)S(1)} %get-tuple-element.55), channel_id=1, source_target_pairs={{0,2},{1,3},{2,0},{3,1},{4,6},{5,7},{6,4},{7,5},{8,10},{9,11},{10,... | collective-permute-start | bytes 393224 | tf_op jit(solution)/shard_map/ppermute | solution.py:18
  41.0 21.7 %collective-permute-start.17 = (f32[512,256]{1,0:T(8,128)S(1)}, f32[512,256]{1,0:T(8,128)S(1)}, u32[]{:S(2)}, u32[]{:S(2)}) collective-permute-start(f32[512,256]{1,0:T(8,128)S(1)} %get-tuple-element.65.odd_ref), channel_id=1, source_target_pairs={{4,8},{8,4},{12,16},{16,12},{20,24},{24,20},{5,9},{9,5},{13,17},{1... | collective-permute-start | bytes 1572872 | tf_op jit(solution)/shard_map/ppermute | solution.py:26
  45.5 3.1 %collective-permute-start.14 = (f32[2,128,128]{2,1,0:T(8,128)S(1)}, f32[2,128,128]{2,1,0:T(8,128)S(1)}, u32[]{:S(2)}, u32[]{:S(2)}) collective-permute-start(f32[2,128,128]{2,1,0:T(8,128)S(1)} %get-tuple-element.63), channel_id=1, source_target_pairs={{0,1},{1,0},{2,3},{3,2},{4,5},{5,4},{6,7},{7,6},{8,9},{9,8},{10,11... | collective-permute-start | bytes 393224 | tf_op jit(solution)/shard_map/ppermute | solution.py:18
  45.6 14.9 %collective-permute-start.12 = (f32[2,128,128]{2,1,0:T(8,128)S(1)}, f32[2,128,128]{2,1,0:T(8,128)S(1)}, u32[]{:S(2)}, u32[]{:S(2)}) collective-permute-start(f32[2,128,128]{2,1,0:T(8,128)S(1)} %get-tuple-element.62.refs_0_), channel_id=1, source_target_pairs={{0,8},{4,12},{8,0},{12,4},{16,24},{20,28},{24,16},{28,20},{1,9},{5... | collective-permute-start | bytes 393224 | tf_op jit(solution)/shard_map/ppermute | solution.py:18
  48.7 11.9 %collective-permute-start.15 = (f32[2,128,128]{2,1,0:T(8,128)S(1)}, f32[2,128,128]{2,1,0:T(8,128)S(1)}, u32[]{:S(2)}, u32[]{:S(2)}) collective-permute-start(f32[2,128,128]{2,1,0:T(8,128)S(1)} %collective-permute-done.14.refs_1_), channel_id=1, source_target_pairs={{0,4},{4,0},{8,12},{12,8},{16,20},{20,16},{24,28},{28,24},{1,5},{5... | collective-permute-start | bytes 393224 | tf_op jit(solution)/shard_map/ppermute | solution.py:18
  51.2 13.3 %collective-permute-start.18 = (f32[2,128,128]{2,1,0:T(8,128)S(1)}, f32[2,128,128]{2,1,0:T(8,128)S(1)}, u32[]{:S(2)}, u32[]{:S(2)}) collective-permute-start(f32[2,128,128]{2,1,0:T(8,128)S(1)} %collective-permute-done.14.refs_1_), channel_id=1, source_target_pairs={{0,8},{4,12},{8,0},{12,4},{16,24},{20,28},{24,16},{28,20},{1,9},{5... | collective-permute-start | bytes 393224 | tf_op jit(solution)/shard_map/ppermute | solution.py:18
  52.5 12.1 %collective-permute-start.19 = (f32[2,128,128]{2,1,0:T(8,128)S(1)}, f32[2,128,128]{2,1,0:T(8,128)S(1)}, u32[]{:S(2)}, u32[]{:S(2)}) collective-permute-start(f32[2,128,128]{2,1,0:T(8,128)S(1)} %get-tuple-element.62.refs_0_), channel_id=1, source_target_pairs={{0,4},{4,0},{8,12},{12,8},{16,20},{20,16},{24,28},{28,24},{1,5},{5... | collective-permute-start | bytes 393224 | tf_op jit(solution)/shard_map/ppermute | solution.py:18
  60.5 6.9 %collective-permute-start.13 = (f32[2,128,128]{2,1,0:T(8,128)S(1)}, f32[2,128,128]{2,1,0:T(8,128)S(1)}, u32[]{:S(2)}, u32[]{:S(2)}) collective-permute-start(f32[2,128,128]{2,1,0:T(8,128)S(1)} %collective-permute-done.12.refs_0_), channel_id=1, source_target_pairs={{0,4},{4,0},{8,12},{12,8},{16,20},{20,16},{24,28},{28,24},{1,5},{5... | collective-permute-start | bytes 393224 | tf_op jit(solution)/shard_map/ppermute | solution.py:18
  60.5 6.9 %collective-permute-start.16 = (f32[2,128,128]{2,1,0:T(8,128)S(1)}, f32[2,128,128]{2,1,0:T(8,128)S(1)}, u32[]{:S(2)}, u32[]{:S(2)}) collective-permute-start(f32[2,128,128]{2,1,0:T(8,128)S(1)} %collective-permute-done.15.refs_3_), channel_id=1, source_target_pairs={{0,8},{4,12},{8,0},{12,4},{16,24},{20,28},{24,16},{28,20},{1,9},{5... | collective-permute-start | bytes 393224 | tf_op jit(solution)/shard_map/ppermute | solution.py:18
